TPU v7x, 32 devices: a whole 2x2x4 slice. The times are simulated.
32 devices in a mesh: dp: 16 (over z, y, x), tensor: 2 (over core).
Axes of the slice: x: 2, y: 2, z: 4, core: 2. Of those that a mesh axis runs over, the one named last changes fastest.
Arguments:
- tokens: bfloat16 [24576, 768], P(('dp', 'tensor')), may hold values from -6 to 6
- kept_patches: int32 [24576], P(('dp', 'tensor')), may hold values from 0 to 1567, as said below
- clip_lengths: int32 [128], replicated, may hold values from 39 to 314, as said below
- clip_device: int32 [128], replicated, may hold values from 0 to 31, as said below
- cot_output: bfloat16 [24576, 768], P(('dp', 'tensor')), may hold values from -6 to 6
- cot_aligned: bfloat16 [24576, 1024], P(('dp', 'tensor')), may hold values from -6 to 6
- entry_weight: float32 [1769472], P(('dp', 'tensor')), may hold values from -0.21875 to 0.21875
- entry_first: float32 [1769472], P(('dp', 'tensor')), may hold values from -112 to 112
- entry_second: float32 [1769472], P(('dp', 'tensor')), may hold values from 245.76 to 4096.8193
- exit_weight: float32 [589824], P(('dp', 'tensor')), may hold values from -1.75 to 1.75
- exit_first: float32 [589824], P(('dp', 'tensor')), may hold values from -24 to 24
- exit_second: float32 [589824], P(('dp', 'tensor')), may hold values from 12.288 to 204.71808
- align_weight: float32 [786432], P(('dp', 'tensor')), may hold values from -0.21875 to 0.21875
- align_first: float32 [786432], P(('dp', 'tensor')), may hold values from -128 to 128
- align_second: float32 [786432], P(('dp', 'tensor')), may hold values from 447.2832 to 8183.808
- expand_weight: float32 [3072, 768], P(('dp', 'tensor')), may hold values from -0.21875 to 0.21875
- expand_first: float32 [3072, 768], P(('dp', 'tensor')), may hold values from -32 to 32
- expand_second: float32 [3072, 768], P(('dp', 'tensor')), may hold values from 24.576 to 409.68192
- reduce_weight: float32 [3072, 768], P(('dp', 'tensor')), may hold values from -0.109375 to 0.109375
- reduce_first: float32 [3072, 768], P(('dp', 'tensor')), may hold values from -80 to 80
- reduce_second: float32 [3072, 768], P(('dp', 'tensor')), may hold values from 144.50688 to 2457.6
- position_table: float32 [1204224], P(('dp', 'tensor')), may hold values from -3 to 3
- position_first: float32 [1204224], P(('dp', 'tensor')), may hold values from -5 to 5
- position_second: float32 [1204224], P(('dp', 'tensor')), may hold values from 0.5219265 to 7.836735
- norm_params: float32 [3072], P(('dp', 'tensor')), may hold values from -1.5 to 1.5, as said below
- norm_first: float32 [3072], P(('dp', 'tensor')), may hold values from -128 to 128
- norm_second: float32 [3072], P(('dp', 'tensor')), may hold values from 447.2832 to 8183.808
Outputs:
- block_out: bfloat16 [24576, 768], P(('dp', 'tensor'))
- aligned: bfloat16 [24576, 1024], P(('dp', 'tensor'))
- token_grad: float32 [24576, 768], P(('dp', 'tensor'))
- new_entry_first: float32 [1769472], P(('dp', 'tensor'))
- new_entry_second: float32 [1769472], P(('dp', 'tensor'))
- new_entry_weight: float32 [1769472], P(('dp', 'tensor'))
- new_exit_first: float32 [589824], P(('dp', 'tensor'))
- new_exit_second: float32 [589824], P(('dp', 'tensor'))
- new_exit_weight: float32 [589824], P(('dp', 'tensor'))
- new_align_first: float32 [786432], P(('dp', 'tensor'))
- new_align_second: float32 [786432], P(('dp', 'tensor'))
- new_align_weight: float32 [786432], P(('dp', 'tensor'))
- new_expand_first: float32 [3072, 768], P(('dp', 'tensor'))
- new_expand_second: float32 [3072, 768], P(('dp', 'tensor'))
- new_expand_weight: float32 [3072, 768], P(('dp', 'tensor'))
- new_reduce_first: float32 [3072, 768], P(('dp', 'tensor'))
- new_reduce_second: float32 [3072, 768], P(('dp', 'tensor'))
- new_reduce_weight: float32 [3072, 768], P(('dp', 'tensor'))
- new_position_first: float32 [1204224], P(('dp', 'tensor'))
- new_position_second: float32 [1204224], P(('dp', 'tensor'))
- new_position_table: float32 [1204224], P(('dp', 'tensor'))
- new_norm_first: float32 [3072], P(('dp', 'tensor'))
- new_norm_second: float32 [3072], P(('dp', 'tensor'))
- new_norm_params: float32 [3072], P(('dp', 'tensor'))
- lamb_stats: float32 [3, 7], replicated
Inputs may be any that keep to these rules, and one draw needn't show every extreme that they name: `clip_lengths`: every clip has 314 rows (a video clip) or 39 rows (an image). `clip_device`: each device index d = i * 2 + j holds exactly 4 clips, at most 2 of them video clips, and some device holds 2. `kept_patches`: within a video clip the rows hold distinct positions below 1568 in rising order, within an image distinct positions below 196 in rising order; padding rows hold 0. `norm_params`: gains lie in 0.5 to 1.5; shifts are normal of deviation 0.5, held within -1.5 to 1.5.
All inputs are finite; a program needn't handle non-finite values.
Results may differ from a plain program's by a relative error of at most 0.0085.
The roundings to bfloat16 on the way count: a program that leaves them out, or rounds other values in their place, can miss the bound.
Values may be sent and summed in bfloat16 or wider, within the bound.
A program may use at most 192 MiB of HBM per device.

v0:
```python
import jax
import jax.numpy as jnp
from jax import lax
from jax.sharding import PartitionSpec as P

H = 12
HD = 64


LN_EPS = 1e-06
MASKED = -1e30
RATE = 0.5
BETA_ONE = 0.9
BETA_TWO = 0.98
ADAM_EPS = 1e-06
DECAY = 0.05
TINY = 1e-06


def contract(left, right, left_dim, right_dim):
    return lax.dot_general(
        left, right, (((left_dim,), (right_dim,)), ((), ())), preferred_element_type=jnp.float32
    )


def layer_norm(values, gain, shift):
    center = values - jnp.mean(values, axis=-1, keepdims=True)
    spread = jnp.mean(center * center, axis=-1, keepdims=True)
    return center * lax.rsqrt(spread + LN_EPS) * gain + shift


def gelu_exact(values):
    return jax.nn.gelu(values, approximate=False)


def row_layout(clip_lengths, clip_device, device, row_count):
    mine = clip_device == device
    own_length = jnp.where(mine, clip_lengths, 0)
    starts = jnp.cumsum(own_length) - own_length
    filled = jnp.sum(own_length)
    positions = jnp.arange(row_count, dtype=jnp.int32)
    begun = mine[None, :] & (starts[None, :] <= positions[:, None])
    segment = jnp.sum(begun.astype(jnp.int32), axis=1)
    valid_rows = positions < filled
    return (jnp.where(valid_rows, segment, 0), valid_rows)


def head_scores(queries, key_rows, same_clip, score_scale):
    scores = contract(queries, key_rows, 1, 1) * score_scale
    return jnp.where(same_clip, scores, MASKED)


def head_forward(queries, key_rows, value_rows, same_clip, score_scale):
    scores = head_scores(queries, key_rows, same_clip, score_scale)
    peak_score = jnp.max(scores, axis=1, keepdims=True)
    raised = jnp.exp(scores - peak_score)
    row_total = jnp.sum(raised, axis=1, keepdims=True)
    attention = raised / row_total
    result = jnp.dot(attention.astype(jnp.bfloat16), value_rows, preferred_element_type=jnp.float32)
    return (result, (peak_score + jnp.log(row_total))[:, 0])


def head_backward(queries, key_rows, value_rows, log_total, grad_heads, same_clip, score_scale):
    scores = head_scores(queries, key_rows, same_clip, score_scale)
    attention = jnp.exp(scores - log_total[:, None])
    attention_low = attention.astype(jnp.bfloat16)
    grad_values = contract(attention_low, grad_heads, 0, 0)
    grad_attention = contract(grad_heads, value_rows, 1, 1)
    inner = jnp.sum(attention * grad_attention, axis=1, keepdims=True)
    grad_score = (attention * (grad_attention - inner)).astype(jnp.bfloat16)
    grad_queries = jnp.dot(grad_score, key_rows, preferred_element_type=jnp.float32) * score_scale
    grad_keys = contract(grad_score, queries, 0, 0) * score_scale
    return (grad_queries, grad_keys, grad_values)


def lamb_moments(weight, gradient, first, second, decay):
    new_first = BETA_ONE * first + (1.0 - BETA_ONE) * gradient
    new_second = BETA_TWO * second + (1.0 - BETA_TWO) * gradient * gradient
    update = new_first / (jnp.sqrt(new_second) + ADAM_EPS) + decay * weight
    return (new_first, new_second, update)


def local(
    tokens,
    kept_patches,
    clip_lengths,
    clip_device,
    cot_output,
    cot_aligned,
    entry_weight,
    entry_first,
    entry_second,
    exit_weight,
    exit_first,
    exit_second,
    align_weight,
    align_first,
    align_second,
    expand_weight,
    expand_first,
    expand_second,
    reduce_weight,
    reduce_first,
    reduce_second,
    position_table,
    position_first,
    position_second,
    norm_params,
    norm_first,
    norm_second,
):
    row_count, model_width = tokens.shape
    align_width = cot_aligned.shape[1]
    score_scale = HD ** (-0.5)
    masters = (
        entry_weight,
        exit_weight,
        align_weight,
        expand_weight,
        reduce_weight,
        position_table,
        norm_params,
    )
    device = lax.axis_index("dp") * lax.axis_size("tensor") + lax.axis_index("tensor")
    segment, valid_rows = row_layout(clip_lengths, clip_device, device, row_count)
    same_clip = segment[:, None] == segment[None, :]
    valid_column = valid_rows[:, None]
    gathered = (
        lax.all_gather(entry_weight.astype(jnp.bfloat16), ("dp", "tensor"), axis=0, tiled=True),
        lax.all_gather(exit_weight.astype(jnp.bfloat16), ("dp", "tensor"), axis=0, tiled=True),
        lax.all_gather(align_weight.astype(jnp.bfloat16), ("dp", "tensor"), axis=0, tiled=True),
        lax.all_gather(position_table.astype(jnp.bfloat16), ("dp", "tensor"), axis=0, tiled=True),
        lax.all_gather(norm_params.astype(jnp.bfloat16), ("dp", "tensor"), axis=0, tiled=True),
    )
    expand_low, reduce_low = (
        lax.all_gather(expand_weight.astype(jnp.bfloat16), "dp", axis=0, tiled=True),
        lax.all_gather(reduce_weight.astype(jnp.bfloat16), "dp", axis=0, tiled=True),
    )
    entry_low = gathered[0].reshape(model_width, 3 * model_width)
    exit_low = gathered[1].reshape(model_width, model_width)
    align_low = gathered[2].reshape(model_width, align_width)
    table_low = gathered[3].reshape(-1, model_width)
    norm_low = gathered[4].astype(jnp.float32).reshape(4, model_width)
    residual = tokens.astype(jnp.float32) + jnp.take(table_low, kept_patches, axis=0).astype(
        jnp.float32
    )
    normed_one = layer_norm(residual, norm_low[0], norm_low[1]).astype(jnp.bfloat16)
    joint_low = jnp.dot(normed_one, entry_low, preferred_element_type=jnp.float32).astype(
        jnp.bfloat16
    )
    split_heads = joint_low.reshape(row_count, 3, H, HD).transpose(1, 2, 0, 3)
    head_outputs, log_totals = lax.map(
        lambda entries: head_forward(entries[0], entries[1], entries[2], same_clip, score_scale),
        (split_heads[0], split_heads[1], split_heads[2]),
    )
    attended = head_outputs.transpose(1, 0, 2).reshape(row_count, model_width).astype(jnp.bfloat16)
    middle = residual + jnp.dot(attended, exit_low, preferred_element_type=jnp.float32)
    normed_two = layer_norm(middle, norm_low[2], norm_low[3]).astype(jnp.bfloat16)
    hidden_in = lax.all_gather(normed_two, "tensor", axis=0, tiled=True)
    hidden_pre = contract(hidden_in, expand_low, 1, 1)
    hidden_act = gelu_exact(hidden_pre).astype(jnp.bfloat16)
    feed_out = lax.psum_scatter(
        jnp.dot(hidden_act, reduce_low, preferred_element_type=jnp.float32).astype(jnp.bfloat16),
        "tensor",
        scatter_dimension=0,
        tiled=True,
    ).astype(jnp.float32)
    out_low = (middle + feed_out).astype(jnp.bfloat16)
    block_out = jnp.where(valid_column, out_low, jnp.zeros_like(out_low))
    align_rows = jnp.dot(out_low, align_low, preferred_element_type=jnp.float32).astype(
        jnp.bfloat16
    )
    aligned = jnp.where(valid_column, align_rows, jnp.zeros_like(align_rows))
    cot_align_valid = jnp.where(valid_column, cot_aligned, jnp.zeros_like(cot_aligned))
    grad_align = contract(out_low, cot_align_valid, 0, 0)
    grad_out = jnp.where(valid_column, cot_output.astype(jnp.float32), 0.0) + contract(
        cot_align_valid, align_low, 1, 1
    )
    grad_feed = grad_out.astype(jnp.bfloat16)
    grad_feed_rows = lax.all_gather(grad_feed, "tensor", axis=0, tiled=True)
    grad_act = contract(grad_feed_rows, reduce_low, 1, 1)
    gelu_value, gelu_back = jax.vjp(gelu_exact, hidden_pre)
    grad_pre = gelu_back(grad_act)[0].astype(jnp.bfloat16)
    grad_reduce = contract(hidden_act, grad_feed_rows, 0, 0)
    grad_expand = contract(grad_pre, hidden_in, 0, 0)
    grad_two = lax.psum_scatter(
        jnp.dot(grad_pre, expand_low, preferred_element_type=jnp.float32),
        "tensor",
        scatter_dimension=0,
        tiled=True,
    )
    grad_expand, grad_reduce = (
        lax.psum_scatter(grad_expand, "dp", scatter_dimension=0, tiled=True),
        lax.psum_scatter(grad_reduce, "dp", scatter_dimension=0, tiled=True),
    )
    norm_value, norm_back_two = jax.vjp(layer_norm, middle, norm_low[2], norm_low[3])
    grad_from_two, grad_gain_two, grad_shift_two = norm_back_two(grad_two)
    grad_middle = grad_out + grad_from_two
    grad_branch = grad_middle.astype(jnp.bfloat16)
    grad_exit = contract(attended, grad_branch, 0, 0)
    grad_attended = contract(grad_branch, exit_low, 1, 1).astype(jnp.bfloat16)
    grad_heads = grad_attended.reshape(row_count, H, HD).transpose(1, 0, 2)
    grad_queries, grad_keys, grad_values = lax.map(
        lambda entries: head_backward(
            entries[0], entries[1], entries[2], entries[3], entries[4], same_clip, score_scale
        ),
        (split_heads[0], split_heads[1], split_heads[2], log_totals, grad_heads),
    )
    grad_joint = jnp.stack((grad_queries, grad_keys, grad_values)).transpose(2, 0, 1, 3)
    grad_joint = grad_joint.reshape(row_count, 3 * model_width).astype(jnp.bfloat16)
    grad_entry = contract(normed_one, grad_joint, 0, 0)
    grad_one = contract(grad_joint, entry_low, 1, 1)
    norm_value_one, norm_back_one = jax.vjp(layer_norm, residual, norm_low[0], norm_low[1])
    grad_from_one, grad_gain_one, grad_shift_one = norm_back_one(grad_one)
    token_grad = grad_middle + grad_from_one
    grad_table = jax.ops.segment_sum(token_grad, kept_patches, num_segments=table_low.shape[0])
    grad_norms = jnp.concatenate((grad_gain_one, grad_shift_one, grad_gain_two, grad_shift_two))
    summed = (
        lax.psum_scatter(grad_entry.reshape(-1), ("dp", "tensor"), scatter_dimension=0, tiled=True),
        lax.psum_scatter(grad_exit.reshape(-1), ("dp", "tensor"), scatter_dimension=0, tiled=True),
        lax.psum_scatter(grad_align.reshape(-1), ("dp", "tensor"), scatter_dimension=0, tiled=True),
        lax.psum_scatter(grad_table.reshape(-1), ("dp", "tensor"), scatter_dimension=0, tiled=True),
        lax.psum_scatter(grad_norms, ("dp", "tensor"), scatter_dimension=0, tiled=True),
    )
    gradients = (summed[0], summed[1], summed[2], grad_expand, grad_reduce, summed[3], summed[4])
    firsts = (
        entry_first,
        exit_first,
        align_first,
        expand_first,
        reduce_first,
        position_first,
        norm_first,
    )
    seconds = (
        entry_second,
        exit_second,
        align_second,
        expand_second,
        reduce_second,
        position_second,
        norm_second,
    )
    decays = (DECAY, DECAY, DECAY, DECAY, DECAY, DECAY, 0.0)
    results = [
        lamb_moments(
            masters[member], gradients[member], firsts[member], seconds[member], decays[member]
        )
        for member in range(7)
    ]
    update_local = jnp.stack([jnp.sum(found[2] * found[2]) for found in results])
    weight_squares, update_squares = lax.psum(
        (jnp.stack([jnp.sum(master * master) for master in masters]), update_local),
        ("dp", "tensor"),
    )
    trust = jnp.sqrt(weight_squares) / jnp.sqrt(update_squares + TINY)
    outputs = [block_out, aligned, token_grad]
    for member in range(7):
        found = results[member]
        outputs = outputs + [found[0], found[1], masters[member] - RATE * trust[member] * found[2]]
    lamb_stats = jnp.stack((trust, jnp.sqrt(weight_squares), jnp.sqrt(update_squares)))
    outputs = outputs + [lamb_stats]
    return tuple(outputs)


def solution(mesh):
    placed = (
        P(("dp", "tensor"), None),
        P(("dp", "tensor")),
        P(),
        P(),
        P(("dp", "tensor"), None),
        P(("dp", "tensor"), None),
        P(("dp", "tensor")),
        P(("dp", "tensor")),
        P(("dp", "tensor")),
        P(("dp", "tensor")),
        P(("dp", "tensor")),
        P(("dp", "tensor")),
        P(("dp", "tensor")),
        P(("dp", "tensor")),
        P(("dp", "tensor")),
        P(("dp", "tensor"), None),
        P(("dp", "tensor"), None),
        P(("dp", "tensor"), None),
        P(("dp", "tensor"), None),
        P(("dp", "tensor"), None),
        P(("dp", "tensor"), None),
        P(("dp", "tensor")),
        P(("dp", "tensor")),
        P(("dp", "tensor")),
        P(("dp", "tensor")),
        P(("dp", "tensor")),
        P(("dp", "tensor")),
    )
    return jax.shard_map(
        local,
        mesh=mesh,
        in_specs=placed,
        out_specs=(
            P(("dp", "tensor"), None),
            P(("dp", "tensor"), None),
            P(("dp", "tensor"), None),
            P(("dp", "tensor")),
            P(("dp", "tensor")),
            P(("dp", "tensor")),
            P(("dp", "tensor")),
            P(("dp", "tensor")),
            P(("dp", "tensor")),
            P(("dp", "tensor")),
            P(("dp", "tensor")),
            P(("dp", "tensor")),
            P(("dp", "tensor"), None),
            P(("dp", "tensor"), None),
            P(("dp", "tensor"), None),
            P(("dp", "tensor"), None),
            P(("dp", "tensor"), None),
            P(("dp", "tensor"), None),
            P(("dp", "tensor")),
            P(("dp", "tensor")),
            P(("dp", "tensor")),
            P(("dp", "tensor")),
            P(("dp", "tensor")),
            P(("dp", "tensor")),
            P(),
        ),
        check_vma=False,
    )
```

profile of v0, /device:TPU:9, one launch (start us, length us, event | category | flops | bytes accessed | tf_op | source)
XLA Modules:
  0.0 1162.6 jit_solution(5532540820435427545)
XLA Ops:
  19.3 40.7 %all-reduce = bf16[3072]{0:T(1024)(128)(2,1)S(1)} all-reduce(bf16[3072]{0:T(1024)(128)(2,1)S(1)} %dynamic-update-slice), channel_id=1, replica_groups=mesh['dp'=16,'tensor'=2] {'dp','tensor'}, use_global_device_ids=true, to_apply=%add | all-reduce | flops 3072 | bytes 12288
  62.5 3.9 all-gather.12.cloned.1.call-done
  66.4 3.3 reshape.249
  69.7 64.5 %all-gather.24.cloned.1.call-done = bf16[32,1,37632]{2,1,0:T(2,128)(2,1)} async-done(((bf16[1,1,37632]{2,1,0:T(2,128)(2,1)}), bf16[32,1,37632]{2,1,0:T(2,128)(2,1)}) %all-gather.24.cloned.1.call-update) | async-done | bytes 2408464 | tf_op jit(solution)/shard_map/all_gather | solution.py:132
  134.3 51.2 %reduce.1 = bf16[32,37632]{1,0:T(8,128)(2,1)} reduce(bf16[32,1,37632]{2,1,0:T(2,128)(2,1)} %all-gather.24.cloned.1.call-done, bf16[]{:T(256)} %constant.226), dimensions={1}, to_apply=%all-gather.reduce_sub_computation | reduce | bytes 4816898 | tf_op jit(solution)/shard_map/all_gather | solution.py:132
  185.4 5.0 reshape.244
  190.4 3.4 gather_fusion
  196.6 7.6 reshape.245
  204.2 6.9 convolution_convert_fusion
  211.1 5.8 copy.127
  216.9 3.3 slice_bitcast_fusion
  220.1 3.7 copy.129
  223.8 2.4 copy.130
  226.2 2.5 copy.131
  229.8 64.7 %while.28 = (s32[]{:T(128)}, bf16[12,768,64]{1,2,0:T(8,128)(2,1)}, f32[12,768]{1,0:T(8,128)}, bf16[12,768,64]{2,1,0:T(8,128)(2,1)}, bf16[12,768,64]{2,1,0:T(8,12...) while((s32[]{:T(128)}, bf16[12,768,64]{1,2,0:T(8,128)(2,1)}, ...), condition=%wide.region_8.9_spmd.clone, body=%wide.region_5.8_spmd.clone.sunk | while | flops 156302592 | bytes 7911521 | solution.py:152
  238.5 2.1 fusion.143
  243.9 2.1 fusion.143
  249.3 2.1 fusion.143
  254.7 2.1 fusion.143
  270.9 2.1 fusion.143
  276.3 2.1 fusion.143
  287.1 2.1 fusion.143
  294.6 3.2 fusion.89
  303.0 3.7 reshape.250
  306.7 5.2 fusion.90
  312.0 5.1 all-gather.16.cloned.1.call-done
  317.1 12.2 %all-gather.14.cloned.1.call-done = bf16[1536,768]{0,1:T(8,128)(2,1)} async-done(((bf16[768,768]{0,1:T(8,128)(2,1)}), bf16[1536,768]{0,1:T(8,128)(2,1)}) %all-gather.14.cloned.1.call-update) | async-done | bytes 2359312 | tf_op jit(solution)/shard_map/all_gather | solution.py:159
  329.2 27.0 %multiply_convert_fusion.1 = (bf16[1536,1536]{1,0:T(8,128)(2,1)}, f32[1536,1536]{1,0:T(8,128)}, f32[1536,1536]{1,0:T(8,128)}) fusion(bf16[1536,768]{0,1:T(8,128)(2,1)} %all-gather.14.cloned.1.call-done, bf16[1536,768]{1,0:T(8,128)(2,1)} %all-gather.16.cloned.1.call-done), kind=kOutput, calls=%fused_computation.57 | convolution fusion | flops 3777232896 | bytes 28311552 | tf_op jit(solution)/shard_map/dot_general | solution.py:21
  356.3 9.2 fusion.95
  365.6 135.9 %reduce-scatter.11.cloned.1.call-done = f32[96,768]{1,0:T(8,128)} async-done(((f32[1536,768]{1,0:T(8,128)}), f32[96,768]{1,0:T(8,128)}) %reduce-scatter.11.cloned.1.call-update) | async-done | bytes 294928 | tf_op jit(solution)/shard_map/reduce_scatter | solution.py:194
  501.5 2.5 multiply_reduce_fusion.9
  504.3 64.0 %all-gather.18.cloned.1.call-done = bf16[1536,768]{1,0:T(8,128)(2,1)} async-done(((bf16[96,768]{1,0:T(8,128)(2,1)}), bf16[1536,768]{1,0:T(8,128)(2,1)}) %all-gather.18.cloned.1.call-update) | async-done | bytes 2359312 | tf_op jit(solution)/shard_map/all_gather | solution.py:137
  568.4 8.5 convolution_convert_fusion.1
  576.9 13.7 %add_convert_fusion = bf16[1536,1536]{1,0:T(8,128)(2,1)S(1)} fusion(f32[1536,1536]{1,0:T(8,128)} %get-tuple-element.433, bf16[1536,768]{0,1:T(8,128)(2,1)} %all-gather.22.cloned.1.call-done, bf16[1536,768]{1,0:T(8,128)(2,1)} %all-gather.18.cloned.1.call-done, f32[1536,1536]{1,0:T(8,128)} %get-tuple-element.462), kind=kOutput, calls=%fused_computation.56 | convolution fusion | flops 3656908800 | bytes 28311552 | tf_op jit(solution)/shard_map/dot_general | solution.py:21
  590.6 2.2 copy-done.69
  592.7 5.7 fusion.92
  599.0 9.8 fusion.94
  609.5 2.8 broadcast_select_fusion.3
  613.8 2.4 copy.148
  616.2 3.3 multiply_reduce_fusion.1
  627.6 107.8 %while.29 = (s32[]{:T(128)}, bf16[12,768,64]{1,2,0:T(8,128)(2,1)S(1)}, bf16[12,768,64]{1,2,0:T(8,128)(2,1)}, bf16[12,768,64]{1,2,0:T(8,128)(2,1)}, bf16[12,768,6...) while((s32[]{:T(128)}, ...), condition=%wide.region_17.18_spmd.clone, body=%wide.region_15.17_spmd.clone.sunk | while | flops 383483136 | bytes 19690608 | solution.py:203
  667.9 2.1 fusion.154
  721.8 2.1 fusion.154
  735.3 2.8 fusion.93
  743.5 5.5 fusion.76
  749.0 7.9 reshape.252
  756.9 7.4 fusion.91
  764.4 3.2 copy.140
  767.5 2.4 multiply_reduce_fusion.3
  772.4 2.6 add_add_fusion.2
  775.0 2.2 copy.144
  777.2 9.7 scatter_custom_fusion
  787.0 5.9 reshape.255
  794.7 2.6 broadcast_select_fusion.1
  797.4 41.0 %all-reduce.5 = f32[3072]{0:T(1024)S(1)} all-reduce(f32[3072]{0:T(1024)S(1)} %pad_maximum_fusion), channel_id=10, replica_groups=mesh['dp'=16,'tensor'=2] {'dp','tensor'}, use_global_device_ids=true, to_apply=%region_45.46.clone | all-reduce | flops 3072 | bytes 24576
  839.6 2.2 multiply_reduce_fusion.10
  841.8 240.4 %all-reduce.10.cloned.1.call-done = (f32[1769472]{0:T(1024)}, f32[589824]{0:T(1024)}, f32[786432]{0:T(1024)}, f32[1204224]{0:T(1024)}) async-done(((f32[1769472]{0:T(1024)}, f32[589824]{0:T(1024)}, f32[786432]{0:T(1024)}, f32[1204224]{0:T(1024)}), (f32[1769472]{0:T(1024)}, f32[589824]{0:T(1024)}, f32[786432]{0:T(1024)}, f32[1204224]{0:T(1024)})) %all-reduce.10.cloned.1.call-update) | async-done | bytes 17399824
  1082.1 2.7 multiply_reduce_fusion.12
  1084.8 2.5 multiply_reduce_fusion.14
  1087.3 2.2 multiply_reduce_fusion.16
  1089.5 2.2 multiply_reduce_fusion.18
  1091.7 4.5 stack.83
  1096.2 4.6 stack.91
  1102.3 39.3 %all-reduce.6 = (f32[7]{0:T(128)S(1)}, f32[7]{0:T(128)S(1)}) all-reduce(f32[7]{0:T(128)S(1)} %stack.91, f32[7]{0:T(128)S(1)} %stack.83), channel_id=1, replica_groups=mesh['dp'=16,'tensor'=2] {'dp','tensor'}, use_global_device_ids=true, to_apply=%region_47.48 | all-reduce | flops 14 | bytes 112 | tf_op jit(solution)/shard_map/psum | solution.py:252
  (380 shorter events, 209.4 us)
Async XLA Ops:
  7.2 9.9 copy-start.18
  7.2 11.3 copy-start.60
  7.2 53.4 %copy-start.59 = (s32[128]{0:T(128)S(1)}, s32[128]{0:T(128)}, u32[]{:S(2)}) copy-start(s32[128]{0:T(128)} %param.33) | copy-start | bytes 1540
  7.2 53.4 %copy-start.64 = (s32[128]{0:T(128)S(1)}, s32[128]{0:T(128)}, u32[]{:S(2)}) copy-start(s32[128]{0:T(128)} %param.34) | copy-start | bytes 1540
  7.2 59.2 %all-gather.12.cloned.1.call-start = ((), (), s32[]{:S(2)}) async-start(), calls=%async_computation.5 | async-start | bytes 1216512 | tf_op jit(solution)/shard_map/all_gather | solution.py:130
  8.9 125.4 %all-gather.24.cloned.1.call-start = ((), (), s32[]{:S(2)}) async-start(), calls=%async_computation.15 | async-start | bytes 4967424 | tf_op jit(solution)/shard_map/all_gather | solution.py:132
  10.6 185.9 %all-gather.10.cloned.1.call-start = ((), (), s32[]{:S(2)}) async-start(), calls=%async_computation.4 | async-start | bytes 3649536 | tf_op jit(solution)/shard_map/all_gather | solution.py:129
  12.3 290.7 %all-gather.20.cloned.1.call-start = ((), (), s32[]{:S(2)}) async-start(), calls=%async_computation.10 | async-start | bytes 1622016 | tf_op jit(solution)/shard_map/all_gather | solution.py:131
  13.9 303.1 %all-gather.16.cloned.1.call-start = ((), (), s32[]{:S(2)}) async-start(), calls=%async_computation.7 | async-start | bytes 2506752 | tf_op jit(solution)/shard_map/all_gather | solution.py:136
  15.6 313.6 %all-gather.14.cloned.1.call-start = ((), (), s32[]{:S(2)}) async-start(), calls=%async_computation.6 | async-start | bytes 3538944 | tf_op jit(solution)/shard_map/all_gather | solution.py:159
  17.1 187.1 %copy-start.51 = (pred[768]{0:T(1024)(128)(4,1)}, pred[768]{0:T(1024)(128)(4,1)S(1)}, u32[]{:S(2)}) copy-start(pred[768]{0:T(1024)(128)(4,1)S(1)} %compare_and_fusion) | copy-start | bytes 2308
  60.6 143.6 %copy-start.43 = (f32[768]{0:T(1024)}, f32[768]{0:T(1024)S(1)}, u32[]{:S(2)}) copy-start(f32[768]{0:T(1024)S(1)} %get-tuple-element.446) | copy-start | bytes 9220
  60.6 143.6 %copy-start.57 = (f32[768]{0:T(1024)}, f32[768]{0:T(1024)S(1)}, u32[]{:S(2)}) copy-start(f32[768]{0:T(1024)S(1)} %get-tuple-element.447) | copy-start | bytes 9220
  195.5 8.7 copy-start.2
  196.0 8.3 copy-start.36
  196.5 7.7 copy-start.45
  196.5 7.7 copy-start.49
  300.2 56.1 %all-gather.22.cloned.1.call-start = ((), (), s32[]{:S(2)}) async-start(), calls=%async_computation.11 | async-start | bytes 3538944 | tf_op jit(solution)/shard_map/all_gather | solution.py:180
  301.7 5.0 copy-start.21
  311.9 189.6 %reduce-scatter.11.cloned.1.call-start = ((), (), s32[]{:S(2)}) async-start(), calls=%async_computation.14 | async-start | bytes 5013504 | tf_op jit(solution)/shard_map/reduce_scatter | solution.py:194
  365.5 136.0 %copy-start.22 = (f32[96,768]{1,0:T(8,128)S(1)}, f32[96,768]{1,0:T(8,128)}, u32[]{:S(2)}) copy-start(f32[96,768]{1,0:T(8,128)} %param.49) | copy-start | bytes 884740
  365.5 136.0 %copy-start.32 = (f32[96,768]{1,0:T(8,128)S(1)}, f32[96,768]{1,0:T(8,128)}, u32[]{:S(2)}) copy-start(f32[96,768]{1,0:T(8,128)} %param.51) | copy-start | bytes 884740
  365.5 136.0 %copy-start.33 = (f32[96,768]{1,0:T(8,128)S(1)}, f32[96,768]{1,0:T(8,128)}, u32[]{:S(2)}) copy-start(f32[96,768]{1,0:T(8,128)} %param.50) | copy-start | bytes 884740
  365.5 202.8 %all-gather.18.cloned.1.call-start = ((), (), s32[]{:S(2)}) async-start(), calls=%async_computation.8 | async-start | bytes 2506752 | tf_op jit(solution)/shard_map/all_gather | solution.py:137
  504.0 104.9 %reduce-scatter.5.cloned.1.call-start = ((), (), s32[]{:S(2)}) async-start(), calls=%async_computation.9 | async-start | bytes 3538944 | tf_op jit(solution)/shard_map/reduce_scatter | solution.py:162
  576.8 39.4 %reduce-scatter.7.cloned.1.call-start = ((), (), s32[]{:S(2)}) async-start(), calls=%async_computation.12 | async-start | bytes 7077888 | tf_op jit(solution)/shard_map/reduce_scatter | solution.py:186
  576.9 15.9 %copy-start.67 = (bf16[1536,768]{1,0:T(8,128)(2,1)S(1)}, bf16[1536,768]{1,0:T(8,128)(2,1)}, u32[]{:S(2)}) copy-start(bf16[1536,768]{1,0:T(8,128)(2,1)} %all-gather.16.cloned.1.call-done) | copy-start | bytes 7077892
  598.5 241.1 %reduce-scatter.9.cloned.1.call-start = ((), (), s32[]{:S(2)}) async-start(), calls=%async_computation.13 | async-start | bytes 5013504 | tf_op jit(solution)/shard_map/reduce_scatter | solution.py:193
  608.9 473.3 %all-reduce.10.cloned.1.call-start = ((), (), s32[]{:S(2)}) async-start(), calls=%async_computation.16 | async-start | bytes 34799616
  609.5 2.8 copy-start.68
  616.2 3.3 copy-start.48
  616.2 3.3 copy-start.7
  739.6 3.8 copy-start.1
  739.6 3.8 copy-start.3
  739.6 3.8 copy-start.37
  739.6 3.8 copy-start.44
  739.7 3.8 copy-start.50
  739.7 3.8 copy-start.52
  739.7 3.8 copy-start.58
  764.4 3.2 copy-start.53
  767.5 2.5 copy-start.4
  777.2 9.8 copy-start.13
  794.6 2.7 copy-start.54
  794.6 2.7 copy-start.55
  794.6 43.7 %copy-start.61 = (f32[96]{0:T(128)S(1)}, f32[96]{0:T(128)}, u32[]{:S(2)}) copy-start(f32[96]{0:T(128)} %param.55) | copy-start | bytes 1156
  794.6 43.7 %copy-start.65 = (f32[96]{0:T(128)S(1)}, f32[96]{0:T(128)}, u32[]{:S(2)}) copy-start(f32[96]{0:T(128)} %param.57) | copy-start | bytes 1156
  794.6 43.7 %copy-start.66 = (f32[96]{0:T(128)S(1)}, f32[96]{0:T(128)}, u32[]{:S(2)}) copy-start(f32[96]{0:T(128)} %param.56) | copy-start | bytes 1156
  794.6 45.0 %copy-start.12 = (f32[96,768]{1,0:T(8,128)S(1)}, f32[96,768]{1,0:T(8,128)}, u32[]{:S(2)}) copy-start(f32[96,768]{1,0:T(8,128)} %param.46) | copy-start | bytes 884740
  794.7 287.5 %copy-start.14 = (f32[55296]{0:T(1024)S(1)}, f32[55296]{0:T(1024)}, u32[]{:S(2)}) copy-start(f32[55296]{0:T(1024)} %param.37) | copy-start | bytes 663556
  797.3 287.6 %copy-start.16 = (f32[37632]{0:T(1024)S(1)}, f32[37632]{0:T(1024)}, u32[]{:S(2)}) copy-start(f32[37632]{0:T(1024)} %param.52) | copy-start | bytes 451588
  797.3 287.6 %copy-start.34 = (f32[37632]{0:T(1024)S(1)}, f32[37632]{0:T(1024)}, u32[]{:S(2)}) copy-start(f32[37632]{0:T(1024)} %param.54) | copy-start | bytes 451588
  797.3 287.6 %copy-start.35 = (f32[37632]{0:T(1024)S(1)}, f32[37632]{0:T(1024)}, u32[]{:S(2)}) copy-start(f32[37632]{0:T(1024)} %param.53) | copy-start | bytes 451588
  797.3 290.0 %copy-start.30 = (f32[24576]{0:T(1024)S(1)}, f32[24576]{0:T(1024)}, u32[]{:S(2)}) copy-start(f32[24576]{0:T(1024)} %param.43) | copy-start | bytes 294916
  797.3 290.0 %copy-start.38 = (f32[24576]{0:T(1024)S(1)}, f32[24576]{0:T(1024)}, u32[]{:S(2)}) copy-start(f32[24576]{0:T(1024)} %param.45) | copy-start | bytes 294916
  797.3 290.0 %copy-start.39 = (f32[24576]{0:T(1024)S(1)}, f32[24576]{0:T(1024)}, u32[]{:S(2)}) copy-start(f32[24576]{0:T(1024)} %param.44) | copy-start | bytes 294916
  797.3 292.2 %copy-start.31 = (f32[18432]{0:T(1024)S(1)}, f32[18432]{0:T(1024)}, u32[]{:S(2)}) copy-start(f32[18432]{0:T(1024)} %param.40) | copy-start | bytes 221188
  797.3 292.2 %copy-start.40 = (f32[18432]{0:T(1024)S(1)}, f32[18432]{0:T(1024)}, u32[]{:S(2)}) copy-start(f32[18432]{0:T(1024)} %param.42) | copy-start | bytes 221188
  797.3 292.2 %copy-start.41 = (f32[18432]{0:T(1024)S(1)}, f32[18432]{0:T(1024)}, u32[]{:S(2)}) copy-start(f32[18432]{0:T(1024)} %param.41) | copy-start | bytes 221188
  839.6 261.2 %copy-start.10 = (bf16[768,768]{0,1:T(8,128)(2,1)S(1)}, bf16[768,768]{0,1:T(8,128)(2,1)}, u32[]{:S(2)}) copy-start(bf16[768,768]{0,1:T(8,128)(2,1)} %get-tuple-element.430) | copy-start | bytes 3538948
  841.8 312.9 %copy-start.28 = (f32[96,768]{1,0:T(8,128)}, f32[96,768]{1,0:T(8,128)S(1)}, u32[]{:S(2)}) copy-start(f32[96,768]{1,0:T(8,128)S(1)} %get-tuple-element.420) | copy-start | bytes 884740
  841.8 312.9 %copy-start.29 = (f32[96,768]{1,0:T(8,128)}, f32[96,768]{1,0:T(8,128)S(1)}, u32[]{:S(2)}) copy-start(f32[96,768]{1,0:T(8,128)S(1)} %get-tuple-element.421) | copy-start | bytes 884740
  1091.7 63.0 %copy-start.23 = (f32[96,768]{1,0:T(8,128)S(1)}, f32[96,768]{1,0:T(8,128)}, u32[]{:S(2)}) copy-start(f32[96,768]{1,0:T(8,128)} %param.49) | copy-start | bytes 884740
  1091.7 63.0 %copy-start.24 = (f32[96,768]{1,0:T(8,128)S(1)}, f32[96,768]{1,0:T(8,128)}, u32[]{:S(2)}) copy-start(f32[96,768]{1,0:T(8,128)} %get-tuple-element.418) | copy-start | bytes 884740
  1091.7 63.0 %copy-start.25 = (f32[96,768]{1,0:T(8,128)S(1)}, f32[96,768]{1,0:T(8,128)}, u32[]{:S(2)}) copy-start(f32[96,768]{1,0:T(8,128)} %get-tuple-element.419) | copy-start | bytes 884740
  (19 other events, 28.8 us)
Sparse Core Ops, SparseCore 0:
  11.6 54.8 all-gather.11
  69.8 64.4 all-gather.23
  137.8 57.9 all-gather.9
  199.0 53.3 all-gather.19
  255.6 61.4 all-gather.15
  318.5 10.7 all-gather.13
  330.8 12.1 all-gather.21
  365.7 135.7 reduce-scatter.10
  505.2 63.0 all-gather.17
  577.0 9.6 reduce-scatter.4
  598.6 12.7 reduce-scatter.6
  617.3 135.9 reduce-scatter.8
  793.0 289.0 all-reduce.9
where the time goes:
time: 1180 us; the launch traced here: 1160 us
  waiting for transfers between devices  526 us (45%)
  matrix products  248 us (21%)
  other arithmetic  125 us (11%)
  local copies, waits for them, and re-layouts  122 us (10%)
  blocking collectives  121 us (10%)
  between operations  19.4 us (2%)
    unnamed x14, waiting for transfers between devices  241 us
    dot_general x70, matrix products, contract(): lax.dot_general(left, right, (((left_dim,), (right_dim,)), ((), ())), pre...  180 us
    reduce_scatter x1, waiting for transfers between devices, local(): lax.psum_scatter(grad_reduce, 'dp', scatter_dimension=0, tiled=True)  136 us
    unnamed x2, blocking collectives  81.7 us
    all_gather x1, waiting for transfers between devices, local(): lax.all_gather(position_table.astype(jnp.bfloat16), ('dp', 'tensor'), axi...  64.5 us
    all_gather x1, waiting for transfers between devices, local(): lax.all_gather(reduce_weight.astype(jnp.bfloat16), 'dp', axis=0, tiled=True)  64 us
    all_gather x1, other arithmetic, local(): lax.all_gather(position_table.astype(jnp.bfloat16), ('dp', 'tensor'), axi...  51.2 us
    psum x1, blocking collectives, local(): lax.psum((jnp.stack([jnp.sum(master * master) for master in masters]), up...  39.3 us
  transfers between devices with their start and end apart: 13, of which 7 were waited for; matrix products, arithmetic and copies ran while one was open for 37% of the time, Pallas kernels for 0%

commit v1 on v0

v1 whole, which is shorter than its diff:
```python
import functools

import jax
import jax.numpy as jnp
from jax import lax
from jax.experimental import pallas as pl
from jax.experimental.pallas import tpu as pltpu
from jax.sharding import PartitionSpec as P

H = 12
HD = 64
LN_EPS = 1e-06
RATE = 0.5
BETA_ONE = 0.9
BETA_TWO = 0.98
ADAM_EPS = 1e-06
DECAY = 0.05
TINY = 1e-06
BF = jnp.bfloat16
F32 = jnp.float32
MESH = pl.DeviceIdType.MESH
ANY = pl.BlockSpec(memory_space=pl.ANY)
VMEM = pl.BlockSpec(memory_space=pltpu.VMEM)
MIB = 1 << 20

TABLE, ENTRY, EXIT, EXPAND, REDUCE, ALIGN = range(6)
TABLE_ROWS = 49
TABLE_SLAB = 56
NORM_LANES = 96
ROUTED_DP = 16


def contract(left, right, left_dim, right_dim):
    return lax.dot_general(
        left, right, (((left_dim,), (right_dim,)), ((), ())), preferred_element_type=F32
    )


def layer_norm(values, gain, shift):
    center = values - jnp.mean(values, axis=-1, keepdims=True)
    spread = jnp.mean(center * center, axis=-1, keepdims=True)
    return center * lax.rsqrt(spread + LN_EPS) * gain + shift


def gelu_exact(values):
    return jax.nn.gelu(values, approximate=False)


def row_layout(clip_lengths, clip_device, device, row_count):
    mine = clip_device == device
    own_length = jnp.where(mine, clip_lengths, 0)
    starts = jnp.cumsum(own_length) - own_length
    filled = jnp.sum(own_length)
    positions = jnp.arange(row_count, dtype=jnp.int32)
    begun = mine[None, :] & (starts[None, :] <= positions[:, None])
    segment = jnp.sum(begun.astype(jnp.int32), axis=1)
    valid_rows = positions < filled
    return (jnp.where(valid_rows, segment, 0), valid_rows)


class Route:
    def __init__(self):
        dp = lax.axis_index("dp")
        core = lax.axis_index("tensor")
        z, y, x = dp // 4, (dp // 2) % 2, dp % 2
        across_y = dp + 2 - 4 * y
        across_x = dp + 1 - 2 * x
        self.dp, self.core, self.me = dp, core, dp * 2 + core
        self.near = across_y * (1 - core) + across_x * core
        self.far = across_x * (1 - core) + across_y * core
        self.both = self.near + self.far - dp
        levels = [z + 1 - 2 * (z % 2), 3 - z, (z + 2) % 4]
        self.peers = [level * 4 + y * 2 + x for level in levels]
        self.levels = [dp] + self.peers
        self.partners = [(peer, core) for peer in self.peers] + [
            (self.near, core),
            (self.far, core),
            (dp, 1 - core),
        ]

    def at_level(self, base, step):
        return (self.levels[step] // 4) * 4 + base % 4


def greet(partners):
    barrier = pltpu.get_barrier_semaphore()
    for partner in partners:
        pl.semaphore_signal(barrier, inc=1, device_id=partner, device_id_type=MESH)
    return lambda: pl.semaphore_wait(barrier, len(partners))


def fold_rows(source, rows, columns):
    blocks = columns // 128
    for block in range(blocks):
        yield block, source[pl.ds(block, rows, stride=blocks), :]


def gather_kernel(shapes, groups, *refs):
    count = len(shapes)
    shards, norm = refs[:count], refs[count]
    outs = refs[count + 1 : 2 * count + 1]
    slabs = refs[2 * count + 1 : 3 * count + 1]
    pad, send_sem, recv_sem, own_sem = refs[3 * count + 1 :]
    route = Route()
    arrive = greet(route.partners)
    for piece, (rows, columns) in enumerate(shapes):
        if piece == TABLE:
            blocks = columns // 128
            pad[...] = jnp.zeros_like(pad)
            pad[0:1, 0:NORM_LANES] = norm[...]
            norm_row = pad[0:1, :]
            row_id = lax.broadcasted_iota(jnp.int32, (8, 128), 0)
            for block in range(blocks):
                lanes = slice(block * 128, block * 128 + 128)
                whole = TABLE_ROWS - 1
                slabs[piece][0:whole, lanes] = shards[piece][
                    pl.ds(block, whole, stride=blocks), :
                ].astype(BF)
                last = shards[piece][pl.ds(whole * blocks + block, 1), :]
                tail = jnp.where(row_id == 0, last, 0.0)
                if block == 0:
                    tail = jnp.where(row_id == 1, norm_row, tail)
                slabs[piece][whole : whole + 8, lanes] = tail.astype(BF)
        elif shards[piece].shape == (rows, columns):
            slabs[piece][...] = shards[piece][...].astype(BF)
        else:
            for block, part in fold_rows(shards[piece], rows, columns):
                slabs[piece][:, block * 128 : block * 128 + 128] = part.astype(BF)
    arrive()
    pending = []

    def send(source, piece, origin, partner):
        copy = pltpu.make_async_remote_copy(
            src_ref=source,
            dst_ref=outs[piece].at[origin],
            send_sem=send_sem.at[len(pending)],
            recv_sem=recv_sem.at[piece, origin],
            device_id=partner,
            device_id_type=MESH,
        )
        copy.start()
        pending.append(copy)

    def wait(piece, origin):
        block = outs[piece].at[origin]
        pltpu.make_async_copy(block, block, recv_sem.at[piece, origin]).wait()

    core = route.core
    near, far, pair = (route.near, core), (route.far, core), (route.dp, 1 - core)
    own = []

    def pass_on(group, origin, partners):
        for piece in group:
            wait(piece, origin)
        for partner in partners:
            for piece in group:
                send(outs[piece].at[origin], piece, origin, partner)

    for group in groups:
        for piece in group:
            for partner in [near, far] + [(peer, core) for peer in route.peers] + [pair]:
                send(slabs[piece], piece, route.me, partner)
            copy = pltpu.make_async_copy(
                slabs[piece], outs[piece].at[route.me], own_sem.at[piece]
            )
            copy.start()
            own.append(copy)
        for step in range(4):
            if step > 0:
                pass_on(group, route.levels[step] * 2 + core, (near, far, pair))
            pass_on(group, route.at_level(route.near, step) * 2 + core, (far, pair))
        for step in range(4):
            for base in (route.far, route.both):
                pass_on(group, route.at_level(base, step) * 2 + core, (pair,))
    for group in groups:
        for piece in group:
            for dp in range(ROUTED_DP):
                wait(piece, dp * 2 + 1 - core)
    for copy in pending:
        copy.wait_send()
    for copy in own:
        copy.wait()


def gather_weights(shards, norm, shapes, devices):
    count = len(shapes)
    groups = ((TABLE, ENTRY), (EXIT, EXPAND, REDUCE, ALIGN))
    return pl.pallas_call(
        functools.partial(gather_kernel, shapes, groups),
        out_shape=[jax.ShapeDtypeStruct((devices,) + shape, BF) for shape in shapes],
        in_specs=[VMEM] * (count + 1),
        out_specs=[ANY] * count,
        scratch_shapes=[pltpu.VMEM(shape, BF) for shape in shapes]
        + [
            pltpu.VMEM((8, 128), F32),
            pltpu.SemaphoreType.DMA((31 * count,)),
            pltpu.SemaphoreType.DMA((count, devices)),
            pltpu.SemaphoreType.DMA((count,)),
        ],
        compiler_params=pltpu.CompilerParams(
            collective_id=0, has_side_effects=True, vmem_limit_bytes=40 * MIB
        ),
        name="gather_weights",
    )(*shards, norm)


def scatter_kernel(shapes, order, *refs):
    count = len(shapes)
    grads, outs = refs[:count], refs[count : 2 * count]
    own = refs[2 * count : 3 * count]
    from_pair = refs[3 * count : 4 * count]
    from_far = refs[4 * count : 5 * count]
    from_near = refs[5 * count : 6 * count]
    from_peer = refs[6 * count : 7 * count]
    send_sem, pair_sem, far_sem, near_sem, peer_sem, own_sem = refs[7 * count :]
    route = Route()
    arrive = greet(route.partners)
    core = route.core
    near, far, pair = (route.near, core), (route.far, core), (route.dp, 1 - core)
    pending, local = [], {}

    def send(source, target, semaphore, partner):
        copy = pltpu.make_async_remote_copy(
            src_ref=source,
            dst_ref=target,
            send_sem=send_sem.at[len(pending)],
            recv_sem=semaphore,
            device_id=partner,
            device_id_type=MESH,
        )
        copy.start()
        pending.append(copy)

    def landed(block, semaphore):
        pltpu.make_async_copy(block, block, semaphore).wait()

    far_list = [route.at_level(base, step) for step in range(4) for base in (route.far, route.both)]
    near_list = [route.at_level(route.near, step) for step in range(4)]
    own_list = route.levels
    for piece in order:
        for index, dp in enumerate(far_list + near_list + own_list):
            copy = pltpu.make_async_copy(
                grads[piece].at[dp * 2 + core], own[piece].at[index], own_sem.at[piece, index]
            )
            copy.start()
            local[piece, index] = copy
    arrive()
    for piece in order:
        for dp in range(ROUTED_DP):
            send(
                grads[piece].at[dp * 2 + 1 - core],
                from_pair[piece].at[dp],
                pair_sem.at[piece, dp],
                pair,
            )

    def total(piece, index, dp, sources):
        local[piece, index].wait()
        landed(from_pair[piece].at[dp], pair_sem.at[piece, dp])
        found = own[piece][index].astype(F32) + from_pair[piece][dp].astype(F32)
        for block, semaphore, slot in sources:
            landed(block.at[slot], semaphore.at[piece, slot])
            found = found + block[slot].astype(F32)
        return found

    def stage_far(piece):
        for index, dp in enumerate(far_list):
            own[piece][index] = total(piece, index, dp, ()).astype(BF)
            send(own[piece].at[index], from_far[piece].at[index], far_sem.at[piece, index], far)

    def stage_near(piece):
        for step, dp in enumerate(near_list):
            index = 8 + step
            found = total(piece, index, dp, ((from_far[piece], far_sem, step * 2 + 1),))
            own[piece][index] = found.astype(BF)
            send(own[piece].at[index], from_near[piece].at[step], near_sem.at[piece, step], near)

    def stage_peer(piece):
        for step in (1, 2, 3):
            index = 12 + step
            dp = own_list[step]
            found = total(
                piece,
                index,
                dp,
                ((from_far[piece], far_sem, step * 2), (from_near[piece], near_sem, step)),
            )
            own[piece][index] = found.astype(BF)
            send(
                own[piece].at[index],
                from_peer[piece].at[step - 1],
                peer_sem.at[piece, step - 1],
                (route.peers[step - 1], core),
            )

    def stage_own(piece):
        found = total(
            piece,
            12,
            own_list[0],
            ((from_far[piece], far_sem, 0), (from_near[piece], near_sem, 0))
            + tuple((from_peer[piece], peer_sem, slot) for slot in range(3)),
        )
        outs[piece][...] = found

    stages = (stage_far, stage_near, stage_peer, stage_own)
    for turn in range(len(order) + 3):
        for late, stage in enumerate(stages):
            if 0 <= turn - late < len(order):
                stage(order[turn - late])
    for copy in pending:
        copy.wait_send()


def scatter_gradients(grads, shapes, devices):
    count = len(shapes)
    order = (EXPAND, REDUCE, ALIGN, ENTRY, TABLE, EXIT)
    rows = devices // 2

    def buffers(slots):
        return [pltpu.VMEM((slots,) + shape, BF) for shape in shapes]

    return pl.pallas_call(
        functools.partial(scatter_kernel, shapes, order),
        out_shape=[jax.ShapeDtypeStruct(shape, F32) for shape in shapes],
        in_specs=[ANY] * count,
        out_specs=[VMEM] * count,
        scratch_shapes=buffers(rows)
        + buffers(rows)
        + buffers(8)
        + buffers(4)
        + buffers(3)
        + [
            pltpu.SemaphoreType.DMA((31 * count,)),
            pltpu.SemaphoreType.DMA((count, rows)),
            pltpu.SemaphoreType.DMA((count, 8)),
            pltpu.SemaphoreType.DMA((count, 4)),
            pltpu.SemaphoreType.DMA((count, 3)),
            pltpu.SemaphoreType.DMA((count, rows)),
        ],
        compiler_params=pltpu.CompilerParams(
            collective_id=1, has_side_effects=True, vmem_limit_bytes=60 * MIB
        ),
        name="scatter_gradients",
    )(*grads)


def exchange_kernel(devices, part, out, held, send_sem, recv_sem):
    dp = lax.axis_index("dp")
    core = lax.axis_index("tensor")
    me = dp * 2 + core
    barrier = pltpu.get_barrier_semaphore()

    def partner(step):
        other = lax.rem(me + step, devices)
        return other, (other // 2, lax.rem(other, 2))

    def hail(step, carry):
        pl.semaphore_signal(
            barrier, inc=1, device_id=partner(step)[1], device_id_type=MESH
        )
        return carry

    lax.fori_loop(1, devices, hail, 0)
    held[me] = part[...]
    pl.semaphore_wait(barrier, devices - 1)

    def copy_to(step):
        return pltpu.make_async_remote_copy(
            src_ref=held.at[me],
            dst_ref=held.at[me],
            send_sem=send_sem.at[step],
            recv_sem=recv_sem.at[me],
            device_id=partner(step)[1],
            device_id_type=MESH,
        )

    def start(step, carry):
        copy_to(step).start()
        return carry

    def take(step, carry):
        other = partner(step)[0]
        block = held.at[other]
        pltpu.make_async_copy(block, block, recv_sem.at[other]).wait()
        return carry

    def sent(step, carry):
        copy_to(step).wait_send()
        return carry

    lax.fori_loop(1, devices, start, 0)
    lax.fori_loop(1, devices, take, 0)
    out[...] = jnp.sum(held[...], axis=0)
    lax.fori_loop(1, devices, sent, 0)


def exchange_sums(part, devices):
    return pl.pallas_call(
        functools.partial(exchange_kernel, devices),
        out_shape=jax.ShapeDtypeStruct(part.shape, F32),
        in_specs=[VMEM],
        out_specs=VMEM,
        scratch_shapes=[
            pltpu.VMEM((devices,) + part.shape, F32),
            pltpu.SemaphoreType.DMA((devices,)),
            pltpu.SemaphoreType.DMA((devices,)),
        ],
        compiler_params=pltpu.CompilerParams(collective_id=2, has_side_effects=True),
        name="exchange_sums",
    )(part)


def lane_marks(head, segment_column):
    lane = lax.broadcasted_iota(jnp.int32, (segment_column.shape[0], 128), 1)
    mine = (lane // HD) == head
    same = (lane % HD) == segment_column
    return mine, same


def attend_kernel(segment, query, key, value, out):
    rows = query.shape[0]
    chunk = 256
    for head in (0, 1):
        mine, same = lane_marks(head, segment[...])
        keys = jnp.where(mine, key[...], jnp.where(same, 0.0, -1e30).astype(BF))
        queries = jnp.where(mine, query[...] * BF(HD**-0.5), same.astype(BF))
        values = value[...]
        for start in range(0, rows, chunk):
            scores = contract(queries[start : start + chunk], keys, 1, 1)
            peak = jnp.max(scores, axis=1, keepdims=True)
            raised = jnp.exp(scores - peak)
            scale = 1.0 / jnp.sum(raised, axis=1, keepdims=True)
            attention = (raised * scale).astype(BF)
            result = contract(attention, values, 1, 0).astype(BF)
            span = slice(start, start + chunk)
            if head == 0:
                out[span, :] = result
            else:
                out[span, :] = jnp.where(mine[span], result, out[span, :])


def attend(segment, joint):
    rows, width = joint.shape[0], joint.shape[1] // 3
    pairs = width // 128
    return pl.pallas_call(
        attend_kernel,
        grid=(pairs,),
        out_shape=jax.ShapeDtypeStruct((rows, width), BF),
        in_specs=[
            pl.BlockSpec((rows, 1), lambda pair: (0, 0)),
            pl.BlockSpec((rows, 128), lambda pair: (0, pair)),
            pl.BlockSpec((rows, 128), lambda pair: (0, pairs + pair)),
            pl.BlockSpec((rows, 128), lambda pair: (0, 2 * pairs + pair)),
        ],
        out_specs=pl.BlockSpec((rows, 128), lambda pair: (0, pair)),
        compiler_params=pltpu.CompilerParams(vmem_limit_bytes=40 * MIB),
        name="attend",
    )(segment, joint, joint, joint)


def attend_back_kernel(segment, query, key, value, grad, out, key_sum, value_sum):
    rows = query.shape[0]
    chunk = 256
    scale = HD**-0.5
    for head in (0, 1):
        mine, same = lane_marks(head, segment[...])
        keys = jnp.where(mine, key[...], jnp.where(same, 0.0, -1e30).astype(BF))
        scaled = query[...] * BF(scale)
        queries = jnp.where(mine, scaled, same.astype(BF))
        zero = jnp.zeros_like(scaled)
        pure_queries = jnp.where(mine, scaled, zero)
        pure_keys = jnp.where(mine, key[...], zero)
        grads = jnp.where(mine, grad[...], zero)
        values = value[...]
        for start in range(0, rows, chunk):
            span = slice(start, start + chunk)
            scores = contract(keys, queries[span], 1, 1)
            peak = jnp.max(scores, axis=0, keepdims=True)
            raised = jnp.exp(scores - peak)
            attention = raised * (1.0 / jnp.sum(raised, axis=0, keepdims=True))
            grad_values = contract(attention.astype(BF), grads[span], 1, 0)
            grad_attention = contract(values, grads[span], 1, 1)
            inner = jnp.sum(attention * grad_attention, axis=0, keepdims=True)
            grad_score = (attention * (grad_attention - inner)).astype(BF)
            grad_keys = contract(grad_score, pure_queries[span], 1, 0)
            grad_queries = contract(grad_score, pure_keys, 0, 0) * scale
            if head == 0:
                out[0, span, :] = grad_queries.astype(BF)
            else:
                out[0, span, :] = jnp.where(mine[span], grad_queries.astype(BF), out[0, span, :])
            if head == 0 and start == 0:
                key_sum[...] = grad_keys
                value_sum[...] = grad_values
            else:
                key_sum[...] += grad_keys
                value_sum[...] += grad_values
    out[1] = key_sum[...].astype(BF)
    out[2] = value_sum[...].astype(BF)


def attend_back(segment, joint, grad_attended):
    rows, width = grad_attended.shape
    pairs = width // 128
    return pl.pallas_call(
        attend_back_kernel,
        grid=(pairs,),
        out_shape=jax.ShapeDtypeStruct((3, rows, width), BF),
        in_specs=[
            pl.BlockSpec((rows, 1), lambda pair: (0, 0)),
            pl.BlockSpec((rows, 128), lambda pair: (0, pair)),
            pl.BlockSpec((rows, 128), lambda pair: (0, pairs + pair)),
            pl.BlockSpec((rows, 128), lambda pair: (0, 2 * pairs + pair)),
            pl.BlockSpec((rows, 128), lambda pair: (0, pair)),
        ],
        out_specs=pl.BlockSpec((3, rows, 128), lambda pair: (0, 0, pair)),
        scratch_shapes=[pltpu.VMEM((rows, 128), F32), pltpu.VMEM((rows, 128), F32)],
        compiler_params=pltpu.CompilerParams(vmem_limit_bytes=40 * MIB),
        name="attend_back",
    )(segment, joint, joint, joint, grad_attended)


def moments_kernel(decays, *refs):
    count = len(decays)
    sums = refs[7 * count]
    row = lax.broadcasted_iota(jnp.int32, (16, 128), 0)
    found = jnp.zeros((16, 128), F32)
    for member, decay in enumerate(decays):
        weight, gradient, first, second = refs[4 * member : 4 * member + 4]
        new_first_ref, new_second_ref, update_ref = refs[
            4 * count + 3 * member : 4 * count + 3 * member + 3
        ]
        slope = gradient[...]
        new_first = BETA_ONE * first[...] + (1.0 - BETA_ONE) * slope
        new_second = BETA_TWO * second[...] + (1.0 - BETA_TWO) * slope * slope
        update = new_first / (jnp.sqrt(new_second) + ADAM_EPS) + decay * weight[...]
        new_first_ref[...] = new_first
        new_second_ref[...] = new_second
        update_ref[...] = update
        found = jnp.where(row == member, jnp.sum(weight[...] * weight[...]), found)
        found = jnp.where(row == 8 + member, jnp.sum(update * update), found)
    sums[...] = found


def moments(members, decays):
    shapes = [jax.ShapeDtypeStruct(member[0].shape, F32) for member in members]
    outs = [shape for shape in shapes for _ in range(3)]
    flat = [array for member in members for array in member]
    return pl.pallas_call(
        functools.partial(moments_kernel, decays),
        out_shape=outs + [jax.ShapeDtypeStruct((16, 128), F32)],
        in_specs=[VMEM] * len(flat),
        out_specs=[VMEM] * (len(outs) + 1),
        compiler_params=pltpu.CompilerParams(vmem_limit_bytes=40 * MIB),
        name="moments",
    )(*flat)


def step_kernel(count, *refs):
    sums = refs[0]
    for member in range(count):
        weight, update = refs[1 + 2 * member : 3 + 2 * member]
        weight_square = sums[member : member + 1, :]
        update_square = sums[8 + member : 9 + member, :]
        trust = jnp.sqrt(weight_square) / jnp.sqrt(update_square + TINY)
        if weight.shape[1] % 128 == 0:
            trust = jnp.concatenate([trust] * (weight.shape[1] // 128), axis=1)
        else:
            trust = trust[:, : weight.shape[1]]
        refs[1 + 2 * count + member][...] = weight[...] - RATE * trust * update[...]


def take_step(sums, pairs):
    count = len(pairs)
    return pl.pallas_call(
        functools.partial(step_kernel, count),
        out_shape=[jax.ShapeDtypeStruct(weight.shape, F32) for weight, _ in pairs],
        in_specs=[VMEM] * (1 + 2 * count),
        out_specs=[VMEM] * count,
        compiler_params=pltpu.CompilerParams(vmem_limit_bytes=40 * MIB),
        name="take_step",
    )(sums, *[array for pair in pairs for array in pair])


def as_rows(flat):
    if flat.ndim == 2:
        return flat
    lanes = max(size for size in range(1, 129) if flat.shape[0] % size == 0)
    return flat.reshape(-1, lanes)


def local(
    tokens,
    kept_patches,
    clip_lengths,
    clip_device,
    cot_output,
    cot_aligned,
    entry_weight,
    entry_first,
    entry_second,
    exit_weight,
    exit_first,
    exit_second,
    align_weight,
    align_first,
    align_second,
    expand_weight,
    expand_first,
    expand_second,
    reduce_weight,
    reduce_first,
    reduce_second,
    position_table,
    position_first,
    position_second,
    norm_params,
    norm_first,
    norm_second,
):
    rows, width = tokens.shape
    align_width = cot_aligned.shape[1]
    axes = ("dp", "tensor")
    pair = lax.axis_size("tensor")
    devices = lax.axis_size("dp") * pair
    hidden = expand_weight.shape[0] * devices
    positions = position_table.shape[0] * devices // width
    routed = devices == 2 * ROUTED_DP and pair == 2
    device = lax.axis_index("dp") * pair + lax.axis_index("tensor")
    segment, valid_rows = row_layout(clip_lengths, clip_device, device, rows)
    segment_column = segment[:, None]
    valid_column = valid_rows[:, None]
    shapes = (
        (TABLE_SLAB, width),
        (width // devices, 3 * width),
        (width // devices, width),
        (hidden // devices, width),
        (hidden // devices, width),
        (width // devices, align_width),
    )
    wholes = (
        (positions, width),
        (width, 3 * width),
        (width, width),
        (hidden, width),
        (hidden, width),
        (width, align_width),
    )
    masters = (position_table, entry_weight, exit_weight, expand_weight, reduce_weight, align_weight)
    if routed:
        blocks = gather_weights(
            [as_rows(master) for master in masters], norm_params.reshape(1, -1), shapes, devices
        )
        lows = [block.reshape(-1, block.shape[2]) for block in blocks]
        norm_low = blocks[TABLE][:, TABLE_ROWS, :NORM_LANES].reshape(4, width)
        patch = kept_patches + (kept_patches // TABLE_ROWS) * (TABLE_SLAB - TABLE_ROWS)
    else:
        lows = [
            lax.all_gather(master.astype(BF).reshape(-1), axes, axis=0, tiled=True).reshape(whole)
            for master, whole in zip(masters, wholes)
        ]
        norm_low = lax.all_gather(norm_params.astype(BF), axes, axis=0, tiled=True).reshape(4, width)
        patch = kept_patches
    table_low, entry_low, exit_low, expand_low, reduce_low, align_low = lows
    norm_low = norm_low.astype(F32)

    residual = tokens.astype(F32) + jnp.take(table_low, patch, axis=0).astype(F32)
    normed_one = layer_norm(residual, norm_low[0], norm_low[1]).astype(BF)
    joint_low = contract(normed_one, entry_low, 1, 0).astype(BF)
    attended = attend(segment_column, joint_low)
    middle = residual + contract(attended, exit_low, 1, 0)
    normed_two = layer_norm(middle, norm_low[2], norm_low[3]).astype(BF)
    hidden_pre = contract(normed_two, expand_low, 1, 1)
    hidden_act = gelu_exact(hidden_pre).astype(BF)
    out_low = (middle + contract(hidden_act, reduce_low, 1, 0)).astype(BF)
    block_out = jnp.where(valid_column, out_low, jnp.zeros_like(out_low))
    align_rows = contract(out_low, align_low, 1, 0).astype(BF)
    aligned = jnp.where(valid_column, align_rows, jnp.zeros_like(align_rows))
    cot_align_valid = jnp.where(valid_column, cot_aligned, jnp.zeros_like(cot_aligned))
    grad_align = contract(out_low, cot_align_valid, 0, 0).astype(BF)
    grad_out = jnp.where(valid_column, cot_output.astype(F32), 0.0) + contract(
        cot_align_valid, align_low, 1, 1
    )
    grad_feed = grad_out.astype(BF)
    grad_act = contract(grad_feed, reduce_low, 1, 1)
    gelu_value, gelu_back = jax.vjp(gelu_exact, hidden_pre)
    grad_pre = gelu_back(grad_act)[0].astype(BF)
    grad_reduce = contract(hidden_act, grad_feed, 0, 0).astype(BF)
    grad_expand = contract(grad_pre, normed_two, 0, 0).astype(BF)
    grad_two = contract(grad_pre, expand_low, 1, 0)
    norm_value, norm_back_two = jax.vjp(layer_norm, middle, norm_low[2], norm_low[3])
    grad_from_two, grad_gain_two, grad_shift_two = norm_back_two(grad_two)
    grad_middle = grad_out + grad_from_two
    grad_branch = grad_middle.astype(BF)
    grad_exit = contract(attended, grad_branch, 0, 0).astype(BF)
    grad_attended = contract(grad_branch, exit_low, 1, 1).astype(BF)
    grad_parts = attend_back(segment_column, joint_low, grad_attended)
    grad_joint = jnp.concatenate([grad_parts[0], grad_parts[1], grad_parts[2]], axis=1)
    grad_entry = contract(normed_one, grad_joint, 0, 0).astype(BF)
    grad_one = contract(grad_joint, entry_low, 1, 1)
    norm_value_one, norm_back_one = jax.vjp(layer_norm, residual, norm_low[0], norm_low[1])
    grad_from_one, grad_gain_one, grad_shift_one = norm_back_one(grad_one)
    token_grad = grad_middle + grad_from_one
    picks = (patch[:, None] == jnp.arange(table_low.shape[0], dtype=jnp.int32)[None, :]).astype(BF)
    grad_table = contract(picks, token_grad.astype(BF), 0, 0)
    grad_norms = jnp.concatenate((grad_gain_one, grad_shift_one, grad_gain_two, grad_shift_two))
    if routed:
        table_part = grad_table.astype(BF).reshape(devices, TABLE_SLAB, width)
        norm_part = grad_norms.reshape(devices, NORM_LANES)
        norm_high = norm_part.astype(BF)
        norm_rest = (norm_part - norm_high.astype(F32)).astype(BF)
        extra = jnp.stack((norm_high, norm_rest), axis=1)
        table_part = table_part.at[:, TABLE_ROWS : TABLE_ROWS + 2, :NORM_LANES].set(extra)
        grads = (table_part, grad_entry, grad_exit, grad_expand, grad_reduce, grad_align)
        summed = scatter_gradients(
            [grad.reshape((devices,) + shape) for grad, shape in zip(grads, shapes)], shapes, devices
        )
        table_sum = summed[TABLE]
        norm_sum = (table_sum[TABLE_ROWS] + table_sum[TABLE_ROWS + 1])[:NORM_LANES]
        summed = [table_sum[:TABLE_ROWS]] + list(summed[1:])
    else:
        grads = (grad_table, grad_entry, grad_exit, grad_expand, grad_reduce, grad_align)
        summed = [
            lax.psum_scatter(grad.reshape(-1).astype(F32), axes, scatter_dimension=0, tiled=True)
            for grad in grads
        ]
        norm_sum = lax.psum_scatter(grad_norms, axes, scatter_dimension=0, tiled=True)

    def summed_like(master, index):
        return summed[index].reshape(master.shape)

    members = (
        (entry_weight, summed_like(entry_weight, ENTRY), entry_first, entry_second),
        (exit_weight, summed_like(exit_weight, EXIT), exit_first, exit_second),
        (align_weight, summed_like(align_weight, ALIGN), align_first, align_second),
        (expand_weight, summed_like(expand_weight, EXPAND), expand_first, expand_second),
        (reduce_weight, summed_like(reduce_weight, REDUCE), reduce_first, reduce_second),
        (position_table, summed_like(position_table, TABLE), position_first, position_second),
        (norm_params, norm_sum, norm_first, norm_second),
    )
    decays = (DECAY, DECAY, DECAY, DECAY, DECAY, DECAY, 0.0)
    members = [tuple(as_rows(array) for array in member) for member in members]
    found = moments(members, decays)
    sums = found[-1]
    sums = exchange_sums(sums, devices) if routed else lax.psum(sums, axes)
    stepped = take_step(
        sums, [(members[member][0], found[3 * member + 2]) for member in range(len(members))]
    )
    weight_squares, update_squares = sums[0:7, 0], sums[8:15, 0]
    trust = jnp.sqrt(weight_squares) / jnp.sqrt(update_squares + TINY)
    outputs = [block_out, aligned, token_grad]
    originals = (
        entry_weight,
        exit_weight,
        align_weight,
        expand_weight,
        reduce_weight,
        position_table,
        norm_params,
    )
    for member, original in enumerate(originals):
        for array in (found[3 * member], found[3 * member + 1], stepped[member]):
            outputs.append(array.reshape(original.shape))
    outputs.append(jnp.stack((trust, jnp.sqrt(weight_squares), jnp.sqrt(update_squares))))
    return tuple(outputs)


def solution(mesh):
    both = ("dp", "tensor")
    rows, flat, whole = P(both, None), P(both), P()
    weight_specs = (flat,) * 9 + (rows,) * 6 + (flat,) * 6
    placed = (rows, flat, whole, whole, rows, rows) + weight_specs
    return jax.shard_map(
        local,
        mesh=mesh,
        in_specs=placed,
        out_specs=(rows, rows, rows) + weight_specs + (whole,),
        check_vma=False,
    )
```

time: 1180 us -> 485 us (0.41)
  waiting for transfers between devices: 526 us -> 0 us
  Pallas kernels: 0 us -> 283 us
  matrix products: 248 us -> 101 us
  blocking collectives: 121 us -> 0 us
  other arithmetic: 125 us -> 25.9 us
  local copies, waits for them, and re-layouts: 122 us -> 63.6 us
  between operations: 19.4 us -> 2.05 us
    pallas_call x0 -> x7, Pallas kernels: none -> 283 us  [the longest x1 102 us: scatter_gradients(): pl.pallas_call(functools.partial(scatter_kernel, shapes, order), out_shap...]
    unnamed x14 -> x0, waiting for transfers between devices: 241 us -> none
    all_gather x8 -> x0, waiting for transfers between devices: 150 us -> none  [the longest x1 64.5 us: local(): lax.all_gather(position_table.astype(jnp.bfloat16), ('dp', 'tensor'), axi...]
    reduce_scatter x4 -> x0, waiting for transfers between devices: 136 us -> none  [the longest x1 136 us: local(): lax.psum_scatter(grad_reduce, 'dp', scatter_dimension=0, tiled=True)]
    unnamed x2 -> x0, blocking collectives: 81.7 us -> none
    dot_general x70 -> x16, matrix products: 180 us -> 101 us  [contract(): lax.dot_general(left, right, (((left_dim,), (right_dim,)), ((), ())), pre...]
    dot_general x29 -> x0, matrix products: 67.9 us -> none  [the longest x12 25.3 us: head_forward(): jnp.dot(attention.astype(jnp.bfloat16), value_rows, preferred_element_typ...]
    all_gather x1 -> x0, other arithmetic: 51.2 us -> none  [local(): lax.all_gather(position_table.astype(jnp.bfloat16), ('dp', 'tensor'), axi...]
  transfers between devices with their start and end apart: 13 -> 0, of which waited for: 7 -> 0; matrix products, arithmetic and copies ran while one was open for 37% -> 0% of each run, Pallas kernels for 0% -> 0%
where the time goes in v1:
time: 485 us; the launch traced here: 476 us
  Pallas kernels  283 us (58%)
  matrix products  101 us (21%)
  local copies, waits for them, and re-layouts  63.6 us (13%)
  other arithmetic  25.9 us (5%)
    pallas_call x1, Pallas kernels, scatter_gradients(): pl.pallas_call(functools.partial(scatter_kernel, shapes, order), out_shap...  102 us
    pallas_call x1, Pallas kernels, gather_weights(): pl.pallas_call(functools.partial(gather_kernel, shapes, groups), out_shap...  101 us
    dot_general x16, matrix products, contract(): lax.dot_general(left, right, (((left_dim,), (right_dim,)), ((), ())), pre...  101 us
    unnamed x197, local copies, waits for them, and re-layouts  41.2 us
    pallas_call x1, Pallas kernels, attend_back(): pl.pallas_call(attend_back_kernel, grid=(pairs,), out_shape=jax.ShapeDtyp...  39.7 us
    pallas_call x1, Pallas kernels, attend(): pl.pallas_call(attend_kernel, grid=(pairs,), out_shape=jax.ShapeDtypeStru...  21.6 us
    pallas_call x1, Pallas kernels, exchange_sums(): pl.pallas_call(functools.partial(exchange_kernel, devices), out_shape=jax...  15.6 us

profile of v1, /device:TPU:9, one launch (start us, length us, event | category | flops | bytes accessed | tf_op | source)
XLA Modules:
  0.0 475.9 jit_solution(5115371680936955982)
XLA Ops:
  0.7 1.4 fusion.32
  6.0 1.6 reshape_select_fusion.segment
  7.5 2.4 copy.77
  10.0 1.4 copy.82
  11.4 0.9 copy-done.6
  12.4 0.9 copy-done.12
  13.3 0.9 copy-done.14
  14.2 101.4 %gather_weights.1 = (bf16[32,56,768]{2,1,0:T(8,128)(2,1)S(1)}, bf16[32,24,2304]{2,1,0:T(8,128)(2,1)S(1)}, bf16[32,24,768]{2,1,0:T(8,128)(2,1)S(1)}, bf16[32,96,7...) custom-call(f32[294,128]{1,0:T(8,128)S(1)} %bitcast.80, ...), custom_call_target="tpu_custom_call" | custom-call | tf_op jit(solution)/shard_map/gather_weights/pallas_call | solution.py:188
  115.6 1.7 copy-done.45
  117.3 1.1 copy-done.48
  118.5 1.0 copy-done.50
  120.5 3.4 gather_fusion
  123.9 1.7 copy.78
  128.3 1.5 select_add_fusion
  131.0 3.5 convolution_convert_fusion.1.query.key.value
  134.5 21.6 %attend.1 = bf16[768,768]{1,0:T(8,128)(2,1)S(1)} custom-call(s32[768,1]{1,0:T(8,128)S(1)} %copy-done, bf16[768,2304]{1,0:T(8,128)(2,1)S(1)} %convolution_convert_fusion.1.query.key.value, bf16[768,2304]{1,0:T(8,128)(2,1)S(1)} %convolution_convert_fusion.1.query.key.value, bf16[768,2304]{1,0:T(8,128)(2,1)S(1)} %convolution_convert_fusion.1.query.key.value), custom_call_target="tpu_custom_call" | custom-call | tf_op jit(solution)/shard_map/attend/pallas_call | solution.py:446
  156.1 1.3 fusion.40
  158.1 26.8 %multiply_convert_fusion = (bf16[768,3072]{1,0:T(8,128)(2,1)}, f32[768,3072]{1,0:T(8,128)}, f32[768,3072]{1,0:T(8,128)}) fusion(bf16[3072,768]{1,0:T(8,128)(2,1)S(1)} %bitcast.119, f32[768,768]{0,1:T(8,128)S(1)} %get-tuple-element.221, f32[768]{0:T(1024)S(1)} %copy-done.83, f32[768]{0:T(1024)S(1)} %mul.173, f32[768]{0:T(1024)S(1)} %fusion.25, ...), kind=kOutput, calls=%fused_computation.4 | convolution fusion | flops 3780182016 | bytes 30683136 | tf_op jit(solution)/shard_map/dot_general | solution.py:34
  185.0 13.0 %add_convert_fusion = bf16[768,3072]{1,0:T(8,128)(2,1)} fusion(f32[768,3072]{1,0:T(8,128)} %get-tuple-element.208, f32[768,3072]{1,0:T(8,128)} %get-tuple-element.222, bf16[3072,768]{1,0:T(8,128)(2,1)} %bitcast.123, f32[768,768]{0,1:T(8,128)S(1)} %select_add_fusion), kind=kOutput, calls=%fused_computation.3 | convolution fusion | flops 3657498624 | bytes 30670848 | tf_op jit(solution)/shard_map/dot_general | solution.py:34
  198.0 9.2 %broadcast_select_fusion.3 = (bf16[768,768]{0,1:T(8,128)(2,1)}, bf16[768,768]{0,1:T(8,128)(2,1)}) fusion(pred[768]{0:T(1024)(128)(4,1)S(1)} %copy-done.87, f32[768,768]{0,1:T(8,128)S(1)} %get-tuple-element.221, bf16[768,3072]{1,0:T(8,128)(2,1)} %get-tuple-element.207, bf16[3072,768]{1,0:T(8,128)(2,1)} %bitcast.124), kind=kOutput, calls=%fused_computation.57 | convolution fusion | flops 3625648128 | bytes 14156544 | tf_op jit(solution)/shard_map/dot_general | solution.py:34
  207.3 5.8 %fusion.42 = (f32[768]{0:T(1024)}, f32[768,768]{1,0:T(8,128)}) fusion(bf16[768,3072]{1,0:T(8,128)(2,1)S(1)} %copy-done.90, bf16[3072,768]{1,0:T(8,128)(2,1)S(1)} %bitcast.122), kind=kOutput, calls=%fused_computation.120 | convolution fusion | flops 3624467712 | bytes 11799552 | tf_op jit(solution)/shard_map/dot_general | solution.py:34
  213.1 6.5 %convolution_convert_fusion.3 = bf16[3072,768]{1,0:T(8,128)(2,1)} fusion(bf16[768,3072]{1,0:T(8,128)(2,1)S(1)} %copy-done.90, f32[768,768]{0,1:T(8,128)S(1)} %get-tuple-element.221, f32[768]{0:T(1024)S(1)} %copy-done.83, f32[768]{0:T(1024)S(1)} %mul.173, f32[768]{0:T(1024)S(1)} %fusion.25, f32[768]{0:T(1024)S(1)} %broadcast_multiply_fusion), kind=kOutput, calls=%fused_computation.23 | convolution fusion | flops 3629187072 | bytes 11808768 | tf_op jit(solution)/shard_map/dot_general | solution.py:34
  219.6 2.4 copy.88
  222.0 4.3 broadcast_select_fusion.1
  226.3 1.4 concatenate.39
  227.7 9.4 %convolution_convert_fusion.2 = bf16[3072,768]{1,0:T(8,128)(2,1)} fusion(bf16[768,3072]{1,0:T(8,128)(2,1)} %get-tuple-element.207, f32[768,768]{0,1:T(8,128)} %copy-done.62), kind=kOutput, calls=%fused_computation.22 | convolution fusion | flops 3626827776 | bytes 11796480 | tf_op jit(solution)/shard_map/dot_general | solution.py:34
  237.0 2.7 convolution_convert_fusion.5
  239.7 3.2 copy.84
  243.0 3.7 multiply_reduce_fusion
  246.7 1.4 concatenate.38
  248.7 3.1 fusion.35
  252.3 1.0 copy-done.61
  254.0 2.1 convolution_convert_fusion.7
  256.1 1.1 convolution_convert_fusion.8.grad
  257.3 39.7 %attend_back.1 = bf16[3,768,768]{2,1,0:T(8,128)(2,1)S(1)} custom-call(s32[768,1]{1,0:T(8,128)S(1)} %copy-done.1, bf16[768,2304]{1,0:T(8,128)(2,1)S(1)} %convolution_convert_fusion.1.query.key.value, bf16[768,2304]{1,0:T(8,128)(2,1)S(1)} %convolution_convert_fusion.1.query.key.value, bf16[768,2304]{1,0:T(8,128)(2,1)S(1)} %convolution_convert_fusion.1.query.key.value, ...), custom_call_target="tpu_custom_call" | custom-call | tf_op jit(solution)/shard_map/attend_back/pallas_call | solution.py:505
  297.3 1.8 copy-done.47
  299.1 4.3 fusion.41
  303.5 5.2 %convolution_convert_fusion = bf16[768,2304]{1,0:T(8,128)(2,1)} fusion(bf16[768,768]{1,0:T(8,128)(2,1)S(1)} %get-tuple-element.214, bf16[768,768]{1,0:T(8,128)(2,1)S(1)} %get-tuple-element.215, bf16[768,768]{1,0:T(8,128)(2,1)S(1)} %get-tuple-element.213, bf16[768,768]{0,1:T(8,128)(2,1)S(1)} %copy-done.55, f32[768]{0:T(1024)S(1)} %copy-done.82, ...), kind=kOutput, calls=%fused_computation.20 | convolution fusion | flops 2735603712 | bytes 9450240 | tf_op jit(solution)/shard_map/dot_general | solution.py:34
  308.8 3.0 copy.85
  311.9 2.4 multiply_reduce_fusion.2
  314.4 1.3 multiply_reduce_fusion.1
  315.7 5.6 %add_add_fusion.2 = f32[768,768]{0,1:T(8,128)} fusion(f32[768]{0:T(1024)S(1)} %negate_multiply_fusion.1, f32[768,768]{0,1:T(8,128)} %copy-done.62, f32[768,768]{0,1:T(8,128)} %copy-done.61, f32[768]{0:T(1024)S(1)} %negate_multiply_fusion.2, f32[768]{0:T(1024)S(1)} %multiply_multiply_fusion.5, f32[768]{0:T(1024)S(1)} %copy-done.68, ...), kind=kLoop, calls=%fused_computation.31 | loop fusion | flops 8257536 | bytes 11815680 | tf_op jit(solution)/shard_map/add | solution.py:703
  321.5 3.2 copy.89
  324.7 4.1 convolution_convert_fusion.4
  328.8 2.4 scatter.4.refs_0_
  331.3 101.5 %scatter_gradients.1 = (f32[56,768]{1,0:T(8,128)}, f32[24,2304]{1,0:T(8,128)}, f32[24,768]{1,0:T(8,128)}, f32[96,768]{1,0:T(8,128)}, f32[96,768]{1,0:T(8,128)}, /*index=5*/f32[24,1024]{1,0:T(8,128)}) custom-call(bf16[32,56,768]{2,1,0:T(8,128)(2,1)} %scatter.4.refs_0_, bf16[32,24,2304]{2,1,0:T(8,128)(2,1)} %bitcast.110, bf16[32,24,768]{2,1,0:T(8,128)(2,1)} %bitcast.113, ...), custom_call_target="tpu_custom_call" | custom-call | tf_op jit(solution)/shard_map/scatter_gradients/pallas_call | solution.py:323
  432.8 1.0 reshape_reshape.12.refs_1_
  435.1 0.9 reshape_reshape.13.refs_5_
  436.0 0.9 reshape_reshape.14.refs_9_
  436.9 0.9 reshape_reshape.15.refs_21_
  438.0 1.0 copy-done.20
  438.9 1.0 copy-done.21
  439.9 0.9 copy-done.22
  440.8 0.9 copy-done.23
  441.8 0.9 copy-done.28
  442.7 0.9 copy-done.29
  443.6 0.9 copy-done.30
  444.5 0.9 copy-done.31
  448.5 2.3 moments.1
  453.9 15.6 %exchange_sums.1.refs_0_ = f32[16,128]{1,0:T(8,128)} custom-call(f32[16,128]{1,0:T(8,128)} %copy-done.37), custom_call_target="tpu_custom_call" | custom-call | tf_op jit(solution)/shard_map/exchange_sums/pallas_call | solution.py:399
  469.5 0.9 copy-done.25
  470.5 0.9 copy-done.27
  472.1 0.9 copy-done.34
  473.6 1.1 take_step.1
  (215 shorter events, 21.4 us)
Async XLA Ops:
  0.7 9.3 %copy-start.65 = (bf16[768,768]{1,0:T(8,128)(2,1)S(1)}, bf16[768,768]{1,0:T(8,128)(2,1)}, u32[]{:S(2)}) copy-start(bf16[768,768]{1,0:T(8,128)(2,1)} %param.33) | copy-start | bytes 3538948
  3.4 123.3 %copy-start.86 = (pred[768]{0:T(1024)(128)(4,1)}, pred[768]{0:T(1024)(128)(4,1)S(1)}, u32[]{:S(2)}) copy-start(pred[768]{0:T(1024)(128)(4,1)S(1)} %iota_compare_fusion.3) | copy-start | bytes 2308
  4.1 152.0 %copy-start.75 = (pred[768]{0:T(1024)(128)(4,1)}, pred[768]{0:T(1024)(128)(4,1)S(1)}, u32[]{:S(2)}) copy-start(pred[768]{0:T(1024)(128)(4,1)S(1)} %get-tuple-element.209) | copy-start | bytes 2308
  7.5 3.9 copy-start.2
  7.5 3.9 copy-start.4
  7.5 3.9 copy-start.8
  7.5 3.9 copy-start.38
  115.6 1.8 copy-start.45
  119.7 10.1 %copy-start.69 = (f32[768]{0:T(1024)}, f32[768]{0:T(1024)S(1)}, u32[]{:S(2)}) copy-start(f32[768]{0:T(1024)S(1)} %mul.167) | copy-start | bytes 9220
  120.5 9.3 %copy-start.81 = (f32[768]{0:T(1024)}, f32[768]{0:T(1024)S(1)}, u32[]{:S(2)}) copy-start(f32[768]{0:T(1024)S(1)} %add.98) | copy-start | bytes 9220
  123.9 1.7 copy-start.53
  125.6 1.8 copy-start.49
  125.6 2.2 copy-start.66
  125.6 2.6 copy-start.84
  126.0 3.7 copy-start.67
  126.6 3.2 copy-start.71
  128.3 1.6 copy-start.73
  128.3 2.0 copy-start.46
  128.3 2.3 copy-start.54
  128.3 2.7 copy-start.57
  130.9 54.0 %copy-start.62 = (f32[768,768]{0,1:T(8,128)}, f32[768,768]{0,1:T(8,128)S(1)}, u32[]{:S(2)}) copy-start(f32[768,768]{0,1:T(8,128)S(1)} %select_add_fusion) | copy-start | bytes 7077892
  130.9 3.5 copy-start
  131.0 26.8 %slice-start = ((s8[4718592]{0:T(1024)(128)(4,1)}), s8[4194304]{0:T(1024)(128)(4,1)S(1)}, s32[]{:S(2)}) async-start(s8[4718592]{0:T(1024)(128)(4,1)} %bitcast.117), calls=%async_computation | async-start | bytes 8388608
  134.4 21.7 %copy-start.51 = (bf16[32,24,768]{2,1,0:T(8,128)(2,1)S(1)}, bf16[32,24,768]{2,1,0:T(8,128)(2,1)}, u32[]{:S(2)}) copy-start(bf16[32,24,768]{2,1,0:T(8,128)(2,1)} %copy-done.50) | copy-start | bytes 3538948
  134.4 23.3 %slice-start.1 = ((s8[4718592]{0:T(1024)(128)(4,1)}), s8[524288]{0:T(1024)(128)(4,1)S(1)}, s32[]{:S(2)}) async-start(s8[4718592]{0:T(1024)(128)(4,1)} %bitcast.117), calls=%async_computation.1 | async-start | bytes 1048576
  156.1 1.3 copy-start.10
  156.1 51.1 %slice-start.2 = ((s8[4718592]{0:T(1024)(128)(4,1)}), s8[524288]{0:T(1024)(128)(4,1)S(1)}, s32[]{:S(2)}) async-start(s8[4718592]{0:T(1024)(128)(4,1)} %bitcast.120), calls=%async_computation.2 | async-start | bytes 1048576
  157.4 55.7 %copy-start.60 = (f32[768,768]{0,1:T(8,128)}, f32[768,768]{0,1:T(8,128)S(1)}, u32[]{:S(2)}) copy-start(f32[768,768]{0,1:T(8,128)S(1)} %get-tuple-element.221) | copy-start | bytes 7077892
  158.1 49.1 %slice-start.3 = ((s8[4718592]{0:T(1024)(128)(4,1)}), s8[4194304]{0:T(1024)(128)(4,1)S(1)}, s32[]{:S(2)}) async-start(s8[4718592]{0:T(1024)(128)(4,1)} %bitcast.120), calls=%async_computation.3 | async-start | bytes 8388608
  185.0 13.0 %copy-start.87 = (pred[768]{0:T(1024)(128)(4,1)S(1)}, pred[768]{0:T(1024)(128)(4,1)}, u32[]{:S(2)}) copy-start(pred[768]{0:T(1024)(128)(4,1)} %copy-done.86) | copy-start | bytes 2308
  198.0 9.2 %copy-start.90 = (bf16[768,3072]{1,0:T(8,128)(2,1)S(1)}, bf16[768,3072]{1,0:T(8,128)(2,1)}, u32[]{:S(2)}) copy-start(bf16[768,3072]{1,0:T(8,128)(2,1)} %add_convert_fusion) | copy-start | bytes 14155780
  227.7 9.4 %copy-start.85 = (bf16[768,1024]{1,0:T(8,128)(2,1)S(1)}, bf16[768,1024]{1,0:T(8,128)(2,1)}, u32[]{:S(2)}) copy-start(bf16[768,1024]{1,0:T(8,128)(2,1)} %param.34) | copy-start | bytes 4718596
  227.7 9.4 %copy-start.88 = (pred[768]{0:T(1024)(128)(4,1)S(1)}, pred[768]{0:T(1024)(128)(4,1)}, u32[]{:S(2)}) copy-start(pred[768]{0:T(1024)(128)(4,1)} %copy-done.86) | copy-start | bytes 2308
  227.7 9.4 %copy-start.89 = (bf16[768,768]{0,1:T(8,128)(2,1)S(1)}, bf16[768,768]{0,1:T(8,128)(2,1)}, u32[]{:S(2)}) copy-start(bf16[768,768]{0,1:T(8,128)(2,1)} %get-tuple-element.228) | copy-start | bytes 3538948
  248.7 3.2 copy-start.63
  251.9 1.4 copy-start.61
  251.9 2.1 copy-start.11
  254.0 2.1 copy-start.52
  297.1 2.0 copy-start.47
  299.1 4.4 copy-start.55
  299.1 4.4 copy-start.58
  299.1 4.4 copy-start.68
  299.1 4.4 copy-start.70
  299.1 4.4 copy-start.74
  299.1 4.4 copy-start.76
  299.1 4.4 copy-start.82
  311.9 2.5 copy-start.72
  311.9 2.5 copy-start.59
  315.7 5.6 %copy-start.80 = (f32[8,1,96]{2,1,0:T(1,128)S(1)}, f32[8,1,96]{2,1,0:T(1,128)}, u32[]{:S(2)}) copy-start(f32[8,1,96]{2,1,0:T(1,128)} %concatenate.38) | copy-start | bytes 9220
  315.7 5.6 %copy-start.79 = (f32[8,1,96]{2,1,0:T(1,128)S(1)}, f32[8,1,96]{2,1,0:T(1,128)}, u32[]{:S(2)}) copy-start(f32[8,1,96]{2,1,0:T(1,128)} %concatenate.39) | copy-start | bytes 9220
  321.4 3.2 copy-start.64
  321.5 3.2 copy-start.78
  331.2 106.7 %copy-start.3 = (f32[96,768]{1,0:T(8,128)S(1)}, f32[96,768]{1,0:T(8,128)}, u32[]{:S(2)}) copy-start(f32[96,768]{1,0:T(8,128)} %refs_7_.1) | copy-start | bytes 884740
  331.2 106.7 %copy-start.5 = (f32[96,768]{1,0:T(8,128)S(1)}, f32[96,768]{1,0:T(8,128)}, u32[]{:S(2)}) copy-start(f32[96,768]{1,0:T(8,128)} %refs_9_.1) | copy-start | bytes 884740
  331.2 106.7 %copy-start.7 = (f32[55296]{0:T(1024)S(1)}, f32[55296]{0:T(1024)}, u32[]{:S(2)}) copy-start(f32[55296]{0:T(1024)} %param.35) | copy-start | bytes 663556
  331.2 106.7 %copy-start.9 = (f32[37632]{0:T(1024)S(1)}, f32[37632]{0:T(1024)}, u32[]{:S(2)}) copy-start(f32[37632]{0:T(1024)} %param.50) | copy-start | bytes 451588
  331.2 106.7 %copy-start.13 = (f32[24576]{0:T(1024)S(1)}, f32[24576]{0:T(1024)}, u32[]{:S(2)}) copy-start(f32[24576]{0:T(1024)} %param.41) | copy-start | bytes 294916
  331.2 106.7 %copy-start.15 = (f32[18432]{0:T(1024)S(1)}, f32[18432]{0:T(1024)}, u32[]{:S(2)}) copy-start(f32[18432]{0:T(1024)} %param.38) | copy-start | bytes 221188
  331.2 106.7 %copy-start.16 = (f32[96,768]{1,0:T(8,128)S(1)}, f32[96,768]{1,0:T(8,128)}, u32[]{:S(2)}) copy-start(f32[96,768]{1,0:T(8,128)} %refs_14_.1) | copy-start | bytes 884740
  331.3 106.7 %copy-start.17 = (f32[96,768]{1,0:T(8,128)S(1)}, f32[96,768]{1,0:T(8,128)}, u32[]{:S(2)}) copy-start(f32[96,768]{1,0:T(8,128)} %refs_15_.1) | copy-start | bytes 884740
  331.3 106.7 %copy-start.18 = (f32[96,768]{1,0:T(8,128)S(1)}, f32[96,768]{1,0:T(8,128)}, u32[]{:S(2)}) copy-start(f32[96,768]{1,0:T(8,128)} %refs_18_.1) | copy-start | bytes 884740
  331.3 106.7 %copy-start.19 = (f32[96,768]{1,0:T(8,128)S(1)}, f32[96,768]{1,0:T(8,128)}, u32[]{:S(2)}) copy-start(f32[96,768]{1,0:T(8,128)} %refs_19_.1) | copy-start | bytes 884740
  331.3 106.7 %copy-start.39 = (f32[96]{0:T(128)S(1)}, f32[96]{0:T(128)}, u32[]{:S(2)}) copy-start(f32[96]{0:T(128)} %param.53) | copy-start | bytes 1156
  331.3 106.7 %copy-start.40 = (f32[96]{0:T(128)S(1)}, f32[96]{0:T(128)}, u32[]{:S(2)}) copy-start(f32[96]{0:T(128)} %param.54) | copy-start | bytes 1156
  (31 other events, 26.0 us)

commit v2 on v1

v2 whole, which is shorter than its diff:
```python
import functools
import math

import jax
import jax.numpy as jnp
from jax import lax
from jax.experimental import pallas as pl
from jax.experimental.pallas import tpu as pltpu
from jax.sharding import PartitionSpec as P

H = 12
HD = 64
LN_EPS = 1e-06
RATE = 0.5
BETA_ONE = 0.9
BETA_TWO = 0.98
ADAM_EPS = 1e-06
DECAY = 0.05
TINY = 1e-06
BF = jnp.bfloat16
F32 = jnp.float32
MESH = pl.DeviceIdType.MESH
ANY = pl.BlockSpec(memory_space=pl.ANY)
VMEM = pl.BlockSpec(memory_space=pltpu.VMEM)
MIB = 1 << 20

TABLE, ENTRY, EXIT, EXPAND, REDUCE, ALIGN = range(6)
TABLE_ROWS = 49
TABLE_SLAB = 56
NORM_LANES = 96
ROUTED_DP = 16


def contract(left, right, left_dim, right_dim):
    return lax.dot_general(
        left, right, (((left_dim,), (right_dim,)), ((), ())), preferred_element_type=F32
    )


def layer_norm(values, gain, shift):
    center = values - jnp.mean(values, axis=-1, keepdims=True)
    spread = jnp.mean(center * center, axis=-1, keepdims=True)
    return center * lax.rsqrt(spread + LN_EPS) * gain + shift


def row_layout(clip_lengths, clip_device, device, row_count):
    mine = clip_device == device
    own_length = jnp.where(mine, clip_lengths, 0)
    starts = jnp.cumsum(own_length) - own_length
    filled = jnp.sum(own_length)
    positions = jnp.arange(row_count, dtype=jnp.int32)
    begun = mine[None, :] & (starts[None, :] <= positions[:, None])
    segment = jnp.sum(begun.astype(jnp.int32), axis=1)
    valid_rows = positions < filled
    return (jnp.where(valid_rows, segment, 0), valid_rows)


class Route:
    def __init__(self):
        dp = lax.axis_index("dp")
        core = lax.axis_index("tensor")
        z, y, x = dp // 4, (dp // 2) % 2, dp % 2
        across_y = dp + 2 - 4 * y
        across_x = dp + 1 - 2 * x
        self.dp, self.core, self.me = dp, core, dp * 2 + core
        self.z, self.column = z, y * 2 + x
        self.near = across_y * (1 - core) + across_x * core
        self.far = across_x * (1 - core) + across_y * core
        self.both = self.near + self.far - dp
        levels = [z + 1 - 2 * (z % 2), 3 - z, (z + 2) % 4]
        self.peers = [level * 4 + y * 2 + x for level in levels]
        self.partners = [(peer, core) for peer in self.peers] + [
            (self.near, core),
            (self.far, core),
            (dp, 1 - core),
        ]

    def level(self, step):
        high = lax.rem(self.z // 2 + step // 2, 2)
        low = lax.rem(self.z % 2 + step // 2 + step % 2, 2)
        return (high * 2 + low) * 4 + self.column

    def at(self, base, step):
        return (self.level(step) // 4) * 4 + base % 4


def greet(partners):
    barrier = pltpu.get_barrier_semaphore()
    for partner in partners:
        pl.semaphore_signal(barrier, inc=1, device_id=partner, device_id_type=MESH)
    return lambda: pl.semaphore_wait(barrier, len(partners))


def fold_rows(source, rows, columns):
    blocks = columns // 128
    for block in range(blocks):
        yield block, source[pl.ds(block, rows, stride=blocks), :]


def exchange_kernel(devices, part, out, held, send_sem, recv_sem):
    dp = lax.axis_index("dp")
    core = lax.axis_index("tensor")
    me = dp * 2 + core
    barrier = pltpu.get_barrier_semaphore()

    def partner(step):
        other = lax.rem(me + step, devices)
        return other, (other // 2, lax.rem(other, 2))

    def hail(step, carry):
        pl.semaphore_signal(
            barrier, inc=1, device_id=partner(step)[1], device_id_type=MESH
        )
        return carry

    lax.fori_loop(1, devices, hail, 0)
    held[me] = part[...]
    pl.semaphore_wait(barrier, devices - 1)

    def copy_to(step):
        return pltpu.make_async_remote_copy(
            src_ref=held.at[me],
            dst_ref=held.at[me],
            send_sem=send_sem.at[step],
            recv_sem=recv_sem.at[me],
            device_id=partner(step)[1],
            device_id_type=MESH,
        )

    def start(step, carry):
        copy_to(step).start()
        return carry

    def take(step, carry):
        other = partner(step)[0]
        block = held.at[other]
        pltpu.make_async_copy(block, block, recv_sem.at[other]).wait()
        return carry

    def sent(step, carry):
        copy_to(step).wait_send()
        return carry

    lax.fori_loop(1, devices, start, 0)
    lax.fori_loop(1, devices, take, 0)
    out[...] = jnp.sum(held[...], axis=0)
    lax.fori_loop(1, devices, sent, 0)


def exchange_sums(part, devices):
    return pl.pallas_call(
        functools.partial(exchange_kernel, devices),
        out_shape=jax.ShapeDtypeStruct(part.shape, F32),
        in_specs=[VMEM],
        out_specs=VMEM,
        scratch_shapes=[
            pltpu.VMEM((devices,) + part.shape, F32),
            pltpu.SemaphoreType.DMA((devices,)),
            pltpu.SemaphoreType.DMA((devices,)),
        ],
        compiler_params=pltpu.CompilerParams(collective_id=2, has_side_effects=True),
        name="exchange_sums",
    )(part)


def lane_marks(head, segment_column):
    lane = lax.broadcasted_iota(jnp.int32, (segment_column.shape[0], 128), 1)
    mine = (lane // HD) == head
    same = (lane % HD) == segment_column
    return mine, same


def attend_kernel(segment, query, key, value, out):
    rows = query.shape[0]
    chunk = 256
    for head in (0, 1):
        mine, same = lane_marks(head, segment[...])
        keys = jnp.where(mine, key[...], jnp.where(same, 0.0, -1e30).astype(BF))
        queries = jnp.where(mine, query[...] * BF(HD**-0.5), same.astype(BF))
        values = value[...]
        for start in range(0, rows, chunk):
            scores = contract(queries[start : start + chunk], keys, 1, 1)
            peak = jnp.max(scores, axis=1, keepdims=True)
            raised = jnp.exp(scores - peak)
            scale = 1.0 / jnp.sum(raised, axis=1, keepdims=True)
            attention = (raised * scale).astype(BF)
            result = contract(attention, values, 1, 0).astype(BF)
            span = slice(start, start + chunk)
            if head == 0:
                out[span, :] = result
            else:
                out[span, :] = jnp.where(mine[span], result, out[span, :])


def attend(segment, joint):
    rows, width = joint.shape[0], joint.shape[1] // 3
    pairs = width // 128
    return pl.pallas_call(
        attend_kernel,
        grid=(pairs,),
        out_shape=jax.ShapeDtypeStruct((rows, width), BF),
        in_specs=[
            pl.BlockSpec((rows, 1), lambda pair: (0, 0)),
            pl.BlockSpec((rows, 128), lambda pair: (0, pair)),
            pl.BlockSpec((rows, 128), lambda pair: (0, pairs + pair)),
            pl.BlockSpec((rows, 128), lambda pair: (0, 2 * pairs + pair)),
        ],
        out_specs=pl.BlockSpec((rows, 128), lambda pair: (0, pair)),
        compiler_params=pltpu.CompilerParams(vmem_limit_bytes=40 * MIB),
        name="attend",
    )(segment, joint, joint, joint)


def attend_back_kernel(segment, query, key, value, grad, out, key_sum, value_sum):
    rows = query.shape[0]
    chunk = 256
    scale = HD**-0.5
    for head in (0, 1):
        mine, same = lane_marks(head, segment[...])
        keys = jnp.where(mine, key[...], jnp.where(same, 0.0, -1e30).astype(BF))
        scaled = query[...] * BF(scale)
        queries = jnp.where(mine, scaled, same.astype(BF))
        zero = jnp.zeros_like(scaled)
        pure_queries = jnp.where(mine, scaled, zero)
        pure_keys = jnp.where(mine, key[...], zero)
        grads = jnp.where(mine, grad[...], zero)
        values = value[...]
        for start in range(0, rows, chunk):
            span = slice(start, start + chunk)
            scores = contract(keys, queries[span], 1, 1)
            peak = jnp.max(scores, axis=0, keepdims=True)
            raised = jnp.exp(scores - peak)
            attention = raised * (1.0 / jnp.sum(raised, axis=0, keepdims=True))
            grad_values = contract(attention.astype(BF), grads[span], 1, 0)
            grad_attention = contract(values, grads[span], 1, 1)
            inner = jnp.sum(attention * grad_attention, axis=0, keepdims=True)
            grad_score = (attention * (grad_attention - inner)).astype(BF)
            grad_keys = contract(grad_score, pure_queries[span], 1, 0)
            grad_queries = contract(grad_score, pure_keys, 0, 0) * scale
            if head == 0:
                out[0, span, :] = grad_queries.astype(BF)
            else:
                out[0, span, :] = jnp.where(mine[span], grad_queries.astype(BF), out[0, span, :])
            if head == 0 and start == 0:
                key_sum[...] = grad_keys
                value_sum[...] = grad_values
            else:
                key_sum[...] += grad_keys
                value_sum[...] += grad_values
    out[1] = key_sum[...].astype(BF)
    out[2] = value_sum[...].astype(BF)


def attend_back(segment, joint, grad_attended):
    rows, width = grad_attended.shape
    pairs = width // 128
    return pl.pallas_call(
        attend_back_kernel,
        grid=(pairs,),
        out_shape=jax.ShapeDtypeStruct((3, rows, width), BF),
        in_specs=[
            pl.BlockSpec((rows, 1), lambda pair: (0, 0)),
            pl.BlockSpec((rows, 128), lambda pair: (0, pair)),
            pl.BlockSpec((rows, 128), lambda pair: (0, pairs + pair)),
            pl.BlockSpec((rows, 128), lambda pair: (0, 2 * pairs + pair)),
            pl.BlockSpec((rows, 128), lambda pair: (0, pair)),
        ],
        out_specs=pl.BlockSpec((3, rows, 128), lambda pair: (0, 0, pair)),
        scratch_shapes=[pltpu.VMEM((rows, 128), F32), pltpu.VMEM((rows, 128), F32)],
        compiler_params=pltpu.CompilerParams(vmem_limit_bytes=40 * MIB),
        name="attend_back",
    )(segment, joint, joint, joint, grad_attended)


def forward_kernel(shapes, *refs):
    (
        tokens_hbm,
        patch,
        segment,
        table_f,
        entry_f,
        exit_f,
        expand_f,
        reduce_f,
        align_f,
        norm,
        entry_out,
        exit_out,
        expand_out,
        reduce_out,
        align_out,
        norms_out,
        residual_out,
        normed_one_out,
        joint_out,
        attended_out,
        middle_out,
        normed_two_out,
        act_out,
        slope_out,
        low_out,
        table_slab,
        entry_slab,
        exit_slab,
        expand_slab,
        reduce_slab,
        align_slab,
        table,
        entry,
        exit_low,
        wide,
        narrow,
        tokens,
        norms,
        residual,
        normed_one,
        joint,
        attended,
        feed,
        normed_two,
        act,
        slope,
        low,
        send_sem,
        recv_sem,
        own_sem,
        load_sem,
        save_sem,
        act_sem,
    ) = refs
    width = residual.shape[1]
    rows = residual.shape[0]
    slabs = (table_slab, entry_slab, exit_slab, expand_slab, reduce_slab, align_slab)
    targets = (table, entry, exit_low, wide, narrow, align_out)
    route = Route()
    core = route.core
    arrive = greet(route.partners)
    tokens_copy = pltpu.make_async_copy(tokens_hbm, tokens, load_sem.at[0])
    tokens_copy.start()
    near, far, pair = (route.near, core), (route.far, core), (route.dp, 1 - core)
    peers = [(peer, core) for peer in route.peers]

    def copy_to(source, piece, origin, partner, slot):
        return pltpu.make_async_remote_copy(
            src_ref=source,
            dst_ref=targets[piece].at[origin],
            send_sem=send_sem.at[piece, slot],
            recv_sem=recv_sem.at[piece, origin],
            device_id=partner,
            device_id_type=MESH,
        )

    def wait(piece, origin):
        block = targets[piece].at[origin]
        pltpu.make_async_copy(block, block, recv_sem.at[piece, origin]).wait()

    def pass_on(group, origin, partners, slot):
        for piece in group:
            wait(piece, origin)
            for index, partner in enumerate(partners):
                copy_to(targets[piece].at[origin], piece, origin, partner, slot + index).start()

    def launch(group, wide_part, plane_part):
        for index, partner in enumerate([near, far] + peers + [pair]):
            if plane_part if index < 2 else wide_part:
                for piece in group:
                    copy_to(slabs[piece], piece, route.me, partner, index).start()
        if wide_part:
            for piece in group:
                pltpu.make_async_copy(
                    slabs[piece], targets[piece].at[route.me], own_sem.at[piece]
                ).start()

    def peer_turn(group, step):
        pass_on(group, route.level(step) * 2 + core, (near, far, pair), 6 + (step - 1) * 3)

    def near_turn(group, step):
        pass_on(group, route.at(route.near, step) * 2 + core, (far, pair), 15 + step * 2)

    def far_turn(group, step):
        pass_on(group, route.at(route.far, step) * 2 + core, (pair,), 23 + step * 2)
        pass_on(group, route.at(route.both, step) * 2 + core, (pair,), 24 + step * 2)

    def pair_turn(group, step):
        for base in (route.dp, route.near, route.far, route.both):
            for piece in group:
                wait(piece, route.at(base, step) * 2 + 1 - core)

    def settle(group):
        for piece in group:
            pltpu.make_async_copy(
                slabs[piece], targets[piece].at[route.me], own_sem.at[piece]
            ).wait()

    blocks = width // 128
    whole = TABLE_ROWS - 1
    row_id = lax.broadcasted_iota(jnp.int32, (8, width), 0)
    lane_id = lax.broadcasted_iota(jnp.int32, (NORM_LANES, width), 1)
    from_id = lax.broadcasted_iota(jnp.int32, (NORM_LANES, width), 0)
    parts = width // NORM_LANES
    offset = lax.rem(route.me, parts) * NORM_LANES
    place = (lane_id == from_id + offset).astype(BF)
    spread = contract(norm[...].astype(BF), place, 1, 0)
    tail = jnp.where(row_id == 1, spread, 0.0)
    for block in range(blocks):
        lanes = slice(block * 128, block * 128 + 128)
        table_slab[0:whole, lanes] = table_f[pl.ds(block, whole, stride=blocks), :].astype(BF)
        last = table_f[pl.ds(whole * blocks + block, 1), :]
        mixed = jnp.where(row_id[:, lanes] == 0, last, tail[:, lanes])
        table_slab[whole : whole + 8, lanes] = mixed.astype(BF)
    for block, part in fold_rows(entry_f, *shapes[ENTRY]):
        entry_slab[:, block * 128 : block * 128 + 128] = part.astype(BF)
    for block, part in fold_rows(exit_f, *shapes[EXIT]):
        exit_slab[:, block * 128 : block * 128 + 128] = part.astype(BF)
    arrive()
    early = (TABLE, ENTRY, EXIT)
    last = (ALIGN,)
    launch(early, True, True)
    expand_slab[...] = expand_f[...].astype(BF)
    reduce_slab[...] = reduce_f[...].astype(BF)
    for block, part in fold_rows(align_f, *shapes[ALIGN]):
        align_slab[:, block * 128 : block * 128 + 128] = part.astype(BF)
    late = (EXPAND, REDUCE)

    def turn_of(group, turn):
        if 1 <= turn <= 3:
            peer_turn(group, turn)
        if 1 <= turn <= 4:
            near_turn(group, turn - 1)
        if 2 <= turn <= 5:
            far_turn(group, turn - 2)

    launch(late, True, False)
    for turn in range(1, 6):
        turn_of(early, turn)
    launch(late, False, True)
    for step in range(4):
        pair_turn((TABLE,), step)
    settle((TABLE,))
    tokens_copy.wait()

    for member in range(4):
        total = jnp.zeros((8, width), F32)
        for part in range(parts):
            total = total + table[member * parts + part, whole : whole + 8, :].astype(F32)
        norms[member : member + 1, :] = total[1:2, :]

    def embed(index, carry):
        span = pl.ds(pl.multiple_of(index * 256, 256), 256)
        entries = table.shape[0] * table.shape[1]
        picks = lax.broadcasted_iota(jnp.int32, (256, entries), 1) == patch[span, :]
        found = contract(picks.astype(BF), table[...].reshape(entries, width), 1, 0)
        values = tokens[span, :].astype(F32) + found
        residual[span, :] = values
        normed_one[span, :] = layer_norm(values, norms[0:1, :], norms[1:2, :]).astype(BF)
        return carry

    lax.fori_loop(0, rows // 256, embed, 0)
    for step in range(4):
        pair_turn((ENTRY, EXIT), step)
    settle((ENTRY, EXIT))

    saves = []

    def save(source, target):
        copy = pltpu.make_async_copy(source, target, save_sem.at[len(saves)])
        copy.start()
        saves.append(copy)

    save(entry, entry_out)
    save(exit_low, exit_out)
    save(norms, norms_out)
    save(residual, residual_out)
    save(normed_one, normed_one_out)

    def project(index, carry):
        span = pl.ds(pl.multiple_of(index * 256, 256), 256)
        weight = entry[:, :, span].reshape(width, 256)
        joint[:, span] = contract(normed_one[...], weight, 1, 0).astype(BF)
        return carry

    lax.fori_loop(0, 3 * width // 256, project, 0)
    save(joint, joint_out)

    def service(group, turn):
        @pl.when(turn <= 3)
        def _():
            peer_turn(group, turn)

        @pl.when(turn <= 4)
        def _():
            near_turn(group, turn - 1)

        @pl.when(jnp.logical_and(turn >= 2, turn <= 5))
        def _():
            far_turn(group, turn - 2)

    def attend_pair(index, carry):
        start = pl.multiple_of(index * 128, 128)
        here = pl.ds(start, 128)
        for head in (0, 1):
            mine, same = lane_marks(head, segment[...])
            marks = jnp.where(same, 0.0, -1e30).astype(BF)
            keys = jnp.where(mine, joint[:, pl.ds(start + width, 128)], marks)
            values = joint[:, pl.ds(start + 2 * width, 128)]

            def chunk(step, inner):
                span = pl.ds(pl.multiple_of(step * 256, 256), 256)
                mine, same = lane_marks(head, segment[span, :])
                queries = jnp.where(mine, joint[span, here] * BF(HD**-0.5), same.astype(BF))
                scores = contract(queries, keys, 1, 1)
                peak = jnp.max(scores, axis=1, keepdims=True)
                raised = jnp.exp(scores - peak)
                scale = 1.0 / jnp.sum(raised, axis=1, keepdims=True)
                attention = (raised * scale).astype(BF)
                result = contract(attention, values, 1, 0).astype(BF)
                if head == 0:
                    attended[span, here] = result
                else:
                    attended[span, here] = jnp.where(mine, result, attended[span, here])
                return inner

            lax.fori_loop(0, rows // 256, chunk, 0)

        @pl.when(lax.rem(index, 2) == 0)
        def _():
            service(late, index // 2 + 1)

        return carry

    lax.fori_loop(0, width // 128, attend_pair, 0)
    save(attended, attended_out)
    launch(last, True, True)
    service(late, 4)

    def leave(index, carry):
        span = pl.ds(pl.multiple_of(index * 256, 256), 256)
        weight = exit_low[...].reshape(width, width)
        values = residual[span, :] + contract(attended[span, :], weight, 1, 0)
        feed[span, :] = values
        normed_two[span, :] = layer_norm(values, norms[2:3, :], norms[3:4, :]).astype(BF)
        return carry

    saves[3].wait()
    lax.fori_loop(0, rows // 256, leave, 0)
    def keep(index, carry):
        span = pl.ds(pl.multiple_of(index * 256, 256), 256)
        residual[span, :] = feed[span, :]
        return carry

    lax.fori_loop(0, rows // 256, keep, 0)
    save(residual, middle_out)
    save(normed_two, normed_two_out)

    plane = width // expand_slab.shape[0]

    def feed_level(step, carry):
        level = route.level(step) // 4
        pair_turn(late, step)

        @pl.when(step == 0)
        def _():
            settle(late)

        slot = lax.rem(step, 2)

        @pl.when(step >= 2)
        def _():
            for copy in outgoing(slot, 0):
                copy.wait()

        slabs_here = pl.ds(level * plane, plane)

        def rows_block(index, inner):
            span = pl.ds(pl.multiple_of(index * 256, 256), 256)
            up = wide[slabs_here].reshape(width, width)
            values = contract(normed_two[span, :], up, 1, 1)
            share = 0.5 + 0.5 * lax.erf(values * (0.5**0.5))
            lifted = (values * share).astype(BF)
            act[slot, span, :] = lifted
            bell = jnp.exp(values * values * -0.5) * (0.5 / math.pi) ** 0.5
            slope[slot, span, :] = share + values * bell
            down = narrow[slabs_here].reshape(width, width)
            feed[span, :] += contract(lifted, down, 1, 0)
            return inner

        lax.fori_loop(0, rows // 256, rows_block, 0)
        for copy in outgoing(slot, level):
            copy.start()

        @pl.when(step == 0)
        def _():
            service(late, 5)

        @pl.when(step >= 1)
        def _():
            service(last, step)

        return carry

    def outgoing(number, level):
        hidden = pl.ds(pl.multiple_of(level * width, width), width)
        return (
            pltpu.make_async_copy(act.at[number], act_out.at[:, hidden], act_sem.at[0, number]),
            pltpu.make_async_copy(slope.at[number], slope_out.at[:, hidden], act_sem.at[1, number]),
        )

    lax.fori_loop(0, 4, feed_level, 0)
    save(wide, expand_out)
    save(narrow, reduce_out)
    service(last, 4)
    service(last, 5)

    def close(index, carry):
        span = pl.ds(pl.multiple_of(index * 256, 256), 256)
        low[span, :] = feed[span, :].astype(BF)
        return carry

    lax.fori_loop(0, rows // 256, close, 0)
    save(low, low_out)
    for step in range(4):
        pair_turn(last, step)
    settle(last)
    for number in (0, 1):
        for copy in outgoing(number, 0):
            copy.wait()
    for copy in saves[:3] + saves[4:]:
        copy.wait()

    def sent(slot, carry):
        for piece in range(len(shapes)):
            copy_to(slabs[piece], piece, route.me, near, slot).wait_send()
        return carry

    lax.fori_loop(0, 31, sent, 0)


def gather_forward(shards, norm, tokens, patch, segment, shapes, devices):
    rows, width = tokens.shape
    hidden = shapes[EXPAND][0] * devices

    def shape(dims, kind=BF):
        return jax.ShapeDtypeStruct(dims, kind)

    pieces = (ENTRY, EXIT, EXPAND, REDUCE, ALIGN)
    flat = (rows, width)
    outs = [shape((devices,) + shapes[piece]) for piece in pieces] + [
        shape((8, width), F32),
        shape(flat, F32),
        shape(flat),
        shape((rows, 3 * width)),
        shape(flat),
        shape(flat, F32),
        shape(flat),
        shape((rows, hidden)),
        shape((rows, hidden), F32),
        shape(flat),
    ]
    scratch = (
        [pltpu.VMEM(dims, BF) for dims in shapes]
        + [pltpu.VMEM((devices,) + shapes[piece], BF) for piece in (TABLE, ENTRY, EXIT)]
        + [
            pltpu.VMEM((devices,) + shapes[EXPAND], BF),
            pltpu.VMEM((devices,) + shapes[REDUCE], BF),
            pltpu.VMEM(flat, BF),
            pltpu.VMEM((8, width), F32),
            pltpu.VMEM(flat, F32),
            pltpu.VMEM(flat, BF),
            pltpu.VMEM((rows, 3 * width), BF),
            pltpu.VMEM(flat, BF),
            pltpu.VMEM(flat, F32),
            pltpu.VMEM(flat, BF),
            pltpu.VMEM((2,) + flat, BF),
            pltpu.VMEM((2,) + flat, F32),
            pltpu.VMEM(flat, BF),
            pltpu.SemaphoreType.DMA((6, 31)),
            pltpu.SemaphoreType.DMA((6, devices)),
            pltpu.SemaphoreType.DMA((6,)),
            pltpu.SemaphoreType.DMA((16,)),
            pltpu.SemaphoreType.DMA((12,)),
            pltpu.SemaphoreType.DMA((2, 2)),
        ]
    )
    return pl.pallas_call(
        functools.partial(forward_kernel, shapes),
        out_shape=outs,
        in_specs=[ANY, VMEM, VMEM] + [VMEM] * 7,
        out_specs=[ANY] * len(outs),
        scratch_shapes=scratch,
        compiler_params=pltpu.CompilerParams(
            collective_id=0, has_side_effects=True, vmem_limit_bytes=58 * MIB
        ),
        name="gather_forward",
    )(tokens, patch, segment, *shards, norm)


def norm_back(values, slope, gain):
    center = values - jnp.mean(values, axis=-1, keepdims=True)
    spread = jnp.mean(center * center, axis=-1, keepdims=True)
    scale = lax.rsqrt(spread + LN_EPS)
    unit = center * scale
    scaled = slope * gain
    level = jnp.mean(scaled, axis=-1, keepdims=True)
    tilt = jnp.mean(scaled * unit, axis=-1, keepdims=True)
    return scale * (scaled - level - unit * tilt), slope * unit


def backward_kernel(shapes, *refs):
    count = len(shapes)
    (
        patch_row,
        segment,
        norms,
        cot_out_hbm,
        cot_align_hbm,
        entry_hbm,
        exit_hbm,
        expand_hbm,
        reduce_hbm,
        align_hbm,
        residual_hbm,
        normed_one_hbm,
        joint_hbm,
        attended_hbm,
        middle_hbm,
        normed_two_hbm,
        act_hbm,
        slope_hbm,
        low_hbm,
    ) = refs[:19]
    outs = refs[19 : 19 + count]
    aligned_out, token_out = refs[19 + count : 21 + count]
    refs = refs[21 + count :]
    grads, refs = refs[:count], refs[count:]
    from_pair, refs = refs[:count], refs[count:]
    from_far, refs = refs[:count], refs[count:]
    from_near, refs = refs[:count], refs[count:]
    from_peer, refs = refs[:count], refs[count:]
    (
        wide_a,
        wide_b,
        spare,
        act,
        expand,
        reduce,
        normed_two,
        grad_feed,
        grad_out,
        grad_two,
        slope,
        key_sum,
        value_sum,
        norm_sums,
        send_sem,
        pair_sem,
        far_sem,
        near_sem,
        peer_sem,
        load_sem,
        save_sem,
    ) = refs
    rows, width = grad_out.shape
    align_width = cot_align_hbm.shape[1]
    route = Route()
    core = route.core
    near, far, pair = (route.near, core), (route.far, core), (route.dp, 1 - core)

    def load(source, target, number):
        copy = pltpu.make_async_copy(source, target, load_sem.at[number])
        copy.start()
        return copy

    align_low = wide_a.at[:, pl.ds(0, align_width)]
    cot_align = wide_a.at[:, pl.ds(align_width, align_width)]
    cot_align_copy = load(cot_align_hbm, cot_align, 0)
    align_copy = load(align_hbm, align_low, 1)
    low_copy = load(low_hbm, act, 2)
    cot_out_copy = load(cot_out_hbm, spare, 3)
    normed_two_copy = load(normed_two_hbm, normed_two, 4)
    joint_copy = load(joint_hbm, wide_b, 5)
    arrive = greet(route.partners)

    def level_rows(step):
        return pl.ds(pl.multiple_of((route.level(step) // 4) * width, width), width)

    def chunk_loads(step):
        here = level_rows(step)
        return (
            pltpu.make_async_copy(reduce_hbm.at[here, :], reduce, load_sem.at[6]),
            pltpu.make_async_copy(expand_hbm.at[here, :], expand, load_sem.at[7]),
            pltpu.make_async_copy(slope_hbm.at[:, here], slope, load_sem.at[8]),
        )

    def act_load(step):
        return pltpu.make_async_copy(act_hbm.at[:, level_rows(step)], act, load_sem.at[9])


    def copy_to(source, target, slot, piece, semaphore, partner):
        return pltpu.make_async_remote_copy(
            src_ref=source,
            dst_ref=target,
            send_sem=send_sem.at[piece, slot],
            recv_sem=semaphore,
            device_id=partner,
            device_id_type=MESH,
        )

    def landed(block, semaphore):
        pltpu.make_async_copy(block, block, semaphore).wait()

    def total(piece, dp, sources):
        landed(from_pair[piece].at[dp], pair_sem.at[piece, dp])
        found = grads[piece][dp * 2 + core].astype(F32) + from_pair[piece][dp].astype(F32)
        for block, semaphore, slot in sources:
            landed(block.at[slot], semaphore.at[piece, slot])
            found = found + block[slot].astype(F32)
        return found

    def stage_pair(piece, step):
        for base in (route.far, route.both, route.near, route.dp):
            dp = route.at(base, step)
            copy_to(
                grads[piece].at[dp * 2 + 1 - core],
                from_pair[piece].at[dp],
                dp,
                piece,
                pair_sem.at[piece, dp],
                pair,
            ).start()

    def forward_sum(piece, dp, sources, target, slot, semaphore, partner):
        grads[piece][dp * 2 + core] = total(piece, dp, sources).astype(BF)
        copy_to(
            grads[piece].at[dp * 2 + core], target, slot, piece, semaphore, partner
        ).start()

    def stage_far(piece, step):
        for side, base in enumerate((route.far, route.both)):
            slot = step * 2 + side
            forward_sum(
                piece,
                route.at(base, step),
                (),
                from_far[piece].at[slot],
                16 + slot,
                far_sem.at[piece, slot],
                far,
            )

    def stage_near(piece, step):
        forward_sum(
            piece,
            route.at(route.near, step),
            ((from_far[piece], far_sem, step * 2 + 1),),
            from_near[piece].at[step],
            24 + step,
            near_sem.at[piece, step],
            near,
        )

    def stage_peer(piece, step):
        forward_sum(
            piece,
            route.level(step),
            ((from_far[piece], far_sem, step * 2), (from_near[piece], near_sem, step)),
            from_peer[piece].at[step - 1],
            27 + step,
            peer_sem.at[piece, step - 1],
            (route.level(step), core),
        )

    def stage_own(piece):
        outs[piece][...] = total(
            piece,
            route.dp,
            ((from_far[piece], far_sem, 0), (from_near[piece], near_sem, 0))
            + tuple((from_peer[piece], peer_sem, slot) for slot in range(3)),
        )

    def each(stage, pieces, first=0):
        def body(turn, carry):
            for piece in pieces:
                stage(piece, turn)
            return carry

        lax.fori_loop(first, 4, body, 0)


    norm_sums[...] = jnp.zeros_like(norm_sums)
    cot_align_copy.wait()
    align_copy.wait()
    low_copy.wait()
    cot_out_copy.wait()
    for copy in chunk_loads(3):
        copy.start()

    def head_rows(index, carry):
        span = pl.ds(pl.multiple_of(index * 256, 256), 256)
        keep = segment[span, :] > 0
        slopes = jnp.where(keep, cot_align[span, :], jnp.zeros((256, align_width), BF))
        cot_align[span, :] = slopes
        found = contract(slopes, align_low[...], 1, 1)
        found = found + jnp.where(keep, spare[span, :].astype(F32), 0.0)
        grad_out[span, :] = found
        grad_feed[span, :] = found.astype(BF)
        return carry

    lax.fori_loop(0, rows // 256, head_rows, 0)

    def head_grads(index, carry):
        span = pl.ds(pl.multiple_of(index * 384, 384), 384)
        found = contract(act[:, span], cot_align[...], 0, 0).astype(BF)
        slabs = 384 // shapes[ALIGN][0]
        grads[ALIGN][pl.ds(index * slabs, slabs)] = found.reshape((slabs,) + shapes[ALIGN])
        return carry

    lax.fori_loop(0, width // 384, head_grads, 0)
    arrive()
    each(stage_pair, (ALIGN,))

    def head_out(index, carry):
        span = pl.ds(pl.multiple_of(index * 256, 256), 256)
        result = contract(act[span, :], align_low[...], 1, 0).astype(BF)
        cot_align[span, :] = result
        return carry

    lax.fori_loop(0, rows // 256, head_out, 0)
    aligned_copy = pltpu.make_async_copy(cot_align, aligned_out, save_sem.at[0])
    aligned_copy.start()
    act_load(3).start()
    normed_two_copy.wait()


    def feed_back(turn, carry):
        step = 3 - turn
        for copy in chunk_loads(step):
            copy.wait()

        def rows_block(index, inner):
            span = pl.ds(pl.multiple_of(index * 256, 256), 256)
            found = contract(grad_feed[span, :], reduce[...], 1, 1)
            before = (found * slope[span, :]).astype(BF)
            spare[span, :] = before
            part = contract(before, expand[...], 1, 0)

            @pl.when(turn == 0)
            def _():
                grad_two[span, :] = part

            @pl.when(turn > 0)
            def _():
                grad_two[span, :] += part

            return inner

        lax.fori_loop(0, rows // 256, rows_block, 0)

        @pl.when(turn < 3)
        def _():
            for copy in chunk_loads(step - 1):
                copy.start()

        @pl.when(turn == 3)
        def _():
            pltpu.make_async_copy(middle_hbm, slope, load_sem.at[8]).start()
            pltpu.make_async_copy(exit_hbm, expand, load_sem.at[7]).start()

        act_load(step).wait()
        per = 384 // shapes[EXPAND][0]
        plane = (route.level(step) // 4) * (width // shapes[EXPAND][0])

        def slabs_block(index, inner):
            span = pl.ds(pl.multiple_of(index * 384, 384), 384)
            here = pl.ds(plane + index * per, per)
            found = contract(act[:, span], grad_feed[...], 0, 0).astype(BF)
            grads[REDUCE][here] = found.reshape((per,) + shapes[REDUCE])
            found = contract(spare[:, span], normed_two[...], 0, 0).astype(BF)
            grads[EXPAND][here] = found.reshape((per,) + shapes[EXPAND])
            return inner

        lax.fori_loop(0, width // 384, slabs_block, 0)

        @pl.when(turn < 3)
        def _():
            act_load(step - 1).start()

        for piece in (REDUCE, EXPAND):
            stage_pair(piece, step)

        @pl.when(turn == 0)
        def _():
            each(stage_far, (ALIGN,))

        @pl.when(turn == 1)
        def _():
            each(stage_near, (ALIGN,))

        @pl.when(turn == 2)
        def _():
            each(stage_peer, (ALIGN,), 1)

        feed_turn(turn - 1)
        return carry

    def feed_turn(turn):
        for late, stage in enumerate((stage_far, stage_near, stage_peer)):
            step = 3 - (turn - late)
            lowest = 1 if stage is stage_peer else 0

            @pl.when(jnp.logical_and(step >= lowest, step <= 3))
            def _():
                for piece in (REDUCE, EXPAND):
                    stage(piece, step)

    lax.fori_loop(0, 4, feed_back, 0)
    aligned_copy.wait()
    attended_copy = load(attended_hbm, normed_two, 2)
    entry_copy = load(entry_hbm, wide_a, 1)
    normed_one_copy = load(normed_one_hbm, act, 9)
    pltpu.make_async_copy(middle_hbm, slope, load_sem.at[8]).wait()
    pltpu.make_async_copy(exit_hbm, expand, load_sem.at[7]).wait()


    def leave_back(index, carry):
        span = pl.ds(pl.multiple_of(index * 256, 256), 256)
        slopes = grad_two[span, :]
        through, gains = norm_back(slope[span, :], slopes, norms[2:3, :])
        norm_sums[2:3, :] += jnp.sum(gains, axis=0, keepdims=True)
        norm_sums[3:4, :] += jnp.sum(slopes, axis=0, keepdims=True)
        found = grad_out[span, :] + through
        grad_out[span, :] = found
        branch = found.astype(BF)
        grad_feed[span, :] = branch
        reduce[span, :] = contract(branch, expand[...], 1, 1).astype(BF)
        return carry

    lax.fori_loop(0, rows // 256, leave_back, 0)
    residual_copy = load(residual_hbm, grad_two, 0)
    attended_copy.wait()

    def exit_grads(index, carry):
        span = pl.ds(pl.multiple_of(index * 384, 384), 384)
        found = contract(normed_two[:, span], grad_feed[...], 0, 0).astype(BF)
        slabs = 384 // shapes[EXIT][0]
        grads[EXIT][pl.ds(index * slabs, slabs)] = found.reshape((slabs,) + shapes[EXIT])
        return carry

    lax.fori_loop(0, width // 384, exit_grads, 0)
    each(stage_pair, (EXIT,))
    feed_turn(3)
    joint_copy.wait()


    scale = HD**-0.5
    query_sum = slope.at[pl.ds(0, 128), :]

    def attend_pair(index, carry):
        start = pl.multiple_of(index * 128, 128)
        at_query = pl.ds(start, 128)
        at_key = pl.ds(start + width, 128)
        at_value = pl.ds(start + 2 * width, 128)
        key_sum[...] = jnp.zeros_like(key_sum)
        value_sum[...] = jnp.zeros_like(value_sum)
        query_sum[...] = jnp.zeros_like(query_sum)
        for head in (0, 1):
            mine, same = lane_marks(head, segment[...])
            marks = jnp.where(same, 0.0, -1e30).astype(BF)
            whole_keys = wide_b[:, at_key]
            keys = jnp.where(mine, whole_keys, marks)
            values = wide_b[:, at_value]
            pure = jnp.where(mine, whole_keys, jnp.zeros_like(whole_keys))
            turned = pure.astype(F32).T.astype(BF)

            def chunk(step, inner):
                span = pl.ds(pl.multiple_of(step * 256, 256), 256)
                mine, same = lane_marks(head, segment[span, :])
                scaled = wide_b[span, at_query] * BF(scale)
                queries = jnp.where(mine, scaled, same.astype(BF))
                pure_queries = jnp.where(mine, scaled, jnp.zeros_like(scaled))
                slopes = reduce[span, at_query]
                slopes = jnp.where(mine, slopes, jnp.zeros_like(slopes))
                scores = contract(keys, queries, 1, 1)
                peak = jnp.max(scores, axis=0, keepdims=True)
                raised = jnp.exp(scores - peak)
                attention = raised * (1.0 / jnp.sum(raised, axis=0, keepdims=True))
                value_sum[...] += contract(attention.astype(BF), slopes, 1, 0)
                slope_attention = contract(values, slopes, 1, 1)
                inner_sum = jnp.sum(attention * slope_attention, axis=0, keepdims=True)
                slope_score = (attention * (slope_attention - inner_sum)).astype(BF)
                key_sum[...] += contract(slope_score, pure_queries, 1, 0)
                query_sum[:, span] += contract(turned, slope_score, 1, 0)
                return inner

            lax.fori_loop(0, rows // 256, chunk, 0)
        wide_b[:, at_query] = (query_sum[...].T * scale).astype(BF)
        wide_b[:, at_key] = key_sum[...].astype(BF)
        wide_b[:, at_value] = value_sum[...].astype(BF)

        @pl.when(index == 0)
        def _():
            each(stage_far, (EXIT,))

        @pl.when(index == 1)
        def _():
            feed_turn(4)

        @pl.when(index == 2)
        def _():
            each(stage_near, (EXIT,))

        @pl.when(index == 3)
        def _():
            feed_turn(5)

        @pl.when(index == 4)
        def _():
            each(stage_peer, (EXIT,), 1)

        return carry

    lax.fori_loop(0, width // 128, attend_pair, 0)


    normed_one_copy.wait()
    for block in range(width // 128):
        lanes = slice(block * 128, block * 128 + 128)
        spare[lanes, :] = act[:, lanes].astype(F32).T.astype(BF)

    def entry_block(index, carry):
        half = index // 3
        column = pl.ds(pl.multiple_of(lax.rem(index, 3) * width, width), width)
        line = pl.ds(pl.multiple_of(half * 384, 384), 384)
        found = contract(spare[line, :], wide_b[:, column], 1, 0).astype(BF)
        slabs = 384 // shapes[ENTRY][0]
        grads[ENTRY][pl.ds(half * slabs, slabs), :, column] = found.reshape(
            (slabs, shapes[ENTRY][0], width)
        )
        return carry

    lax.fori_loop(0, 6, entry_block, 0)
    each(stage_pair, (ENTRY,))
    entry_copy.wait()
    residual_copy.wait()

    def enter_back(index, carry):
        span = pl.ds(pl.multiple_of(index * 256, 256), 256)
        slopes = contract(wide_b[span, :], wide_a[...], 1, 1)
        through, gains = norm_back(grad_two[span, :], slopes, norms[0:1, :])
        norm_sums[0:1, :] += jnp.sum(gains, axis=0, keepdims=True)
        norm_sums[1:2, :] += jnp.sum(slopes, axis=0, keepdims=True)
        found = grad_out[span, :] + through
        grad_out[span, :] = found
        grad_feed[span, :] = found.astype(BF)
        return carry

    lax.fori_loop(0, rows // 256, enter_back, 0)
    token_copy = pltpu.make_async_copy(grad_out, token_out, save_sem.at[1])
    token_copy.start()
    each(stage_far, (ENTRY,))

    slabs = 4
    block_rows = slabs * TABLE_SLAB

    def table_block(index, carry):
        entries = lax.broadcasted_iota(jnp.int32, (block_rows, rows), 0) + index * block_rows
        picks = (entries == patch_row[...]).astype(BF)
        found = contract(picks, grad_feed[...], 1, 0).astype(BF)
        grads[TABLE][pl.ds(index * slabs, slabs)] = found.reshape((slabs, TABLE_SLAB, width))
        return carry

    devices = grads[TABLE].shape[0]
    lax.fori_loop(0, devices // slabs, table_block, 0)
    whole = TABLE_ROWS - 1
    row_id = lax.broadcasted_iota(jnp.int32, (8, width), 0)
    for member in range(4):
        line = norm_sums[member : member + 1, :]
        high = line.astype(BF).astype(F32)
        tail = jnp.where(row_id == 1, high, jnp.where(row_id == 2, line - high, 0.0))

        def tuck(index, carry):
            slab = member * (devices // 4) + index
            kept = grads[TABLE][slab, whole : whole + 8, :].astype(F32)
            grads[TABLE][slab, whole : whole + 8, :] = jnp.where(row_id == 0, kept, tail).astype(BF)
            return carry

        lax.fori_loop(0, devices // 4, tuck, 0)
    each(stage_pair, (TABLE,))
    each(stage_near, (ENTRY,))
    each(stage_far, (TABLE,))
    each(stage_peer, (ENTRY,), 1)
    each(stage_near, (TABLE,))
    for piece in (ALIGN, REDUCE, EXPAND, EXIT):
        stage_own(piece)
    each(stage_peer, (TABLE,), 1)
    stage_own(ENTRY)
    stage_own(TABLE)

    def sent(slot, carry):
        for piece in range(count):
            copy_to(
                grads[piece].at[0], from_pair[piece].at[0], slot, piece, pair_sem.at[piece, 0], pair
            ).wait_send()
        return carry

    lax.fori_loop(0, 31, sent, 0)
    token_copy.wait()


def scatter_backward(patch_row, segment, norms, arrays, shapes, devices):
    rows, width = arrays[0].shape
    align_width = arrays[1].shape[1]
    dps = devices // 2
    flat = (rows, width)

    def buffers(slots):
        return [pltpu.VMEM((slots,) + dims, BF) for dims in shapes]

    count = len(shapes)
    scratch = (
        buffers(devices)
        + buffers(dps)
        + buffers(8)
        + buffers(4)
        + buffers(3)
        + [pltpu.VMEM((rows, 3 * width), BF)] * 2
        + [pltpu.VMEM(flat, BF)] * 6
        + [pltpu.VMEM(flat, F32)] * 3
        + [
            pltpu.VMEM((rows, 128), F32),
            pltpu.VMEM((rows, 128), F32),
            pltpu.VMEM((8, width), F32),
            pltpu.SemaphoreType.DMA((count, 31)),
            pltpu.SemaphoreType.DMA((count, dps)),
            pltpu.SemaphoreType.DMA((count, 8)),
            pltpu.SemaphoreType.DMA((count, 4)),
            pltpu.SemaphoreType.DMA((count, 3)),
            pltpu.SemaphoreType.DMA((10,)),
            pltpu.SemaphoreType.DMA((2,)),
        ]
    )
    outs = [jax.ShapeDtypeStruct(dims, F32) for dims in shapes] + [
        jax.ShapeDtypeStruct((rows, align_width), BF),
        jax.ShapeDtypeStruct(flat, F32),
    ]
    return pl.pallas_call(
        functools.partial(backward_kernel, shapes),
        out_shape=outs,
        in_specs=[VMEM] * 3 + [ANY] * len(arrays),
        out_specs=[VMEM] * count + [ANY] * 2,
        scratch_shapes=scratch,
        compiler_params=pltpu.CompilerParams(
            collective_id=1, has_side_effects=True, vmem_limit_bytes=60 * MIB
        ),
        name="scatter_backward",
    )(patch_row, segment, norms, *arrays)


def moments_kernel(decays, *refs):
    count = len(decays)
    sums = refs[7 * count]
    row = lax.broadcasted_iota(jnp.int32, (16, 128), 0)
    found = jnp.zeros((16, 128), F32)
    for member, decay in enumerate(decays):
        weight, gradient, first, second = refs[4 * member : 4 * member + 4]
        new_first_ref, new_second_ref, update_ref = refs[
            4 * count + 3 * member : 4 * count + 3 * member + 3
        ]
        slope = gradient[...]
        new_first = BETA_ONE * first[...] + (1.0 - BETA_ONE) * slope
        new_second = BETA_TWO * second[...] + (1.0 - BETA_TWO) * slope * slope
        update = new_first / (jnp.sqrt(new_second) + ADAM_EPS) + decay * weight[...]
        new_first_ref[...] = new_first
        new_second_ref[...] = new_second
        update_ref[...] = update
        found = jnp.where(row == member, jnp.sum(weight[...] * weight[...]), found)
        found = jnp.where(row == 8 + member, jnp.sum(update * update), found)
    sums[...] = found


def moments(members, decays):
    shapes = [jax.ShapeDtypeStruct(member[0].shape, F32) for member in members]
    outs = [shape for shape in shapes for _ in range(3)]
    flat = [array for member in members for array in member]
    return pl.pallas_call(
        functools.partial(moments_kernel, decays),
        out_shape=outs + [jax.ShapeDtypeStruct((16, 128), F32)],
        in_specs=[VMEM] * len(flat),
        out_specs=[VMEM] * (len(outs) + 1),
        compiler_params=pltpu.CompilerParams(vmem_limit_bytes=40 * MIB),
        name="moments",
    )(*flat)


def step_kernel(count, *refs):
    sums = refs[0]
    for member in range(count):
        weight, update = refs[1 + 2 * member : 3 + 2 * member]
        weight_square = sums[member : member + 1, :]
        update_square = sums[8 + member : 9 + member, :]
        trust = jnp.sqrt(weight_square) / jnp.sqrt(update_square + TINY)
        if weight.shape[1] % 128 == 0:
            trust = jnp.concatenate([trust] * (weight.shape[1] // 128), axis=1)
        else:
            trust = trust[:, : weight.shape[1]]
        refs[1 + 2 * count + member][...] = weight[...] - RATE * trust * update[...]


def take_step(sums, pairs):
    count = len(pairs)
    return pl.pallas_call(
        functools.partial(step_kernel, count),
        out_shape=[jax.ShapeDtypeStruct(weight.shape, F32) for weight, _ in pairs],
        in_specs=[VMEM] * (1 + 2 * count),
        out_specs=[VMEM] * count,
        compiler_params=pltpu.CompilerParams(vmem_limit_bytes=40 * MIB),
        name="take_step",
    )(sums, *[array for pair in pairs for array in pair])


def as_rows(flat):
    if flat.ndim == 2:
        return flat
    lanes = max(size for size in range(1, 129) if flat.shape[0] % size == 0)
    return flat.reshape(-1, lanes)


def local(
    tokens,
    kept_patches,
    clip_lengths,
    clip_device,
    cot_output,
    cot_aligned,
    entry_weight,
    entry_first,
    entry_second,
    exit_weight,
    exit_first,
    exit_second,
    align_weight,
    align_first,
    align_second,
    expand_weight,
    expand_first,
    expand_second,
    reduce_weight,
    reduce_first,
    reduce_second,
    position_table,
    position_first,
    position_second,
    norm_params,
    norm_first,
    norm_second,
):
    rows, width = tokens.shape
    align_width = cot_aligned.shape[1]
    axes = ("dp", "tensor")
    pair = lax.axis_size("tensor")
    devices = lax.axis_size("dp") * pair
    hidden = expand_weight.shape[0] * devices
    positions = position_table.shape[0] * devices // width
    routed = devices == 2 * ROUTED_DP and pair == 2
    device = lax.axis_index("dp") * pair + lax.axis_index("tensor")
    segment, valid_rows = row_layout(clip_lengths, clip_device, device, rows)
    segment_column = segment[:, None]
    valid_column = valid_rows[:, None]
    shapes = (
        (TABLE_SLAB, width),
        (width // devices, 3 * width),
        (width // devices, width),
        (hidden // devices, width),
        (hidden // devices, width),
        (width // devices, align_width),
    )
    wholes = (
        (positions, width),
        (width, 3 * width),
        (width, width),
        (hidden, width),
        (hidden, width),
        (width, align_width),
    )
    masters = (position_table, entry_weight, exit_weight, expand_weight, reduce_weight, align_weight)
    if routed:
        patch = kept_patches + (kept_patches // TABLE_ROWS) * (TABLE_SLAB - TABLE_ROWS)
        found = gather_forward(
            [as_rows(master) for master in masters],
            norm_params.reshape(1, -1),
            tokens,
            patch[:, None],
            segment_column,
            shapes,
            devices,
        )
        lows = [block.reshape(-1, block.shape[2]) for block in found[:5]]
        entry_low, exit_low, expand_low, reduce_low, align_low = lows
        norm_low = found[5]
        residual, normed_one, joint_low, attended, middle = found[6:11]
        normed_two, hidden_act, hidden_slope, out_low = found[11:]
    else:
        lows = [
            lax.all_gather(master.astype(BF).reshape(-1), axes, axis=0, tiled=True).reshape(whole)
            for master, whole in zip(masters, wholes)
        ]
        norm_low = lax.all_gather(norm_params.astype(BF), axes, axis=0, tiled=True).reshape(4, width)
        patch = kept_patches
        table_low, entry_low, exit_low, expand_low, reduce_low, align_low = lows
        norm_low = norm_low.astype(F32)
        residual = tokens.astype(F32) + jnp.take(table_low, patch, axis=0).astype(F32)
        normed_one = layer_norm(residual, norm_low[0], norm_low[1]).astype(BF)
        joint_low = contract(normed_one, entry_low, 1, 0).astype(BF)
        attended = attend(segment_column, joint_low)
        middle = residual + contract(attended, exit_low, 1, 0)
        normed_two = layer_norm(middle, norm_low[2], norm_low[3]).astype(BF)
        hidden_pre = contract(normed_two, expand_low, 1, 1)
        share = 0.5 + 0.5 * lax.erf(hidden_pre * 0.5**0.5)
        hidden_act = (hidden_pre * share).astype(BF)
        hidden_slope = share + hidden_pre * jnp.exp(-0.5 * hidden_pre * hidden_pre) * (0.5 / math.pi) ** 0.5
        out_low = (middle + contract(hidden_act, reduce_low, 1, 0)).astype(BF)
    if routed:
        arrays = (cot_output, cot_aligned) + tuple(lows) + tuple(found[6:])
        results = scatter_backward(
            patch[None, :],
            segment_column,
            norm_low,
            arrays,
            shapes,
            devices,
        )
        align_rows, token_grad = results[6:]
        table_sum = results[TABLE]
        norm_row = table_sum[TABLE_ROWS] + table_sum[TABLE_ROWS + 1]
        norm_sum = lax.dynamic_slice_in_dim(
            norm_row, (device % (width // NORM_LANES)) * NORM_LANES, NORM_LANES
        )
        summed = [table_sum[:TABLE_ROWS]] + list(results[1:6])
    else:
        align_rows = contract(out_low, align_low, 1, 0).astype(BF)
        cot_align_valid = jnp.where(valid_column, cot_aligned, jnp.zeros_like(cot_aligned))
        grad_align = contract(out_low, cot_align_valid, 0, 0)
        grad_out = jnp.where(valid_column, cot_output.astype(F32), 0.0) + contract(
            cot_align_valid, align_low, 1, 1
        )
        grad_feed = grad_out.astype(BF)
        grad_act = contract(grad_feed, reduce_low, 1, 1)
        grad_pre = (grad_act * hidden_slope).astype(BF)
        grad_reduce = contract(hidden_act, grad_feed, 0, 0)
        grad_expand = contract(grad_pre, normed_two, 0, 0)
        grad_two = contract(grad_pre, expand_low, 1, 0)
        through, gains = norm_back(middle, grad_two, norm_low[2])
        grad_middle = grad_out + through
        grad_branch = grad_middle.astype(BF)
        grad_exit = contract(attended, grad_branch, 0, 0)
        grad_attended = contract(grad_branch, exit_low, 1, 1).astype(BF)
        grad_parts = attend_back(segment_column, joint_low, grad_attended)
        grad_joint = jnp.concatenate([grad_parts[0], grad_parts[1], grad_parts[2]], axis=1)
        grad_entry = contract(normed_one, grad_joint, 0, 0)
        grad_one = contract(grad_joint, entry_low, 1, 1)
        through_one, gains_one = norm_back(residual, grad_one, norm_low[0])
        token_grad = grad_middle + through_one
        places = jnp.arange(positions, dtype=jnp.int32)
        picks = (patch[:, None] == places[None, :]).astype(BF)
        grad_table = contract(picks, token_grad.astype(BF), 0, 0)
        grad_norms = jnp.concatenate(
            [jnp.sum(part, axis=0) for part in (gains_one, grad_one, gains, grad_two)]
        )
        grads = (grad_table, grad_entry, grad_exit, grad_expand, grad_reduce, grad_align)
        summed = [
            lax.psum_scatter(grad.reshape(-1), axes, scatter_dimension=0, tiled=True)
            for grad in grads
        ]
        norm_sum = lax.psum_scatter(grad_norms, axes, scatter_dimension=0, tiled=True)
    block_out = jnp.where(valid_column, out_low, jnp.zeros_like(out_low))
    aligned = jnp.where(valid_column, align_rows, jnp.zeros_like(align_rows))

    def summed_like(master, index):
        return summed[index].reshape(master.shape)

    members = (
        (entry_weight, summed_like(entry_weight, ENTRY), entry_first, entry_second),
        (exit_weight, summed_like(exit_weight, EXIT), exit_first, exit_second),
        (align_weight, summed_like(align_weight, ALIGN), align_first, align_second),
        (expand_weight, summed_like(expand_weight, EXPAND), expand_first, expand_second),
        (reduce_weight, summed_like(reduce_weight, REDUCE), reduce_first, reduce_second),
        (position_table, summed_like(position_table, TABLE), position_first, position_second),
        (norm_params, norm_sum, norm_first, norm_second),
    )
    decays = (DECAY, DECAY, DECAY, DECAY, DECAY, DECAY, 0.0)
    members = [tuple(as_rows(array) for array in member) for member in members]
    found = moments(members, decays)
    sums = found[-1]
    sums = exchange_sums(sums, devices) if routed else lax.psum(sums, axes)
    stepped = take_step(
        sums, [(members[member][0], found[3 * member + 2]) for member in range(len(members))]
    )
    weight_squares, update_squares = sums[0:7, 0], sums[8:15, 0]
    trust = jnp.sqrt(weight_squares) / jnp.sqrt(update_squares + TINY)
    outputs = [block_out, aligned, token_grad]
    originals = (
        entry_weight,
        exit_weight,
        align_weight,
        expand_weight,
        reduce_weight,
        position_table,
        norm_params,
    )
    for member, original in enumerate(originals):
        for array in (found[3 * member], found[3 * member + 1], stepped[member]):
            outputs.append(array.reshape(original.shape))
    outputs.append(jnp.stack((trust, jnp.sqrt(weight_squares), jnp.sqrt(update_squares))))
    return tuple(outputs)


def solution(mesh):
    both = ("dp", "tensor")
    rows, flat, whole = P(both, None), P(both), P()
    weight_specs = (flat,) * 9 + (rows,) * 6 + (flat,) * 6
    placed = (rows, flat, whole, whole, rows, rows) + weight_specs
    return jax.shard_map(
        local,
        mesh=mesh,
        in_specs=placed,
        out_specs=(rows, rows, rows) + weight_specs + (whole,),
        check_vma=False,
    )
```

time: 485 us -> 320 us (0.66); the launches traced: 476 us -> 318 us
  matrix products: 101 us -> 0 us
  local copies, waits for them, and re-layouts: 63.6 us -> 26.1 us
  other arithmetic: 25.9 us -> 11.5 us
    dot_general x16 -> x0, matrix products: 101 us -> none  [contract(): lax.dot_general(left, right, (((left_dim,), (right_dim,)), ((), ())), pre...]
    unnamed x197 -> x71, local copies, waits for them, and re-layouts: 41.2 us -> 20 us
    reduce_sum x7 -> x0, other arithmetic: 11.8 us -> none  [the longest x3 7.41 us: layer_norm(): return center * lax.rsqrt(spread + LN_EPS) * gain + shift]
    dot_general x2 -> x0, local copies, waits for them, and re-layouts: 6.27 us -> none  [contract(): lax.dot_general(left, right, (((left_dim,), (right_dim,)), ((), ())), pre...]
    add x2, other arithmetic: 6.09 us -> 0.77 us  [the longest x1 0.7 us: local(): kept_patches + kept_patches // TABLE_ROWS * (TABLE_SLAB - TABLE_ROWS)]
    gather x2 -> x0, local copies, waits for them, and re-layouts: 5.1 us -> none  [local(): jnp.take(table_low, patch, axis=0).astype(F32)]
    pallas_call x4 -> x2, Pallas kernels: 264 us -> 260 us  [the longest x1 148 us: scatter_backward(): pl.pallas_call(functools.partial(backward_kernel, shapes), out_shape=outs...]
where the time goes in v2:
time: 320 us; the launch traced here: 318 us
  Pallas kernels  280 us (88%)
  local copies, waits for them, and re-layouts  26.1 us (8%)
  other arithmetic  11.5 us (4%)
    pallas_call x1, Pallas kernels, scatter_backward(): pl.pallas_call(functools.partial(backward_kernel, shapes), out_shape=outs...  148 us
    pallas_call x1, Pallas kernels, gather_forward(): pl.pallas_call(functools.partial(forward_kernel, shapes), out_shape=outs,...  112 us
    unnamed x71, local copies, waits for them, and re-layouts  20 us
    pallas_call x1, Pallas kernels, exchange_sums(): pl.pallas_call(functools.partial(exchange_kernel, devices), out_shape=jax...  16.9 us

profile of v2, /device:TPU:9, one launch (start us, length us, event | category | flops | bytes accessed | tf_op | source)
XLA Modules:
  0.0 318.5 jit_solution(14278724065866205484)
XLA Ops:
  0.7 1.3 fusion.6
  2.0 0.7 fusion.5
  2.6 0.1 copy.56
  2.8 0.2 reduce-window.9
  2.9 0.1 reduce
  3.0 0.7 fusion.4
  3.7 0.2 convert_reduce_fusion
  3.9 1.6 reshape_select_fusion.refs_2_.refs_1_
  5.4 0.7 fusion.2
  6.1 0.9 broadcast_in_dim.46.refs_1_
  7.1 111.8 %gather_forward.1 = (bf16[32,24,2304]{2,1,0:T(8,128)(2,1)}, bf16[32,24,768]{2,1,0:T(8,128)(2,1)}, bf16[32,96,768]{2,1,0:T(8,128)(2,1)}, bf16[32,96,768]{2,1,0:T(...) custom-call(bf16[768,768]{1,0:T(8,128)(2,1)} %refs_0_.1, ...), custom_call_target="tpu_custom_call" | custom-call | tf_op jit(solution)/shard_map/gather_forward/pallas_call | solution.py:684
  118.9 0.6 broadcast_in_dim.44.refs_0_
  119.5 0.0 copy-start.4
  119.5 0.0 copy-start.5
  119.5 0.0 copy-start.6
  119.5 0.0 copy-start.7
  119.5 0.0 copy-start.8
  119.5 0.0 copy-start.9
  119.5 0.0 copy-start.28
  119.5 147.8 %scatter_backward.1 = (f32[56,768]{1,0:T(8,128)}, f32[24,2304]{1,0:T(8,128)}, f32[24,768]{1,0:T(8,128)}, f32[96,768]{1,0:T(8,128)}, f32[96,768]{1,0:T(8,128)}, /...) custom-call(s32[1,768]{1,0:T(1,128)} %broadcast_in_dim.44.refs_0_, ...), custom_call_target="tpu_custom_call" | custom-call | tf_op jit(solution)/shard_map/scatter_backward/pallas_call | solution.py:1245
  267.3 0.8 fusion.7
  268.1 0.1 dynamic-slice_add_fusion.refs_25_
  268.2 1.0 reshape_reshape.12.refs_1_
  269.2 0.9 reshape_reshape.15.refs_21_
  270.1 0.9 reshape_reshape.14.refs_9_
  271.0 0.9 reshape_reshape.13.refs_5_
  271.9 0.0 copy-done
  271.9 0.0 copy-done.1
  271.9 0.0 copy-done.2
  271.9 0.0 copy-done.3
  271.9 0.0 copy-done.4
  272.0 1.0 copy-done.10
  273.0 1.0 copy-done.11
  273.9 0.9 copy-done.12
  274.9 0.9 copy-done.13
  275.8 0.9 copy-done.18
  276.7 0.9 copy-done.19
  277.6 0.9 copy-done.20
  278.5 0.9 copy-done.21
  279.4 0.9 copy-done.25
  280.3 0.9 copy-done.26
  281.2 0.7 copy-done.29
  281.9 0.7 copy-done.30
  282.5 2.3 moments.1
  284.8 0.7 copy-done.14
  285.5 0.7 copy-done.16
  286.2 0.6 copy-done.23
  286.8 0.6 copy-done.27
  287.4 0.5 copy-done.31
  287.9 16.9 %exchange_sums.1.refs_0_ = f32[16,128]{1,0:T(8,128)} custom-call(f32[16,128]{1,0:T(8,128)} %copy-done.27), custom_call_target="tpu_custom_call" | custom-call | tf_op jit(solution)/shard_map/exchange_sums/pallas_call | solution.py:151
  304.9 0.9 rsqrt_reduce_fusion
  305.7 0.6 pad_maximum_fusion
  306.3 0.9 copy-done.15
  307.3 0.9 copy-done.17
  308.2 0.7 copy-done.22
  308.9 0.9 copy-done.24
  309.8 0.7 copy-done.32
  310.4 1.1 take_step.1
  311.5 0.6 iota_compare_fusion.2
  312.1 0.0 copy-start.33
  312.1 2.8 broadcast_select_fusion
  315.0 1.2 broadcast_select_fusion.1
  316.1 0.9 copy-done.34
  317.1 1.4 copy.60
  (35 shorter events, 0.1 us)
Async XLA Ops:
  119.4 152.5 %copy-start = (f32[96,768]{1,0:T(8,128)S(1)}, f32[96,768]{1,0:T(8,128)}, u32[]{:S(2)}) copy-start(f32[96,768]{1,0:T(8,128)} %refs_7_.3) | copy-start | bytes 884740
  119.4 152.5 %copy-start.1 = (f32[96,768]{1,0:T(8,128)S(1)}, f32[96,768]{1,0:T(8,128)}, u32[]{:S(2)}) copy-start(f32[96,768]{1,0:T(8,128)} %refs_9_.1) | copy-start | bytes 884740
  119.4 152.5 %copy-start.2 = (f32[55296]{0:T(1024)S(1)}, f32[55296]{0:T(1024)}, u32[]{:S(2)}) copy-start(f32[55296]{0:T(1024)} %param.33) | copy-start | bytes 663556
  119.5 152.5 %copy-start.3 = (f32[37632]{0:T(1024)S(1)}, f32[37632]{0:T(1024)}, u32[]{:S(2)}) copy-start(f32[37632]{0:T(1024)} %param.48) | copy-start | bytes 451588
  119.5 152.5 %copy-start.4 = (f32[24576]{0:T(1024)S(1)}, f32[24576]{0:T(1024)}, u32[]{:S(2)}) copy-start(f32[24576]{0:T(1024)} %param.39) | copy-start | bytes 294916
  119.5 152.5 %copy-start.5 = (f32[18432]{0:T(1024)S(1)}, f32[18432]{0:T(1024)}, u32[]{:S(2)}) copy-start(f32[18432]{0:T(1024)} %param.36) | copy-start | bytes 221188
  119.5 152.5 %copy-start.6 = (f32[96,768]{1,0:T(8,128)S(1)}, f32[96,768]{1,0:T(8,128)}, u32[]{:S(2)}) copy-start(f32[96,768]{1,0:T(8,128)} %refs_14_.1) | copy-start | bytes 884740
  119.5 152.5 %copy-start.7 = (f32[96,768]{1,0:T(8,128)S(1)}, f32[96,768]{1,0:T(8,128)}, u32[]{:S(2)}) copy-start(f32[96,768]{1,0:T(8,128)} %refs_15_.1) | copy-start | bytes 884740
  119.5 152.5 %copy-start.8 = (f32[96,768]{1,0:T(8,128)S(1)}, f32[96,768]{1,0:T(8,128)}, u32[]{:S(2)}) copy-start(f32[96,768]{1,0:T(8,128)} %refs_18_.1) | copy-start | bytes 884740
  119.5 152.5 %copy-start.9 = (f32[96,768]{1,0:T(8,128)S(1)}, f32[96,768]{1,0:T(8,128)}, u32[]{:S(2)}) copy-start(f32[96,768]{1,0:T(8,128)} %refs_19_.1) | copy-start | bytes 884740
  119.5 152.5 %copy-start.28 = (f32[96]{0:T(128)S(1)}, f32[96]{0:T(128)}, u32[]{:S(2)}) copy-start(f32[96]{0:T(128)} %param.51) | copy-start | bytes 1156
  272.0 1.0 copy-start.10
  273.0 1.0 copy-start.11
  273.9 0.9 copy-start.12
  274.9 0.9 copy-start.13
  275.8 0.9 copy-start.18
  276.7 0.9 copy-start.19
  277.6 0.9 copy-start.20
  278.5 0.9 copy-start.21
  279.4 0.9 copy-start.25
  280.3 0.9 copy-start.26
  281.2 0.7 copy-start.29
  281.9 0.7 copy-start.30
  284.8 0.7 copy-start.14
  285.5 0.7 copy-start.16
  286.2 0.6 copy-start.23
  286.8 0.6 copy-start.27
  287.4 0.5 copy-start.31
  306.3 0.9 copy-start.15
  307.3 0.9 copy-start.17
  308.2 0.7 copy-start.22
  308.9 0.9 copy-start.24
  309.7 0.7 copy-start.32
  312.1 2.8 copy-start.33
  315.0 2.1 copy-start.34

commit v3 on v2

--- a/solution.py
+++ b/solution.py
@@ -25,6 +25,7 @@
 MIB = 1 << 20
 
 TABLE, ENTRY, EXIT, EXPAND, REDUCE, ALIGN = range(6)
+MEMBERS = (ENTRY, EXIT, ALIGN, EXPAND, REDUCE, TABLE)
 TABLE_ROWS = 49
 TABLE_SLAB = 56
 NORM_LANES = 96
@@ -74,6 +75,7 @@
             (self.far, core),
             (dp, 1 - core),
         ]
+        self.corner = (self.both, core)
 
     def level(self, step):
         high = lax.rem(self.z // 2 + step // 2, 2)
@@ -97,76 +99,10 @@
         yield block, source[pl.ds(block, rows, stride=blocks), :]
 
 
-def exchange_kernel(devices, part, out, held, send_sem, recv_sem):
-    dp = lax.axis_index("dp")
-    core = lax.axis_index("tensor")
-    me = dp * 2 + core
-    barrier = pltpu.get_barrier_semaphore()
-
-    def partner(step):
-        other = lax.rem(me + step, devices)
-        return other, (other // 2, lax.rem(other, 2))
-
-    def hail(step, carry):
-        pl.semaphore_signal(
-            barrier, inc=1, device_id=partner(step)[1], device_id_type=MESH
-        )
-        return carry
-
-    lax.fori_loop(1, devices, hail, 0)
-    held[me] = part[...]
-    pl.semaphore_wait(barrier, devices - 1)
-
-    def copy_to(step):
-        return pltpu.make_async_remote_copy(
-            src_ref=held.at[me],
-            dst_ref=held.at[me],
-            send_sem=send_sem.at[step],
-            recv_sem=recv_sem.at[me],
-            device_id=partner(step)[1],
-            device_id_type=MESH,
-        )
-
-    def start(step, carry):
-        copy_to(step).start()
-        return carry
-
-    def take(step, carry):
-        other = partner(step)[0]
-        block = held.at[other]
-        pltpu.make_async_copy(block, block, recv_sem.at[other]).wait()
-        return carry
-
-    def sent(step, carry):
-        copy_to(step).wait_send()
-        return carry
-
-    lax.fori_loop(1, devices, start, 0)
-    lax.fori_loop(1, devices, take, 0)
-    out[...] = jnp.sum(held[...], axis=0)
-    lax.fori_loop(1, devices, sent, 0)
-
-
-def exchange_sums(part, devices):
-    return pl.pallas_call(
-        functools.partial(exchange_kernel, devices),
-        out_shape=jax.ShapeDtypeStruct(part.shape, F32),
-        in_specs=[VMEM],
-        out_specs=VMEM,
-        scratch_shapes=[
-            pltpu.VMEM((devices,) + part.shape, F32),
-            pltpu.SemaphoreType.DMA((devices,)),
-            pltpu.SemaphoreType.DMA((devices,)),
-        ],
-        compiler_params=pltpu.CompilerParams(collective_id=2, has_side_effects=True),
-        name="exchange_sums",
-    )(part)
-
-
 def lane_marks(head, segment_column):
     lane = lax.broadcasted_iota(jnp.int32, (segment_column.shape[0], 128), 1)
-    mine = (lane // HD) == head
-    same = (lane % HD) == segment_column
+    mine = lax.shift_right_logical(lane, 6) == head
+    same = jnp.bitwise_and(lane, HD - 1) == segment_column
     return mine, same
 
 
@@ -272,11 +208,36 @@
     )(segment, joint, joint, joint, grad_attended)
 
 
+def segments(lengths, owners, device, rows):
+    count = lengths.shape[1]
+    mine = owners == device
+    own = jnp.broadcast_to(jnp.where(mine, lengths, 0).astype(F32), (8, count))
+    before = lax.broadcasted_iota(jnp.int32, (count, count), 0)
+    after = lax.broadcasted_iota(jnp.int32, (count, count), 1)
+    starts = lax.dot_general(
+        own,
+        (before < after).astype(F32),
+        (((1,), (0,)), ((), ())),
+        precision=lax.Precision.HIGHEST,
+        preferred_element_type=F32,
+    )[0:1, :]
+    filled = jnp.sum(own[0:1, :], axis=1, keepdims=True)
+    place = lax.broadcasted_iota(jnp.int32, (rows, count), 0).astype(F32)
+    begun = jnp.where(jnp.logical_and(mine, starts <= place), 1.0, 0.0)
+    number = jnp.sum(begun, axis=1, keepdims=True)
+    return jnp.where(place[:, 0:1] < filled, number, 0.0).astype(jnp.int32)
+
+
+def slab_places(patch):
+    return patch + lax.shift_right_logical(patch * 1338, 16) * (TABLE_SLAB - TABLE_ROWS)
+
+
 def forward_kernel(shapes, *refs):
     (
         tokens_hbm,
-        patch,
-        segment,
+        kept,
+        lengths,
+        owners,
         table_f,
         entry_f,
         exit_f,
@@ -299,6 +260,8 @@
         act_out,
         slope_out,
         low_out,
+        totals_out,
+        segment_out,
         table_slab,
         entry_slab,
         exit_slab,
@@ -321,6 +284,9 @@
         act,
         slope,
         low,
+        totals,
+        patch,
+        segment,
         send_sem,
         recv_sem,
         own_sem,
@@ -392,6 +358,10 @@
                 slabs[piece], targets[piece].at[route.me], own_sem.at[piece]
             ).wait()
 
+    totals[...] = jnp.zeros_like(totals)
+    segment[...] = segments(lengths[...], owners[...], route.me, rows)
+    lifted = jnp.broadcast_to(slab_places(kept[...]).astype(F32), (8, rows))
+    patch[...] = lifted.T[:, 0:1].astype(jnp.int32)
     blocks = width // 128
     whole = TABLE_ROWS - 1
     row_id = lax.broadcasted_iota(jnp.int32, (8, width), 0)
@@ -470,6 +440,7 @@
     save(entry, entry_out)
     save(exit_low, exit_out)
     save(norms, norms_out)
+    save(segment, segment_out)
     save(residual, residual_out)
     save(normed_one, normed_one_out)
 
@@ -498,29 +469,34 @@
     def attend_pair(index, carry):
         start = pl.multiple_of(index * 128, 128)
         here = pl.ds(start, 128)
+        whole_keys = joint[:, pl.ds(start + width, 128)]
+        values = joint[:, pl.ds(start + 2 * width, 128)]
+        keys = []
         for head in (0, 1):
             mine, same = lane_marks(head, segment[...])
-            marks = jnp.where(same, 0.0, -1e30).astype(BF)
-            keys = jnp.where(mine, joint[:, pl.ds(start + width, 128)], marks)
-            values = joint[:, pl.ds(start + 2 * width, 128)]
-
-            def chunk(step, inner):
-                span = pl.ds(pl.multiple_of(step * 256, 256), 256)
+            keys.append(jnp.where(mine, whole_keys, jnp.where(same, 0.0, -1e30).astype(BF)))
+
+        def chunk(step, inner):
+            span = pl.ds(pl.multiple_of(step * 256, 256), 256)
+            lane = lax.broadcasted_iota(jnp.int32, (256, 128), 1)
+            scaled = joint[span, here] * BF(HD**-0.5)
+            found = []
+            logs = totals[span, :]
+            for head in (0, 1):
                 mine, same = lane_marks(head, segment[span, :])
-                queries = jnp.where(mine, joint[span, here] * BF(HD**-0.5), same.astype(BF))
-                scores = contract(queries, keys, 1, 1)
+                queries = jnp.where(mine, scaled, same.astype(BF))
+                scores = contract(queries, keys[head], 1, 1)
                 peak = jnp.max(scores, axis=1, keepdims=True)
                 raised = jnp.exp(scores - peak)
-                scale = 1.0 / jnp.sum(raised, axis=1, keepdims=True)
-                attention = (raised * scale).astype(BF)
-                result = contract(attention, values, 1, 0).astype(BF)
-                if head == 0:
-                    attended[span, here] = result
-                else:
-                    attended[span, here] = jnp.where(mine, result, attended[span, here])
-                return inner
-
-            lax.fori_loop(0, rows // 256, chunk, 0)
+                total = jnp.sum(raised, axis=1, keepdims=True)
+                attention = (raised * (1.0 / total)).astype(BF)
+                found.append(contract(attention, values, 1, 0))
+                logs = jnp.where(lane == index * 2 + head, peak + jnp.log(total), logs)
+            totals[span, :] = logs
+            attended[span, here] = jnp.where(lane < HD, found[0], found[1]).astype(BF)
+            return inner
+
+        lax.fori_loop(0, rows // 256, chunk, 0)
 
         @pl.when(lax.rem(index, 2) == 0)
         def _():
@@ -530,6 +506,7 @@
 
     lax.fori_loop(0, width // 128, attend_pair, 0)
     save(attended, attended_out)
+    save(totals, totals_out)
     launch(last, True, True)
     service(late, 4)
 
@@ -541,7 +518,7 @@
         normed_two[span, :] = layer_norm(values, norms[2:3, :], norms[3:4, :]).astype(BF)
         return carry
 
-    saves[3].wait()
+    saves[4].wait()
     lax.fori_loop(0, rows // 256, leave, 0)
     def keep(index, carry):
         span = pl.ds(pl.multiple_of(index * 256, 256), 256)
@@ -624,7 +601,7 @@
     for number in (0, 1):
         for copy in outgoing(number, 0):
             copy.wait()
-    for copy in saves[:3] + saves[4:]:
+    for copy in saves[:4] + saves[5:]:
         copy.wait()
 
     def sent(slot, carry):
@@ -635,7 +612,7 @@
     lax.fori_loop(0, 31, sent, 0)
 
 
-def gather_forward(shards, norm, tokens, patch, segment, shapes, devices):
+def gather_forward(shards, norm, tokens, kept, lengths, owners, shapes, devices):
     rows, width = tokens.shape
     hidden = shapes[EXPAND][0] * devices
 
@@ -655,6 +632,8 @@
         shape((rows, hidden)),
         shape((rows, hidden), F32),
         shape(flat),
+        shape((rows, 128), F32),
+        shape((rows, 1), jnp.int32),
     ]
     scratch = (
         [pltpu.VMEM(dims, BF) for dims in shapes]
@@ -673,25 +652,28 @@
             pltpu.VMEM((2,) + flat, BF),
             pltpu.VMEM((2,) + flat, F32),
             pltpu.VMEM(flat, BF),
+            pltpu.VMEM((rows, 128), F32),
+            pltpu.VMEM((rows, 1), jnp.int32),
+            pltpu.VMEM((rows, 1), jnp.int32),
             pltpu.SemaphoreType.DMA((6, 31)),
             pltpu.SemaphoreType.DMA((6, devices)),
             pltpu.SemaphoreType.DMA((6,)),
             pltpu.SemaphoreType.DMA((16,)),
-            pltpu.SemaphoreType.DMA((12,)),
+            pltpu.SemaphoreType.DMA((16,)),
             pltpu.SemaphoreType.DMA((2, 2)),
         ]
     )
     return pl.pallas_call(
         functools.partial(forward_kernel, shapes),
         out_shape=outs,
-        in_specs=[ANY, VMEM, VMEM] + [VMEM] * 7,
+        in_specs=[ANY] + [VMEM] * 10,
         out_specs=[ANY] * len(outs),
         scratch_shapes=scratch,
         compiler_params=pltpu.CompilerParams(
             collective_id=0, has_side_effects=True, vmem_limit_bytes=58 * MIB
         ),
         name="gather_forward",
-    )(tokens, patch, segment, *shards, norm)
+    )(tokens, kept, lengths, owners, *shards, norm)
 
 
 def norm_back(values, slope, gain):
@@ -708,9 +690,12 @@
 def backward_kernel(shapes, *refs):
     count = len(shapes)
     (
-        patch_row,
+        kept,
         segment,
         norms,
+        norm_weight,
+        norm_first,
+        norm_second,
         cot_out_hbm,
         cot_align_hbm,
         entry_hbm,
@@ -727,17 +712,19 @@
         act_hbm,
         slope_hbm,
         low_hbm,
-    ) = refs[:19]
-    outs = refs[19 : 19 + count]
-    aligned_out, token_out = refs[19 + count : 21 + count]
-    refs = refs[21 + count :]
+        totals_hbm,
+    ) = refs[:23]
+    states = [refs[23 + 3 * piece : 26 + 3 * piece] for piece in range(count)]
+    refs = refs[23 + 3 * count :]
+    outs = refs[:count]
+    norm_out, sums_out, aligned_out, token_out = refs[count : 4 + count]
+    refs = refs[4 + count :]
     grads, refs = refs[:count], refs[count:]
     from_pair, refs = refs[:count], refs[count:]
     from_far, refs = refs[:count], refs[count:]
     from_near, refs = refs[:count], refs[count:]
     from_peer, refs = refs[:count], refs[count:]
     (
-        wide_a,
         wide_b,
         spare,
         act,
@@ -748,9 +735,12 @@
         grad_out,
         grad_two,
         slope,
-        key_sum,
-        value_sum,
+        query_sum,
         norm_sums,
+        held,
+        table_first,
+        table_second,
+        table_third,
         send_sem,
         pair_sem,
         far_sem,
@@ -758,6 +748,9 @@
         peer_sem,
         load_sem,
         save_sem,
+        state_sem,
+        held_sem,
+        sums_sem,
     ) = refs
     rows, width = grad_out.shape
     align_width = cot_align_hbm.shape[1]
@@ -770,15 +763,14 @@
         copy.start()
         return copy
 
-    align_low = wide_a.at[:, pl.ds(0, align_width)]
-    cot_align = wide_a.at[:, pl.ds(align_width, align_width)]
+    align_low = wide_b.at[:, pl.ds(0, align_width)]
+    cot_align = wide_b.at[:, pl.ds(align_width, align_width)]
     cot_align_copy = load(cot_align_hbm, cot_align, 0)
     align_copy = load(align_hbm, align_low, 1)
     low_copy = load(low_hbm, act, 2)
     cot_out_copy = load(cot_out_hbm, spare, 3)
     normed_two_copy = load(normed_two_hbm, normed_two, 4)
-    joint_copy = load(joint_hbm, wide_b, 5)
-    arrive = greet(route.partners)
+    arrive = greet(route.partners + [route.corner])
 
     def level_rows(step):
         return pl.ds(pl.multiple_of((route.level(step) // 4) * width, width), width)
@@ -870,12 +862,24 @@
         )
 
     def stage_own(piece):
-        outs[piece][...] = total(
+        found = total(
             piece,
             route.dp,
             ((from_far[piece], far_sem, 0), (from_near[piece], near_sem, 0))
             + tuple((from_peer[piece], peer_sem, slot) for slot in range(3)),
         )
+        if outs[piece].shape == found.shape:
+            outs[piece][...] = found
+            return
+        blocks = found.shape[1] // 128
+        lines = TABLE_ROWS - 1 if piece == TABLE else found.shape[0]
+        for block in range(blocks):
+            part = found[:, block * 128 : block * 128 + 128]
+            outs[piece][pl.ds(block, lines, stride=blocks), :] = part[:lines]
+            if piece == TABLE:
+                outs[piece][pl.ds(lines * blocks + block, 1), :] = part[lines : lines + 1]
+        if piece == TABLE:
+            norm_sums[4:5, :] = found[lines + 1 : lines + 2] + found[lines + 2 : lines + 3]
 
     def each(stage, pieces, first=0):
         def body(turn, carry):
@@ -884,6 +888,15 @@
             return carry
 
         lax.fori_loop(first, 4, body, 0)
+
+    def flow(piece, turn):
+        for late, stage in enumerate((stage_far, stage_near, stage_peer)):
+            step = 3 - (turn - late)
+            lowest = 1 if stage is stage_peer else 0
+
+            @pl.when(jnp.logical_and(step >= lowest, step <= 3))
+            def _():
+                stage(piece, step)
 
 
     norm_sums[...] = jnp.zeros_like(norm_sums)
@@ -965,6 +978,14 @@
             pltpu.make_async_copy(middle_hbm, slope, load_sem.at[8]).start()
             pltpu.make_async_copy(exit_hbm, expand, load_sem.at[7]).start()
 
+        @pl.when(turn == 0)
+        def _():
+            each(stage_far, (ALIGN,))
+
+        @pl.when(turn > 0)
+        def _():
+            feed_stage(stage_far, step + 1)
+
         act_load(step).wait()
         per = 384 // shapes[EXPAND][0]
         plane = (route.level(step) // 4) * (width // shapes[EXPAND][0])
@@ -987,35 +1008,20 @@
         for piece in (REDUCE, EXPAND):
             stage_pair(piece, step)
 
-        @pl.when(turn == 0)
-        def _():
-            each(stage_far, (ALIGN,))
-
-        @pl.when(turn == 1)
-        def _():
-            each(stage_near, (ALIGN,))
-
-        @pl.when(turn == 2)
-        def _():
-            each(stage_peer, (ALIGN,), 1)
-
-        feed_turn(turn - 1)
+        @pl.when(turn == 3)
+        def _():
+            feed_stage(stage_near, 3)
+
         return carry
 
-    def feed_turn(turn):
-        for late, stage in enumerate((stage_far, stage_near, stage_peer)):
-            step = 3 - (turn - late)
-            lowest = 1 if stage is stage_peer else 0
-
-            @pl.when(jnp.logical_and(step >= lowest, step <= 3))
-            def _():
-                for piece in (REDUCE, EXPAND):
-                    stage(piece, step)
+    def feed_stage(stage, step):
+        for piece in (REDUCE, EXPAND):
+            stage(piece, step)
 
     lax.fori_loop(0, 4, feed_back, 0)
     aligned_copy.wait()
+    joint_copy = load(joint_hbm, wide_b, 5)
     attended_copy = load(attended_hbm, normed_two, 2)
-    entry_copy = load(entry_hbm, wide_a, 1)
     normed_one_copy = load(normed_one_hbm, act, 9)
     pltpu.make_async_copy(middle_hbm, slope, load_sem.at[8]).wait()
     pltpu.make_async_copy(exit_hbm, expand, load_sem.at[7]).wait()
@@ -1036,6 +1042,13 @@
 
     lax.fori_loop(0, rows // 256, leave_back, 0)
     residual_copy = load(residual_hbm, grad_two, 0)
+
+    def load_entry(part, target):
+        return load(entry_hbm.at[:, pl.ds(part * width, width)], target, (1, 3, 6)[part])
+
+    entry_copies = [load_entry(0, expand)]
+    key_sum, value_sum, totals = (slope.at[:, pl.ds(number * 128, 128)] for number in range(3))
+    totals_copy = load(totals_hbm, totals, 10)
     attended_copy.wait()
 
     def exit_grads(index, carry):
@@ -1047,12 +1060,24 @@
 
     lax.fori_loop(0, width // 384, exit_grads, 0)
     each(stage_pair, (EXIT,))
-    feed_turn(3)
+    feed_stage(stage_far, 0)
     joint_copy.wait()
 
 
     scale = HD**-0.5
-    query_sum = slope.at[pl.ds(0, 128), :]
+    totals_copy.wait()
+
+    def split(values):
+        high = values.astype(BF)
+        rest = values - high.astype(F32)
+        middle = rest.astype(BF)
+        return high, middle, (rest - middle.astype(F32)).astype(BF)
+
+    def with_parts(lane, values, others):
+        parts = split(values)
+        for number in range(3):
+            others = jnp.where(lane == 8 + number, parts[number], others)
+        return others
 
     def attend_pair(index, carry):
         start = pl.multiple_of(index * 128, 128)
@@ -1061,56 +1086,81 @@
         at_value = pl.ds(start + 2 * width, 128)
         key_sum[...] = jnp.zeros_like(key_sum)
         value_sum[...] = jnp.zeros_like(value_sum)
-        query_sum[...] = jnp.zeros_like(query_sum)
+        whole_keys = wide_b[:, at_key]
+        whole_values = wide_b[:, at_value]
+        turned = whole_keys.astype(F32).T.astype(BF)
+        lane = jnp.bitwise_and(lax.broadcasted_iota(jnp.int32, (rows, 128), 1), HD - 1)
+        parted = jnp.logical_and(lane >= 8, lane < 11)
+        ones = parted.astype(BF)
+        keys = []
         for head in (0, 1):
             mine, same = lane_marks(head, segment[...])
             marks = jnp.where(same, 0.0, -1e30).astype(BF)
-            whole_keys = wide_b[:, at_key]
-            keys = jnp.where(mine, whole_keys, marks)
-            values = wide_b[:, at_value]
-            pure = jnp.where(mine, whole_keys, jnp.zeros_like(whole_keys))
-            turned = pure.astype(F32).T.astype(BF)
-
-            def chunk(step, inner):
-                span = pl.ds(pl.multiple_of(step * 256, 256), 256)
+            keys.append(jnp.where(mine, whole_keys, jnp.where(parted, ones, marks)))
+
+        def chunk(step, inner):
+            span = pl.ds(pl.multiple_of(step * 256, 256), 256)
+            whole_lane = lax.broadcasted_iota(jnp.int32, (256, 128), 1)
+            lane = jnp.bitwise_and(whole_lane, HD - 1)
+            scaled = wide_b[span, at_query] * BF(scale)
+            both_slopes = reduce[span, at_query]
+            zero = jnp.zeros_like(scaled)
+            queries, pure_queries, slopes = [], [], []
+            for head in (0, 1):
                 mine, same = lane_marks(head, segment[span, :])
-                scaled = wide_b[span, at_query] * BF(scale)
-                queries = jnp.where(mine, scaled, same.astype(BF))
-                pure_queries = jnp.where(mine, scaled, jnp.zeros_like(scaled))
-                slopes = reduce[span, at_query]
-                slopes = jnp.where(mine, slopes, jnp.zeros_like(slopes))
-                scores = contract(keys, queries, 1, 1)
-                peak = jnp.max(scores, axis=0, keepdims=True)
-                raised = jnp.exp(scores - peak)
-                attention = raised * (1.0 / jnp.sum(raised, axis=0, keepdims=True))
-                value_sum[...] += contract(attention.astype(BF), slopes, 1, 0)
-                slope_attention = contract(values, slopes, 1, 1)
-                inner_sum = jnp.sum(attention * slope_attention, axis=0, keepdims=True)
-                slope_score = (attention * (slope_attention - inner_sum)).astype(BF)
-                key_sum[...] += contract(slope_score, pure_queries, 1, 0)
-                query_sum[:, span] += contract(turned, slope_score, 1, 0)
-                return inner
-
-            lax.fori_loop(0, rows // 256, chunk, 0)
+                log_total = jnp.sum(
+                    jnp.where(whole_lane == index * 2 + head, totals[span, :], 0.0),
+                    axis=1,
+                    keepdims=True,
+                )
+                marks = with_parts(lane, -log_total, same.astype(BF))
+                queries.append(jnp.where(mine, scaled, marks))
+                pure_queries.append(jnp.where(mine, scaled, zero))
+                slopes.append(jnp.where(mine, both_slopes, zero))
+            pure_queries = jnp.concatenate(pure_queries, axis=0)
+            slopes = jnp.concatenate(slopes, axis=0)
+            scores = [contract(keys[head], queries[head], 1, 1) for head in (0, 1)]
+            slope_attention = contract(whole_values, slopes, 1, 1)
+            attentions, slope_scores = [], []
+            for head in (0, 1):
+                attention = jnp.exp(scores[head])
+                mine = slope_attention[:, head * 256 : head * 256 + 256]
+                inner_sum = jnp.sum(attention * mine, axis=0, keepdims=True)
+                slope_scores.append((attention * (mine - inner_sum)).astype(BF))
+                attentions.append(attention.astype(BF))
+            value_sum[...] += contract(jnp.concatenate(attentions, axis=1), slopes, 1, 0)
+            key_sum[...] += contract(jnp.concatenate(slope_scores, axis=1), pure_queries, 1, 0)
+            for head in (0, 1):
+                half = slice(head * HD, head * HD + HD)
+                query_sum[half, span] = contract(turned[half, :], slope_scores[head], 1, 0)
+            return inner
+
+        lax.fori_loop(0, rows // 256, chunk, 0)
         wide_b[:, at_query] = (query_sum[...].T * scale).astype(BF)
         wide_b[:, at_key] = key_sum[...].astype(BF)
         wide_b[:, at_value] = value_sum[...].astype(BF)
 
         @pl.when(index == 0)
         def _():
+            feed_stage(stage_near, 2)
             each(stage_far, (EXIT,))
 
         @pl.when(index == 1)
         def _():
-            feed_turn(4)
+            feed_stage(stage_near, 1)
+            feed_stage(stage_peer, 3)
+            each(stage_near, (ALIGN,))
 
         @pl.when(index == 2)
         def _():
+            feed_stage(stage_near, 0)
+            feed_stage(stage_peer, 2)
             each(stage_near, (EXIT,))
 
         @pl.when(index == 3)
         def _():
-            feed_turn(5)
+            feed_stage(stage_peer, 1)
+            each(stage_peer, (ALIGN,), 1)
 
         @pl.when(index == 4)
         def _():
@@ -1119,12 +1169,42 @@
         return carry
 
     lax.fori_loop(0, width // 128, attend_pair, 0)
+
+    table_states = (table_first, table_second, table_third)
+    homes, line = {}, {}
+    for number in range(3):
+        for piece in (ENTRY, EXIT, ALIGN):
+            start = line.get(number, 0)
+            size = states[piece][number].shape[0]
+            homes[piece, number] = slope.at[
+                pl.ds(start, size), pl.ds(number * 128, 128)
+            ]
+            line[number] = start + size
+        homes[TABLE, number] = table_states[number]
+        for turn, piece in enumerate((EXPAND, REDUCE)):
+            size = shapes[piece][0]
+            homes[piece, number] = grad_two.at[pl.ds((turn * 3 + number) * size, size), :]
+
+    def state_copy(piece, number):
+        return pltpu.make_async_copy(
+            states[piece][number], homes[piece, number], state_sem.at[piece, number]
+        )
+
+    def start_states(pieces):
+        for piece in pieces:
+            for number in range(3):
+                state_copy(piece, number).start()
+
+    entry_copies.append(load_entry(1, reduce))
+    start_states((ENTRY, EXIT, ALIGN, TABLE))
 
 
     normed_one_copy.wait()
     for block in range(width // 128):
         lanes = slice(block * 128, block * 128 + 128)
         spare[lanes, :] = act[:, lanes].astype(F32).T.astype(BF)
+
+    entry_copies.append(load_entry(2, act))
 
     def entry_block(index, carry):
         half = index // 3
@@ -1139,33 +1219,42 @@
 
     lax.fori_loop(0, 6, entry_block, 0)
     each(stage_pair, (ENTRY,))
-    entry_copy.wait()
+    for copy in entry_copies:
+        copy.wait()
     residual_copy.wait()
 
     def enter_back(index, carry):
         span = pl.ds(pl.multiple_of(index * 256, 256), 256)
-        slopes = contract(wide_b[span, :], wide_a[...], 1, 1)
+        slopes = contract(wide_b[span, 0:width], expand[...], 1, 1)
+        slopes += contract(wide_b[span, width : 2 * width], reduce[...], 1, 1)
+        slopes += contract(wide_b[span, 2 * width : 3 * width], act[...], 1, 1)
         through, gains = norm_back(grad_two[span, :], slopes, norms[0:1, :])
         norm_sums[0:1, :] += jnp.sum(gains, axis=0, keepdims=True)
         norm_sums[1:2, :] += jnp.sum(slopes, axis=0, keepdims=True)
         found = grad_out[span, :] + through
         grad_out[span, :] = found
         grad_feed[span, :] = found.astype(BF)
+        flow(ENTRY, index)
         return carry
 
     lax.fori_loop(0, rows // 256, enter_back, 0)
     token_copy = pltpu.make_async_copy(grad_out, token_out, save_sem.at[1])
     token_copy.start()
-    each(stage_far, (ENTRY,))
+    start_states((EXPAND, REDUCE))
 
     slabs = 4
     block_rows = slabs * TABLE_SLAB
 
     def table_block(index, carry):
         entries = lax.broadcasted_iota(jnp.int32, (block_rows, rows), 0) + index * block_rows
-        picks = (entries == patch_row[...]).astype(BF)
+        picks = (entries == slab_places(kept[...])).astype(BF)
         found = contract(picks, grad_feed[...], 1, 0).astype(BF)
         grads[TABLE][pl.ds(index * slabs, slabs)] = found.reshape((slabs, TABLE_SLAB, width))
+
+        @pl.when(lax.rem(index, 2) == 0)
+        def _():
+            flow(ENTRY, 3 + index // 2)
+
         return carry
 
     devices = grads[TABLE].shape[0]
@@ -1185,15 +1274,75 @@
 
         lax.fori_loop(0, devices // 4, tuck, 0)
     each(stage_pair, (TABLE,))
-    each(stage_near, (ENTRY,))
-    each(stage_far, (TABLE,))
-    each(stage_peer, (ENTRY,), 1)
-    each(stage_near, (TABLE,))
+    row_id16 = lax.broadcasted_iota(jnp.int32, (16, 128), 0)
+
+    def squares(piece):
+        for number in range(3):
+            state_copy(piece, number).wait()
+        weight, first, second = (homes[piece, number][...] for number in range(3))
+        update = lamb_update(weight, outs[piece][...], first, second, DECAY)[2]
+        note(MEMBERS.index(piece), total_square(weight), total_square(update))
+
+    def note(member, weight_square, update_square):
+        kept = held[0]
+        kept = jnp.where(row_id16 == member, weight_square, kept)
+        held[0] = jnp.where(row_id16 == 8 + member, update_square, kept)
+
+    held[0] = jnp.zeros_like(held[0])
+    for turn in range(3):
+        flow(TABLE, turn)
     for piece in (ALIGN, REDUCE, EXPAND, EXIT):
         stage_own(piece)
-    each(stage_peer, (TABLE,), 1)
+        squares(piece)
+    for turn in range(3, 6):
+        flow(TABLE, turn)
     stage_own(ENTRY)
+    squares(ENTRY)
     stage_own(TABLE)
+    squares(TABLE)
+    norm_row = norm_sums[4:5, :]
+    share = lax.rem(route.me, width // NORM_LANES)
+    norm_slope = jnp.zeros((1, NORM_LANES), F32)
+    for number in range(width // NORM_LANES):
+        part = norm_row[:, number * NORM_LANES : (number + 1) * NORM_LANES]
+        norm_slope = jnp.where(share == number, part, norm_slope)
+    norm_out[...] = norm_slope
+    update = lamb_update(norm_weight[...], norm_slope, norm_first[...], norm_second[...], 0.0)[2]
+    note(len(MEMBERS), total_square(norm_weight[...]), total_square(update))
+
+
+    def sums_to(slot, target, partner, number):
+        copy = pltpu.make_async_remote_copy(
+            src_ref=held.at[slot],
+            dst_ref=held.at[target],
+            send_sem=sums_sem.at[number],
+            recv_sem=held_sem.at[target],
+            device_id=partner,
+            device_id_type=MESH,
+        )
+        copy.start()
+        return copy
+
+    def sums_from(slot):
+        pltpu.make_async_copy(held.at[slot], held.at[slot], held_sem.at[slot]).wait()
+
+    sums_sent = [sums_to(0, 1, pair, 0)]
+    sums_from(1)
+    column = route.column
+    held[2 + column] = held[0] + held[1]
+    plane = [(route.near, core), (route.far, core), route.corner]
+    for number, partner in enumerate(plane):
+        sums_sent.append(sums_to(2 + column, 2 + column, partner, 1 + number))
+    for partner, _ in plane:
+        sums_from(2 + lax.rem(partner, 4))
+    held[6 + route.z] = held[2] + held[3] + held[4] + held[5]
+    for number, peer in enumerate(route.peers):
+        sums_sent.append(sums_to(6 + route.z, 6 + route.z, (peer, core), 4 + number))
+    for peer in route.peers:
+        sums_from(6 + peer // 4)
+    sums_out[...] = held[6] + held[7] + held[8] + held[9]
+    for copy in sums_sent:
+        copy.wait_send()
 
     def sent(slot, carry):
         for piece in range(count):
@@ -1206,7 +1355,7 @@
     token_copy.wait()
 
 
-def scatter_backward(patch_row, segment, norms, arrays, shapes, devices):
+def scatter_backward(kept, segment, norms, norm_states, arrays, states, shapes, devices):
     rows, width = arrays[0].shape
     align_width = arrays[1].shape[1]
     dps = devices // 2
@@ -1222,37 +1371,182 @@
         + buffers(8)
         + buffers(4)
         + buffers(3)
-        + [pltpu.VMEM((rows, 3 * width), BF)] * 2
+        + [pltpu.VMEM((rows, 3 * width), BF)]
         + [pltpu.VMEM(flat, BF)] * 6
         + [pltpu.VMEM(flat, F32)] * 3
         + [
-            pltpu.VMEM((rows, 128), F32),
-            pltpu.VMEM((rows, 128), F32),
+            pltpu.VMEM((128, rows), F32),
             pltpu.VMEM((8, width), F32),
+            pltpu.VMEM((10, 16, 128), F32),
+        ]
+        + [pltpu.VMEM(states[3 * TABLE].shape, F32)] * 3
+        + [
             pltpu.SemaphoreType.DMA((count, 31)),
             pltpu.SemaphoreType.DMA((count, dps)),
             pltpu.SemaphoreType.DMA((count, 8)),
             pltpu.SemaphoreType.DMA((count, 4)),
             pltpu.SemaphoreType.DMA((count, 3)),
+            pltpu.SemaphoreType.DMA((11,)),
+            pltpu.SemaphoreType.DMA((2,)),
+            pltpu.SemaphoreType.DMA((count, 3)),
             pltpu.SemaphoreType.DMA((10,)),
-            pltpu.SemaphoreType.DMA((2,)),
+            pltpu.SemaphoreType.DMA((7,)),
         ]
     )
-    outs = [jax.ShapeDtypeStruct(dims, F32) for dims in shapes] + [
+    outs = [jax.ShapeDtypeStruct(state.shape, F32) for state in states[::3]] + [
+        jax.ShapeDtypeStruct((1, NORM_LANES), F32),
+        jax.ShapeDtypeStruct((16, 128), F32),
         jax.ShapeDtypeStruct((rows, align_width), BF),
         jax.ShapeDtypeStruct(flat, F32),
     ]
     return pl.pallas_call(
         functools.partial(backward_kernel, shapes),
         out_shape=outs,
-        in_specs=[VMEM] * 3 + [ANY] * len(arrays),
-        out_specs=[VMEM] * count + [ANY] * 2,
+        in_specs=[VMEM] * 6 + [ANY] * (len(arrays) + len(states)),
+        out_specs=[VMEM] * (count + 2) + [ANY] * 2,
         scratch_shapes=scratch,
         compiler_params=pltpu.CompilerParams(
             collective_id=1, has_side_effects=True, vmem_limit_bytes=60 * MIB
         ),
         name="scatter_backward",
-    )(patch_row, segment, norms, *arrays)
+    )(kept, segment, norms, *norm_states, *arrays, *states)
+
+
+def lamb_update(weight, gradient, first, second, decay):
+    new_first = BETA_ONE * first + (1.0 - BETA_ONE) * gradient
+    new_second = BETA_TWO * second + (1.0 - BETA_TWO) * gradient * gradient
+    update = new_first / (jnp.sqrt(new_second) + ADAM_EPS) + decay * weight
+    return new_first, new_second, update
+
+
+def total_square(values):
+    return jnp.sum(jnp.sum(values * values, axis=1, keepdims=True), axis=0, keepdims=True)
+
+
+def finish_kernel(count, *refs):
+    segment, sums, norm_slope = refs[:3]
+    norm_states = refs[3:6]
+    slopes_hbm = refs[6 : 6 + count]
+    refs = refs[6 + count :]
+    states, refs = refs[: 3 * count], refs[3 * count :]
+    low_hbm, aligned_hbm, token_hbm = refs[:3]
+    outs, refs = refs[3 : 3 + 3 * count], refs[3 + 3 * count :]
+    norm_outs = refs[:3]
+    block_out, aligned_out, token_out, stats = refs[3:7]
+    refs = refs[7:]
+    held, refs = refs[: 3 * count], refs[3 * count :]
+    made, refs = refs[: 3 * count], refs[3 * count :]
+    slopes, refs = refs[:count], refs[count:]
+    slope_sem, low, aligned, token, in_sem, out_sem, row_sem = refs
+    slope_loads = [
+        pltpu.make_async_copy(slopes_hbm[piece], slopes[piece], slope_sem.at[piece])
+        for piece in range(count)
+    ]
+    for copy in slope_loads:
+        copy.start()
+    token_copy = pltpu.make_async_copy(token_hbm, token, row_sem.at[0])
+    token_copy.start()
+    low_copy = pltpu.make_async_copy(low_hbm, low, row_sem.at[1])
+    low_copy.start()
+    aligned_copy = pltpu.make_async_copy(aligned_hbm, aligned, row_sem.at[2])
+    aligned_copy.start()
+    loads = [
+        pltpu.make_async_copy(states[number], held[number], in_sem.at[number])
+        for number in range(3 * count)
+    ]
+    for copy in loads:
+        copy.start()
+
+    def trust_of(member):
+        weight_square = sums[member : member + 1, :]
+        update_square = sums[8 + member : 9 + member, :]
+        return jnp.sqrt(weight_square) / jnp.sqrt(update_square + TINY)
+
+    lane = lax.broadcasted_iota(jnp.int32, (1, 128), 1)
+    lines = [jnp.zeros((1, 128), F32)] * 3
+    for member in range(len(MEMBERS) + 1):
+        found = (
+            trust_of(member),
+            jnp.sqrt(sums[member : member + 1, :]),
+            jnp.sqrt(sums[8 + member : 9 + member, :]),
+        )
+        lines = [jnp.where(lane == member, new, line) for new, line in zip(found, lines)]
+    for row, line in enumerate(lines):
+        stats[row : row + 1, :] = line[:, : stats.shape[1]]
+    weight, first, second = (state[...] for state in norm_states)
+    made_norm = lamb_update(weight, norm_slope[...], first, second, 0.0)
+    norm_outs[0][...] = made_norm[0]
+    norm_outs[1][...] = made_norm[1]
+    step = RATE * trust_of(len(MEMBERS))[:, :NORM_LANES] * made_norm[2]
+    norm_outs[2][...] = weight - step
+    token_copy.wait()
+    token_copy = pltpu.make_async_copy(token, token_out, row_sem.at[0])
+    token_copy.start()
+    low_copy.wait()
+    keep = segment[...] > 0
+    low[...] = jnp.where(keep, low[...], jnp.zeros_like(low))
+    low_copy = pltpu.make_async_copy(low, block_out, row_sem.at[1])
+    low_copy.start()
+    aligned_copy.wait()
+    aligned[...] = jnp.where(keep, aligned[...], jnp.zeros_like(aligned))
+    aligned_copy = pltpu.make_async_copy(aligned, aligned_out, row_sem.at[2])
+    aligned_copy.start()
+    saves = []
+    for member, piece in enumerate(MEMBERS):
+        trust = trust_of(member)
+        for number in range(3):
+            loads[3 * piece + number].wait()
+        slope_loads[piece].wait()
+        weight, first, second = (held[3 * piece + number][...] for number in range(3))
+        new_first, new_second, update = lamb_update(
+            weight, slopes[piece][...], first, second, DECAY
+        )
+        wide = trust if update.shape[1] == 128 else trust[:, 0:1]
+        made[3 * piece][...] = new_first
+        made[3 * piece + 1][...] = new_second
+        made[3 * piece + 2][...] = weight - RATE * wide * update
+        for number in range(3):
+            copy = pltpu.make_async_copy(
+                made[3 * piece + number], outs[3 * piece + number], out_sem.at[3 * piece + number]
+            )
+            copy.start()
+            saves.append(copy)
+    for copy in saves + [low_copy, aligned_copy, token_copy]:
+        copy.wait()
+
+
+def finish(segment, sums, norm_slope, norm_states, slopes, states, rows):
+    count = len(slopes)
+    low, aligned, token = rows
+
+    def like(array):
+        return jax.ShapeDtypeStruct(array.shape, array.dtype)
+
+    outs = (
+        [like(state) for state in states]
+        + [like(state) for state in norm_states]
+        + [like(low), like(aligned), like(token)]
+        + [jax.ShapeDtypeStruct((3, len(MEMBERS) + 1), F32)]
+    )
+    return pl.pallas_call(
+        functools.partial(finish_kernel, count),
+        out_shape=outs,
+        in_specs=[VMEM] * 6 + [ANY] * (4 * count + 3),
+        out_specs=[ANY] * (3 * count) + [VMEM] * 3 + [ANY] * 3 + [VMEM],
+        scratch_shapes=[pltpu.VMEM(state.shape, F32) for state in states] * 2
+        + [pltpu.VMEM(slope.shape, F32) for slope in slopes]
+        + [
+            pltpu.SemaphoreType.DMA((count,)),
+            pltpu.VMEM(low.shape, BF),
+            pltpu.VMEM(aligned.shape, BF),
+            pltpu.VMEM(token.shape, F32),
+            pltpu.SemaphoreType.DMA((3 * count,)),
+            pltpu.SemaphoreType.DMA((3 * count,)),
+            pltpu.SemaphoreType.DMA((3,)),
+        ],
+        compiler_params=pltpu.CompilerParams(vmem_limit_bytes=60 * MIB),
+        name="finish",
+    )(segment, sums, norm_slope, *norm_states, *slopes, *states, low, aligned, token)
 
 
 def moments_kernel(decays, *refs):
@@ -1362,9 +1656,6 @@
     positions = position_table.shape[0] * devices // width
     routed = devices == 2 * ROUTED_DP and pair == 2
     device = lax.axis_index("dp") * pair + lax.axis_index("tensor")
-    segment, valid_rows = row_layout(clip_lengths, clip_device, device, rows)
-    segment_column = segment[:, None]
-    valid_column = valid_rows[:, None]
     shapes = (
         (TABLE_SLAB, width),
         (width // devices, 3 * width),
@@ -1382,95 +1673,109 @@
         (width, align_width),
     )
     masters = (position_table, entry_weight, exit_weight, expand_weight, reduce_weight, align_weight)
+    triples = {
+        TABLE: (position_table, position_first, position_second),
+        ENTRY: (entry_weight, entry_first, entry_second),
+        EXIT: (exit_weight, exit_first, exit_second),
+        EXPAND: (expand_weight, expand_first, expand_second),
+        REDUCE: (reduce_weight, reduce_first, reduce_second),
+        ALIGN: (align_weight, align_first, align_second),
+    }
+    norms = (norm_params, norm_first, norm_second)
     if routed:
-        patch = kept_patches + (kept_patches // TABLE_ROWS) * (TABLE_SLAB - TABLE_ROWS)
+        states = [as_rows(array) for piece in range(6) for array in triples[piece]]
+        norm_states = [array.reshape(1, -1) for array in norms]
+        kept = kept_patches.reshape(1, -1)
         found = gather_forward(
-            [as_rows(master) for master in masters],
-            norm_params.reshape(1, -1),
+            states[::3],
+            norm_states[0],
             tokens,
-            patch[:, None],
-            segment_column,
+            kept,
+            clip_lengths.reshape(1, -1),
+            clip_device.reshape(1, -1),
             shapes,
             devices,
         )
         lows = [block.reshape(-1, block.shape[2]) for block in found[:5]]
-        entry_low, exit_low, expand_low, reduce_low, align_low = lows
-        norm_low = found[5]
-        residual, normed_one, joint_low, attended, middle = found[6:11]
-        normed_two, hidden_act, hidden_slope, out_low = found[11:]
-    else:
-        lows = [
-            lax.all_gather(master.astype(BF).reshape(-1), axes, axis=0, tiled=True).reshape(whole)
-            for master, whole in zip(masters, wholes)
-        ]
-        norm_low = lax.all_gather(norm_params.astype(BF), axes, axis=0, tiled=True).reshape(4, width)
-        patch = kept_patches
-        table_low, entry_low, exit_low, expand_low, reduce_low, align_low = lows
-        norm_low = norm_low.astype(F32)
-        residual = tokens.astype(F32) + jnp.take(table_low, patch, axis=0).astype(F32)
-        normed_one = layer_norm(residual, norm_low[0], norm_low[1]).astype(BF)
-        joint_low = contract(normed_one, entry_low, 1, 0).astype(BF)
-        attended = attend(segment_column, joint_low)
-        middle = residual + contract(attended, exit_low, 1, 0)
-        normed_two = layer_norm(middle, norm_low[2], norm_low[3]).astype(BF)
-        hidden_pre = contract(normed_two, expand_low, 1, 1)
-        share = 0.5 + 0.5 * lax.erf(hidden_pre * 0.5**0.5)
-        hidden_act = (hidden_pre * share).astype(BF)
-        hidden_slope = share + hidden_pre * jnp.exp(-0.5 * hidden_pre * hidden_pre) * (0.5 / math.pi) ** 0.5
-        out_low = (middle + contract(hidden_act, reduce_low, 1, 0)).astype(BF)
-    if routed:
-        arrays = (cot_output, cot_aligned) + tuple(lows) + tuple(found[6:])
+        out_low, segment = found[14], found[16]
+        arrays = (cot_output, cot_aligned) + tuple(lows) + tuple(found[6:16])
         results = scatter_backward(
-            patch[None, :],
-            segment_column,
-            norm_low,
-            arrays,
-            shapes,
-            devices,
+            kept, segment, found[5], norm_states, arrays, states, shapes, devices
         )
-        align_rows, token_grad = results[6:]
-        table_sum = results[TABLE]
-        norm_row = table_sum[TABLE_ROWS] + table_sum[TABLE_ROWS + 1]
-        norm_sum = lax.dynamic_slice_in_dim(
-            norm_row, (device % (width // NORM_LANES)) * NORM_LANES, NORM_LANES
+        norm_slope, sums, align_rows, token_grad = results[6:]
+        done = finish(
+            segment,
+            sums,
+            norm_slope,
+            norm_states,
+            results[:6],
+            states,
+            (out_low, align_rows, token_grad),
         )
-        summed = [table_sum[:TABLE_ROWS]] + list(results[1:6])
-    else:
-        align_rows = contract(out_low, align_low, 1, 0).astype(BF)
-        cot_align_valid = jnp.where(valid_column, cot_aligned, jnp.zeros_like(cot_aligned))
-        grad_align = contract(out_low, cot_align_valid, 0, 0)
-        grad_out = jnp.where(valid_column, cot_output.astype(F32), 0.0) + contract(
-            cot_align_valid, align_low, 1, 1
-        )
-        grad_feed = grad_out.astype(BF)
-        grad_act = contract(grad_feed, reduce_low, 1, 1)
-        grad_pre = (grad_act * hidden_slope).astype(BF)
-        grad_reduce = contract(hidden_act, grad_feed, 0, 0)
-        grad_expand = contract(grad_pre, normed_two, 0, 0)
-        grad_two = contract(grad_pre, expand_low, 1, 0)
-        through, gains = norm_back(middle, grad_two, norm_low[2])
-        grad_middle = grad_out + through
-        grad_branch = grad_middle.astype(BF)
-        grad_exit = contract(attended, grad_branch, 0, 0)
-        grad_attended = contract(grad_branch, exit_low, 1, 1).astype(BF)
-        grad_parts = attend_back(segment_column, joint_low, grad_attended)
-        grad_joint = jnp.concatenate([grad_parts[0], grad_parts[1], grad_parts[2]], axis=1)
-        grad_entry = contract(normed_one, grad_joint, 0, 0)
-        grad_one = contract(grad_joint, entry_low, 1, 1)
-        through_one, gains_one = norm_back(residual, grad_one, norm_low[0])
-        token_grad = grad_middle + through_one
-        places = jnp.arange(positions, dtype=jnp.int32)
-        picks = (patch[:, None] == places[None, :]).astype(BF)
-        grad_table = contract(picks, token_grad.astype(BF), 0, 0)
-        grad_norms = jnp.concatenate(
-            [jnp.sum(part, axis=0) for part in (gains_one, grad_one, gains, grad_two)]
-        )
-        grads = (grad_table, grad_entry, grad_exit, grad_expand, grad_reduce, grad_align)
-        summed = [
-            lax.psum_scatter(grad.reshape(-1), axes, scatter_dimension=0, tiled=True)
-            for grad in grads
-        ]
-        norm_sum = lax.psum_scatter(grad_norms, axes, scatter_dimension=0, tiled=True)
+        outputs = list(done[21:24])
+        for piece in MEMBERS:
+            for number in range(3):
+                outputs.append(done[3 * piece + number].reshape(triples[piece][number].shape))
+        outputs = outputs + [array.reshape(-1) for array in done[18:21]] + [done[24]]
+        return tuple(outputs)
+
+    segment, valid_rows = row_layout(clip_lengths, clip_device, device, rows)
+    segment_column = segment[:, None]
+    valid_column = valid_rows[:, None]
+    lows = [
+        lax.all_gather(master.astype(BF).reshape(-1), axes, axis=0, tiled=True).reshape(whole)
+        for master, whole in zip(masters, wholes)
+    ]
+    norm_low = lax.all_gather(norm_params.astype(BF), axes, axis=0, tiled=True).reshape(4, width)
+    patch = kept_patches
+    table_low, entry_low, exit_low, expand_low, reduce_low, align_low = lows
+    norm_low = norm_low.astype(F32)
+    residual = tokens.astype(F32) + jnp.take(table_low, patch, axis=0).astype(F32)
+    normed_one = layer_norm(residual, norm_low[0], norm_low[1]).astype(BF)
+    joint_low = contract(normed_one, entry_low, 1, 0).astype(BF)
+    attended = attend(segment_column, joint_low)
+    middle = residual + contract(attended, exit_low, 1, 0)
+    normed_two = layer_norm(middle, norm_low[2], norm_low[3]).astype(BF)
+    hidden_pre = contract(normed_two, expand_low, 1, 1)
+    share = 0.5 + 0.5 * lax.erf(hidden_pre * 0.5**0.5)
+    hidden_act = (hidden_pre * share).astype(BF)
+    hidden_slope = share + hidden_pre * jnp.exp(-0.5 * hidden_pre * hidden_pre) * (0.5 / math.pi) ** 0.5
+    out_low = (middle + contract(hidden_act, reduce_low, 1, 0)).astype(BF)
+    align_rows = contract(out_low, align_low, 1, 0).astype(BF)
+    cot_align_valid = jnp.where(valid_column, cot_aligned, jnp.zeros_like(cot_aligned))
+    grad_align = contract(out_low, cot_align_valid, 0, 0)
+    grad_out = jnp.where(valid_column, cot_output.astype(F32), 0.0) + contract(
+        cot_align_valid, align_low, 1, 1
+    )
+    grad_feed = grad_out.astype(BF)
+    grad_act = contract(grad_feed, reduce_low, 1, 1)
+    grad_pre = (grad_act * hidden_slope).astype(BF)
+    grad_reduce = contract(hidden_act, grad_feed, 0, 0)
+    grad_expand = contract(grad_pre, normed_two, 0, 0)
+    grad_two = contract(grad_pre, expand_low, 1, 0)
+    through, gains = norm_back(middle, grad_two, norm_low[2])
+    grad_middle = grad_out + through
+    grad_branch = grad_middle.astype(BF)
+    grad_exit = contract(attended, grad_branch, 0, 0)
+    grad_attended = contract(grad_branch, exit_low, 1, 1).astype(BF)
+    grad_parts = attend_back(segment_column, joint_low, grad_attended)
+    grad_joint = jnp.concatenate([grad_parts[0], grad_parts[1], grad_parts[2]], axis=1)
+    grad_entry = contract(normed_one, grad_joint, 0, 0)
+    grad_one = contract(grad_joint, entry_low, 1, 1)
+    through_one, gains_one = norm_back(residual, grad_one, norm_low[0])
+    token_grad = grad_middle + through_one
+    places = jnp.arange(positions, dtype=jnp.int32)
+    picks = (patch[:, None] == places[None, :]).astype(BF)
+    grad_table = contract(picks, token_grad.astype(BF), 0, 0)
+    grad_norms = jnp.concatenate(
+        [jnp.sum(part, axis=0) for part in (gains_one, grad_one, gains, grad_two)]
+    )
+    grads = (grad_table, grad_entry, grad_exit, grad_expand, grad_reduce, grad_align)
+    summed = [
+        lax.psum_scatter(grad.reshape(-1), axes, scatter_dimension=0, tiled=True)
+        for grad in grads
+    ]
+    norm_sum = lax.psum_scatter(grad_norms, axes, scatter_dimension=0, tiled=True)
     block_out = jnp.where(valid_column, out_low, jnp.zeros_like(out_low))
     aligned = jnp.where(valid_column, align_rows, jnp.zeros_like(align_rows))
 
@@ -1490,7 +1795,7 @@
     members = [tuple(as_rows(array) for array in member) for member in members]
     found = moments(members, decays)
     sums = found[-1]
-    sums = exchange_sums(sums, devices) if routed else lax.psum(sums, axes)
+    sums = lax.psum(sums, axes)
     stepped = take_step(
         sums, [(members[member][0], found[3 * member + 2]) for member in range(len(members))]
     )

time: 320 us -> 257 us (0.80)
  Pallas kernels: 280 us -> 252 us
  local copies, waits for them, and re-layouts: 26.1 us -> 1.27 us
  other arithmetic: 11.5 us -> 0 us
    unnamed x71 -> x0, local copies, waits for them, and re-layouts: 20 us -> none
    pallas_call x1, Pallas kernels: 148 us -> 134 us  [scatter_backward(): pl.pallas_call(functools.partial(backward_kernel, shapes), out_shape=outs...]
    pallas_call x3 -> x1, Pallas kernels: 20.3 us -> 8.49 us  [finish(): pl.pallas_call(functools.partial(finish_kernel, count), out_shape=outs, i...]
    select_n x3 -> x0, other arithmetic: 5.58 us -> none  [the longest x1 2.83 us: local(): aligned = jnp.where(valid_column, align_rows, jnp.zeros_like(align_rows))]
    another operation x5 -> x0, local copies, waits for them, and re-layouts: 3.81 us -> none  [the longest x4 3.69 us: as_rows(): return flat.reshape(-1, lanes)]
where the time goes in v3:
time: 257 us; the launch traced here: 254 us
  Pallas kernels  252 us (98%)
    pallas_call x1, Pallas kernels, scatter_backward(): pl.pallas_call(functools.partial(backward_kernel, shapes), out_shape=outs...  134 us
    pallas_call x1, Pallas kernels, gather_forward(): pl.pallas_call(functools.partial(forward_kernel, shapes), out_shape=outs,...  110 us
    pallas_call x1, Pallas kernels, finish(): pl.pallas_call(functools.partial(finish_kernel, count), out_shape=outs, i...  8.49 us

profile of v3, /device:TPU:9, one launch (start us, length us, event | category | flops | bytes accessed | tf_op | source)
XLA Modules:
  0.0 254.1 jit_solution(7720014938049810831)
XLA Ops:
  0.7 1.3 reshape.164.refs_1_.refs_0_
  1.9 109.7 %gather_forward.1 = (bf16[32,24,2304]{2,1,0:T(8,128)(2,1)}, bf16[32,24,768]{2,1,0:T(8,128)(2,1)}, bf16[32,96,768]{2,1,0:T(8,128)(2,1)}, bf16[32,96,768]{2,1,0:T(...) custom-call(bf16[768,768]{1,0:T(8,128)(2,1)} %refs_0_.1, ...), custom_call_target="tpu_custom_call" | custom-call | tf_op jit(solution)/shard_map/gather_forward/pallas_call | solution.py:666
  111.7 133.8 %scatter_backward.1 = (f32[294,128]{1,0:T(8,128)}, f32[432,128]{1,0:T(8,128)}, f32[144,128]{1,0:T(8,128)}, f32[96,768]{1,0:T(8,128)}, f32[96,768]{1,0:T(8,128)},...) custom-call(s32[1,768]{1,0:T(1,128)} %reshape.164.refs_1_.refs_0_, ...), custom_call_target="tpu_custom_call" | custom-call | tf_op jit(solution)/shard_map/scatter_backward/pallas_call | solution.py:1402
  245.4 8.5 %finish.1 = (f32[294,128]{1,0:T(8,128)}, f32[294,128]{1,0:T(8,128)}, f32[294,128]{1,0:T(8,128)}, f32[432,128]{1,0:T(8,128)}, f32[432,128]{1,0:T(8,128)}, /*index...) custom-call(s32[768,1]{1,0:T(8,128)} %get-tuple-element.77.refs_1_.r, ...), custom_call_target="tpu_custom_call" | custom-call | tf_op jit(solution)/shard_map/finish/pallas_call | solution.py:1531

commit v4 on v3

--- a/solution.py
+++ b/solution.py
@@ -390,7 +390,7 @@
     reduce_slab[...] = reduce_f[...].astype(BF)
     for block, part in fold_rows(align_f, *shapes[ALIGN]):
         align_slab[:, block * 128 : block * 128 + 128] = part.astype(BF)
-    late = (EXPAND, REDUCE)
+    late = (EXPAND, REDUCE, ALIGN)
 
     def turn_of(group, turn):
         if 1 <= turn <= 3:
@@ -454,17 +454,17 @@
     save(joint, joint_out)
 
     def service(group, turn):
+        @pl.when(turn <= 4)
+        def _():
+            near_turn(group, turn - 1)
+
+        @pl.when(jnp.logical_and(turn >= 2, turn <= 5))
+        def _():
+            far_turn(group, turn - 2)
+
         @pl.when(turn <= 3)
         def _():
             peer_turn(group, turn)
-
-        @pl.when(turn <= 4)
-        def _():
-            near_turn(group, turn - 1)
-
-        @pl.when(jnp.logical_and(turn >= 2, turn <= 5))
-        def _():
-            far_turn(group, turn - 2)
 
     def attend_pair(index, carry):
         start = pl.multiple_of(index * 128, 128)
@@ -507,8 +507,6 @@
     lax.fori_loop(0, width // 128, attend_pair, 0)
     save(attended, attended_out)
     save(totals, totals_out)
-    launch(last, True, True)
-    service(late, 4)
 
     def leave(index, carry):
         span = pl.ds(pl.multiple_of(index * 256, 256), 256)
@@ -533,11 +531,11 @@
 
     def feed_level(step, carry):
         level = route.level(step) // 4
-        pair_turn(late, step)
+        pair_turn((EXPAND, REDUCE), step)
 
         @pl.when(step == 0)
         def _():
-            settle(late)
+            settle((EXPAND, REDUCE))
 
         slot = lax.rem(step, 2)
 
@@ -565,13 +563,9 @@
         for copy in outgoing(slot, level):
             copy.start()
 
-        @pl.when(step == 0)
+        @pl.when(step <= 1)
         def _():
-            service(late, 5)
-
-        @pl.when(step >= 1)
-        def _():
-            service(last, step)
+            service(late, step + 4)
 
         return carry
 
@@ -585,8 +579,6 @@
     lax.fori_loop(0, 4, feed_level, 0)
     save(wide, expand_out)
     save(narrow, reduce_out)
-    service(last, 4)
-    service(last, 5)
 
     def close(index, carry):
         span = pl.ds(pl.multiple_of(index * 256, 256), 256)
@@ -1008,10 +1000,6 @@
         for piece in (REDUCE, EXPAND):
             stage_pair(piece, step)
 
-        @pl.when(turn == 3)
-        def _():
-            feed_stage(stage_near, 3)
-
         return carry
 
     def feed_stage(stage, step):
@@ -1142,28 +1130,29 @@
 
         @pl.when(index == 0)
         def _():
+            feed_stage(stage_near, 3)
+            each(stage_far, (EXIT,))
+
+        @pl.when(index == 1)
+        def _():
             feed_stage(stage_near, 2)
-            each(stage_far, (EXIT,))
-
-        @pl.when(index == 1)
+            each(stage_near, (ALIGN,))
+
+        @pl.when(index == 2)
         def _():
             feed_stage(stage_near, 1)
             feed_stage(stage_peer, 3)
-            each(stage_near, (ALIGN,))
-
-        @pl.when(index == 2)
+            each(stage_near, (EXIT,))
+
+        @pl.when(index == 3)
         def _():
             feed_stage(stage_near, 0)
             feed_stage(stage_peer, 2)
-            each(stage_near, (EXIT,))
-
-        @pl.when(index == 3)
+            each(stage_peer, (ALIGN,), 1)
+
+        @pl.when(index == 4)
         def _():
             feed_stage(stage_peer, 1)
-            each(stage_peer, (ALIGN,), 1)
-
-        @pl.when(index == 4)
-        def _():
             each(stage_peer, (EXIT,), 1)
 
         return carry

time: 257 us -> 246 us (0.957)
  Pallas kernels: 252 us -> 241 us
    pallas_call x1, Pallas kernels: 110 us -> 102 us  [gather_forward(): pl.pallas_call(functools.partial(forward_kernel, shapes), out_shape=outs,...]
    pallas_call x1, Pallas kernels: 134 us -> 130 us  [scatter_backward(): pl.pallas_call(functools.partial(backward_kernel, shapes), out_shape=outs...]
where the time goes in v4:
time: 246 us; the launch traced here: 243 us
  Pallas kernels  241 us (98%)
    pallas_call x1, Pallas kernels, scatter_backward(): pl.pallas_call(functools.partial(backward_kernel, shapes), out_shape=outs...  130 us
    pallas_call x1, Pallas kernels, gather_forward(): pl.pallas_call(functools.partial(forward_kernel, shapes), out_shape=outs,...  102 us
    pallas_call x1, Pallas kernels, finish(): pl.pallas_call(functools.partial(finish_kernel, count), out_shape=outs, i...  8.49 us

profile of v4, /device:TPU:9, one launch (start us, length us, event | category | flops | bytes accessed | tf_op | source)
XLA Modules:
  0.0 243.4 jit_solution(16802683708570843929)
XLA Ops:
  0.7 1.3 reshape.164.refs_1_.refs_0_
  1.9 102.5 %gather_forward.1 = (bf16[32,24,2304]{2,1,0:T(8,128)(2,1)}, bf16[32,24,768]{2,1,0:T(8,128)(2,1)}, bf16[32,96,768]{2,1,0:T(8,128)(2,1)}, bf16[32,96,768]{2,1,0:T(...) custom-call(bf16[768,768]{1,0:T(8,128)(2,1)} %refs_0_.1, ...), custom_call_target="tpu_custom_call" | custom-call | tf_op jit(solution)/shard_map/gather_forward/pallas_call | solution.py:658
  104.4 130.4 %scatter_backward.1 = (f32[294,128]{1,0:T(8,128)}, f32[432,128]{1,0:T(8,128)}, f32[144,128]{1,0:T(8,128)}, f32[96,768]{1,0:T(8,128)}, f32[96,768]{1,0:T(8,128)},...) custom-call(s32[1,768]{1,0:T(1,128)} %reshape.164.refs_1_.refs_0_, ...), custom_call_target="tpu_custom_call" | custom-call | tf_op jit(solution)/shard_map/scatter_backward/pallas_call | solution.py:1391
  234.8 8.5 %finish.1 = (f32[294,128]{1,0:T(8,128)}, f32[294,128]{1,0:T(8,128)}, f32[294,128]{1,0:T(8,128)}, f32[432,128]{1,0:T(8,128)}, f32[432,128]{1,0:T(8,128)}, /*index...) custom-call(s32[768,1]{1,0:T(8,128)} %get-tuple-element.77.refs_1_.r, ...), custom_call_target="tpu_custom_call" | custom-call | tf_op jit(solution)/shard_map/finish/pallas_call | solution.py:1520

commit v5 on v4

--- a/solution.py
+++ b/solution.py
@@ -1039,6 +1039,8 @@
     totals_copy = load(totals_hbm, totals, 10)
     attended_copy.wait()
 
+    feed_stage(stage_far, 0)
+
     def exit_grads(index, carry):
         span = pl.ds(pl.multiple_of(index * 384, 384), 384)
         found = contract(normed_two[:, span], grad_feed[...], 0, 0).astype(BF)
@@ -1048,7 +1050,6 @@
 
     lax.fori_loop(0, width // 384, exit_grads, 0)
     each(stage_pair, (EXIT,))
-    feed_stage(stage_far, 0)
     joint_copy.wait()
 
 
@@ -1130,30 +1131,33 @@
 
         @pl.when(index == 0)
         def _():
-            feed_stage(stage_near, 3)
             each(stage_far, (EXIT,))
 
         @pl.when(index == 1)
         def _():
+            feed_stage(stage_near, 3)
+            each(stage_near, (ALIGN,))
+
+        @pl.when(index == 2)
+        def _():
             feed_stage(stage_near, 2)
-            each(stage_near, (ALIGN,))
-
-        @pl.when(index == 2)
+            each(stage_near, (EXIT,))
+
+        @pl.when(index == 3)
         def _():
             feed_stage(stage_near, 1)
             feed_stage(stage_peer, 3)
-            each(stage_near, (EXIT,))
-
-        @pl.when(index == 3)
+            each(stage_peer, (ALIGN,), 1)
+
+        @pl.when(index == 4)
         def _():
             feed_stage(stage_near, 0)
             feed_stage(stage_peer, 2)
-            each(stage_peer, (ALIGN,), 1)
-
-        @pl.when(index == 4)
+            each(stage_peer, (EXIT,), 1)
+
+        @pl.when(index == 5)
         def _():
             feed_stage(stage_peer, 1)
-            each(stage_peer, (EXIT,), 1)
 
         return carry
 

time: 246 us -> 245 us (level)
  no operation moved by 1% of the time
where the time goes in v5:
time: 245 us; the launch traced here: 242 us
  Pallas kernels  239 us (98%)
    pallas_call x1, Pallas kernels, scatter_backward(): pl.pallas_call(functools.partial(backward_kernel, shapes), out_shape=outs...  128 us
    pallas_call x1, Pallas kernels, gather_forward(): pl.pallas_call(functools.partial(forward_kernel, shapes), out_shape=outs,...  102 us
    pallas_call x1, Pallas kernels, finish(): pl.pallas_call(functools.partial(finish_kernel, count), out_shape=outs, i...  8.49 us

profile of v5, /device:TPU:9, one launch (start us, length us, event | category | flops | bytes accessed | tf_op | source)
XLA Modules:
  0.0 241.5 jit_solution(7313061423234750710)
XLA Ops:
  0.7 1.3 reshape.164.refs_1_.refs_0_
  1.9 102.5 %gather_forward.1 = (bf16[32,24,2304]{2,1,0:T(8,128)(2,1)}, bf16[32,24,768]{2,1,0:T(8,128)(2,1)}, bf16[32,96,768]{2,1,0:T(8,128)(2,1)}, bf16[32,96,768]{2,1,0:T(...) custom-call(bf16[768,768]{1,0:T(8,128)(2,1)} %refs_0_.1, ...), custom_call_target="tpu_custom_call" | custom-call | tf_op jit(solution)/shard_map/gather_forward/pallas_call | solution.py:658
  104.4 128.5 %scatter_backward.1 = (f32[294,128]{1,0:T(8,128)}, f32[432,128]{1,0:T(8,128)}, f32[144,128]{1,0:T(8,128)}, f32[96,768]{1,0:T(8,128)}, f32[96,768]{1,0:T(8,128)},...) custom-call(s32[1,768]{1,0:T(1,128)} %reshape.164.refs_1_.refs_0_, ...), custom_call_target="tpu_custom_call" | custom-call | tf_op jit(solution)/shard_map/scatter_backward/pallas_call | solution.py:1395
  232.9 8.5 %finish.1 = (f32[294,128]{1,0:T(8,128)}, f32[294,128]{1,0:T(8,128)}, f32[294,128]{1,0:T(8,128)}, f32[432,128]{1,0:T(8,128)}, f32[432,128]{1,0:T(8,128)}, /*index...) custom-call(s32[768,1]{1,0:T(8,128)} %get-tuple-element.77.refs_1_.r, ...), custom_call_target="tpu_custom_call" | custom-call | tf_op jit(solution)/shard_map/finish/pallas_call | solution.py:1524
